TPU v7x, 32 devices: a whole 2x2x4 slice. The times are simulated.
32 devices in a mesh: rep: 4 (over x, core), shard: 8 (over z, y).
Axes of the slice: x: 2, y: 2, z: 4, core: 2. Of those that a mesh axis runs over, the one named last changes fastest.
Arguments:
- inputs: bfloat16 [2, 8192, 768], P(None, ('rep', 'shard')), may hold values from -6 to 6
- cotangent: bfloat16 [2, 8192, 768], P(None, ('rep', 'shard')), may hold values from -6 to 6
- segment_ids: int32 [2, 8192], P(None, 'rep'), may hold values from 0 to 9, as said below
- memory_slot: int32 [2, 8192], P(None, ('rep', 'shard')), may hold values from -1 to 19, as said below
- memory_table: bfloat16 [20, 768], P(None, 'shard'), may hold values from -6 to 6
- qkv_weight: bfloat16 [2, 768, 2304], P(None, 'shard'), may hold values from -0.21875 to 0.21875
- query_bias: bfloat16 [2, 768], P(None, 'shard'), may hold values from -3 to 3
- value_bias: bfloat16 [2, 768], P(None, 'shard'), may hold values from -3 to 3
- proj_weight: bfloat16 [2, 768, 768], P(None, 'shard'), may hold values from -4 to 4
- proj_bias: bfloat16 [2, 768], P(None, 'shard'), may hold values from -2 to 2
- attn_gain: bfloat16 [2, 768], P(None, 'shard'), may hold values from 0.099609375 to 1.8984375
- attn_shift: bfloat16 [2, 768], P(None, 'shard'), may hold values from -2 to 2
- up_weight: bfloat16 [2, 768, 3072], P(None, 'shard'), may hold values from -0.21875 to 0.21875
- up_bias: bfloat16 [2, 3072], P(None, 'shard'), may hold values from -3 to 3
- down_weight: bfloat16 [2, 3072, 768], P(None, 'shard'), may hold values from -0.109375 to 0.109375
- down_bias: bfloat16 [2, 768], P(None, 'shard'), may hold values from -2 to 2
- ffn_gain: bfloat16 [2, 768], P(None, 'shard'), may hold values from 0.099609375 to 1.8984375
- ffn_shift: bfloat16 [2, 768], P(None, 'shard'), may hold values from -2 to 2
Outputs:
- layer_output: float32 [2, 8192, 768], P(None, ('rep', 'shard'))
- input_grad: float32 [2, 8192, 768], P(None, ('rep', 'shard'))
- memory_grad: float32 [20, 768], P(None, 'shard')
- qkv_grad: float32 [2, 768, 2304], P(None, 'shard')
- querybias_grad: float32 [2, 768], P(None, 'shard')
- valuebias_grad: float32 [2, 768], P(None, 'shard')
- proj_grad: float32 [2, 768, 768], P(None, 'shard')
- projbias_grad: float32 [2, 768], P(None, 'shard')
- attngain_grad: float32 [2, 768], P(None, 'shard')
- attnshift_grad: float32 [2, 768], P(None, 'shard')
- upweight_grad: float32 [2, 768, 3072], P(None, 'shard')
- upbias_grad: float32 [2, 3072], P(None, 'shard')
- downweight_grad: float32 [2, 3072, 768], P(None, 'shard')
- downbias_grad: float32 [2, 768], P(None, 'shard')
- ffngain_grad: float32 [2, 768], P(None, 'shard')
- ffnshift_grad: float32 [2, 768], P(None, 'shard')
Inputs may be any that keep to these rules, and one draw needn't show every extreme that they name: `segment_ids`: within each sequence (a run of 2048 tokens of one micro-batch) ids start at 0 and never fall; each id marks one document of at most 1024 tokens, one document of every sequence has exactly 1024, and every document except a sequence's first and last has 128 or more. `memory_slot`: the first 10 tokens of each document hold 0 to 9 in order (read memory); the last 10 tokens hold 10 to 19 in order (write memory) where they are not read tokens; all others hold -1.
All inputs are finite; a program needn't handle non-finite values.
Results may differ from a plain program's by a relative error of at most 0.028.
Values may be sent and summed in bfloat16 or wider, within the bound.
A program may use at most 320 MiB of HBM per device.

v0:
```python
import jax
import jax.numpy as jnp
from jax import lax
from jax.sharding import PartitionSpec as P

HEADS = 12
HEAD_DIM = 64
LAYERS = 2
MEMS = 20
REACH = 4


norm_eps = 1e-12
masked_score = -1e30


def passed_along(block, axis, distance):
    devices = range(lax.axis_size(axis))
    route = [(i - distance, i) for i in devices if i - distance in devices]
    return lax.ppermute(block, axis, route)


def layer_norm(tensor, norm_gain, norm_shift):
    center = tensor - jnp.mean(tensor, axis=-1, keepdims=True)
    inverse = lax.rsqrt(jnp.mean(center * center, axis=-1, keepdims=True) + norm_eps)
    normed = center * inverse
    return (normed * norm_gain + norm_shift, normed, inverse)


def norm_backward(grad_out, normed, inverse, norm_gain):
    scaled = grad_out * norm_gain
    inner_term = (
        scaled
        - jnp.mean(scaled, axis=-1, keepdims=True)
        - normed * jnp.mean(scaled * normed, axis=-1, keepdims=True)
    )
    return (
        inner_term * inverse,
        jnp.sum(grad_out * normed, axis=(0, 1)),
        jnp.sum(grad_out, axis=(0, 1)),
    )


def gelu_exact(tensor):
    return jax.nn.gelu(tensor, approximate=False)


def split_heads(tensor):
    return tensor.reshape(tensor.shape[0], tensor.shape[1], HEADS, HEAD_DIM)


def merge_heads(tensor):
    return tensor.reshape(tensor.shape[0], tensor.shape[1], HEADS * HEAD_DIM)


def product(left_side, right_side):
    return jnp.einsum("btd,de->bte", left_side, right_side, preferred_element_type=jnp.float32)


def product_back(left_side, right_side):
    return jnp.einsum("bte,de->btd", left_side, right_side, preferred_element_type=jnp.float32)


def weight_grad(left_side, right_side):
    return jnp.einsum("btd,bte->de", left_side, right_side, preferred_element_type=jnp.float32)


def token_sum(tensor):
    return jnp.sum(tensor.astype(jnp.float32), axis=(0, 1))


def piece_mask(segment_ids, seg_here, my_index, shards, row_count, offset):
    target = my_index + offset
    inside = jnp.logical_and(target >= 0, target < shards)
    start_row = jnp.clip(target, 0, shards - 1) * row_count
    seg_there = lax.dynamic_slice_in_dim(segment_ids, start_row, row_count, 1)
    key_mask = jnp.logical_and(seg_here[:, None, :, None] == seg_there[:, None, None, :], inside)
    return (key_mask, jnp.any(key_mask))


def scaled_scores(query_heads, key_part, key_mask):
    scores = (
        jnp.einsum(
            "bqhe,bkhe->bhqk",
            query_heads,
            split_heads(key_part),
            preferred_element_type=jnp.float32,
        )
        * 0.125
    )
    return jnp.where(key_mask, scores, masked_score)


def stats_update(carry_in, query_heads, key_part, key_mask):
    old_max, old_sum = carry_in
    scores = scaled_scores(query_heads, key_part, key_mask)
    new_max = jnp.maximum(old_max, jnp.max(scores, axis=-1))
    fresh = jnp.sum(jnp.where(key_mask, jnp.exp(scores - new_max[..., None]), 0.0), axis=-1)
    return (new_max, old_sum * jnp.exp(old_max - new_max) + fresh)


def stats_keep(carry_in, query_heads, key_part, key_mask):
    return carry_in


def mix_update(context, query_heads, key_part, value_part, key_mask, log_sum):
    scores = scaled_scores(query_heads, key_part, key_mask)
    soft_probs = jnp.where(key_mask, jnp.exp(scores - log_sum[..., None]), 0.0).astype(jnp.bfloat16)
    return context + jnp.einsum(
        "bhqk,bkhe->bqhe", soft_probs, split_heads(value_part), preferred_element_type=jnp.float32
    )


def mix_keep(context, query_heads, key_part, value_part, key_mask, log_sum):
    return context


def piece_update(
    grad_query, query_heads, grad_heads, key_part, value_part, key_mask, log_sum, row_delta
):
    scores = scaled_scores(query_heads, key_part, key_mask)
    soft_probs = jnp.where(key_mask, jnp.exp(scores - log_sum[..., None]), 0.0)
    grad_probs = jnp.einsum(
        "bqhe,bkhe->bhqk", grad_heads, split_heads(value_part), preferred_element_type=jnp.float32
    )
    grad_scores = (soft_probs * (grad_probs - row_delta[..., None])).astype(jnp.bfloat16)
    grad_query = grad_query + jnp.einsum(
        "bhqk,bkhe->bqhe", grad_scores, split_heads(key_part), preferred_element_type=jnp.float32
    )
    key_grad = jnp.einsum(
        "bhqk,bqhe->bkhe", grad_scores, query_heads, preferred_element_type=jnp.float32
    )
    value_grad = jnp.einsum(
        "bhqk,bqhe->bkhe",
        soft_probs.astype(jnp.bfloat16),
        grad_heads,
        preferred_element_type=jnp.float32,
    )
    return (grad_query, merge_heads(key_grad), merge_heads(value_grad))


def piece_skip(
    grad_query, query_heads, grad_heads, key_part, value_part, key_mask, log_sum, row_delta
):
    empty = jnp.zeros(key_part.shape, jnp.float32)
    return (grad_query, empty, empty)


def attend_forward(query_rows, key_rows, value_rows, offsets, key_masks):
    micro_count, row_count = (query_rows.shape[0], query_rows.shape[1])
    query_heads = split_heads(query_rows)
    pieces = [(key_rows, value_rows)]
    for offset in offsets:
        pieces.append(passed_along((key_rows, value_rows), "shard", -offset))
    row_max = jnp.full((micro_count, HEADS, row_count), masked_score, jnp.float32)
    row_sum = jnp.zeros((micro_count, HEADS, row_count), jnp.float32)
    for (key_part, value_part), (key_mask, is_live) in zip(pieces, key_masks):
        row_max, row_sum = lax.cond(
            is_live, stats_update, stats_keep, (row_max, row_sum), query_heads, key_part, key_mask
        )
    log_sum = row_max + jnp.log(row_sum)
    context = jnp.zeros((micro_count, row_count, HEADS, HEAD_DIM), jnp.float32)
    for (key_part, value_part), (key_mask, is_live) in zip(pieces, key_masks):
        context = lax.cond(
            is_live,
            mix_update,
            mix_keep,
            context,
            query_heads,
            key_part,
            value_part,
            key_mask,
            log_sum,
        )
    return (merge_heads(context), log_sum, pieces)


def attend_backward(query_rows, grad_context, context, log_sum, pieces, key_masks, offsets):
    query_heads = split_heads(query_rows)
    grad_heads = split_heads(grad_context)
    row_delta = jnp.transpose(
        jnp.sum(split_heads(grad_context.astype(jnp.float32) * context), axis=-1), (0, 2, 1)
    )
    grad_query = jnp.zeros(query_heads.shape, jnp.float32)
    own_keys = jnp.zeros(query_rows.shape, jnp.float32)
    own_values = jnp.zeros(query_rows.shape, jnp.float32)
    for index_num in range(len(pieces)):
        key_part, value_part = pieces[index_num]
        key_mask, is_live = key_masks[index_num]
        grad_query, key_grad, value_grad = lax.cond(
            is_live,
            piece_update,
            piece_skip,
            grad_query,
            query_heads,
            grad_heads,
            key_part,
            value_part,
            key_mask,
            log_sum,
            row_delta,
        )
        if index_num == 0:
            own_keys = key_grad
            own_values = value_grad
        else:
            back_keys, back_values = (
                passed_along(key_grad.astype(jnp.bfloat16), "shard", offsets[index_num - 1]).astype(
                    key_grad.dtype
                ),
                passed_along(
                    value_grad.astype(jnp.bfloat16), "shard", offsets[index_num - 1]
                ).astype(value_grad.dtype),
            )
            own_keys = own_keys + back_keys
            own_values = own_values + back_values
    query_out = (merge_heads(grad_query) * 0.125).astype(jnp.bfloat16)
    return (query_out, (own_keys * 0.125).astype(jnp.bfloat16), own_values.astype(jnp.bfloat16))


def layer_forward(hidden, weights, offsets, key_masks):
    (
        qkv_w,
        query_b,
        value_b,
        proj_w,
        proj_b,
        attn_g,
        attn_s,
        up_w,
        up_b,
        down_w,
        down_b,
        ffn_g,
        ffn_s,
    ) = weights
    model_width = qkv_w.shape[0]
    hidden_low = hidden.astype(jnp.bfloat16)
    mixed_all = product(hidden_low, qkv_w)
    query_rows = (mixed_all[..., :model_width] + query_b.astype(jnp.float32)).astype(jnp.bfloat16)
    key_rows = mixed_all[..., model_width : 2 * model_width].astype(jnp.bfloat16)
    value_rows = (mixed_all[..., 2 * model_width :] + value_b.astype(jnp.float32)).astype(
        jnp.bfloat16
    )
    context, log_sum, pieces = attend_forward(query_rows, key_rows, value_rows, offsets, key_masks)
    context_low = context.astype(jnp.bfloat16)
    attn_out = product(context_low, proj_w) + proj_b.astype(jnp.float32)
    settled, normed_one, inverse_one = layer_norm(
        hidden + attn_out, attn_g.astype(jnp.float32), attn_s.astype(jnp.float32)
    )
    settled_low = settled.astype(jnp.bfloat16)
    before = product(settled_low, up_w) + up_b.astype(jnp.float32)
    active = gelu_exact(before).astype(jnp.bfloat16)
    ffn_out = product(active, down_w) + down_b.astype(jnp.float32)
    result, normed_two, inverse_two = layer_norm(
        settled + ffn_out, ffn_g.astype(jnp.float32), ffn_s.astype(jnp.float32)
    )
    saved_state = (
        hidden_low,
        query_rows,
        key_rows,
        value_rows,
        context,
        log_sum,
        pieces,
        context_low,
        normed_one,
        inverse_one,
        settled_low,
        before,
        active,
        normed_two,
        inverse_two,
    )
    return (result, saved_state)


def layer_backward(grad_out, weights, saved_state, offsets, key_masks):
    (
        qkv_w,
        query_b,
        value_b,
        proj_w,
        proj_b,
        attn_g,
        attn_s,
        up_w,
        up_b,
        down_w,
        down_b,
        ffn_g,
        ffn_s,
    ) = weights
    (
        hidden_low,
        query_rows,
        key_rows,
        value_rows,
        context,
        log_sum,
        pieces,
        context_low,
        normed_one,
        inverse_one,
        settled_low,
        before,
        active,
        normed_two,
        inverse_two,
    ) = saved_state
    grad_two, ffngain_part, ffnshift_part = norm_backward(
        grad_out, normed_two, inverse_two, ffn_g.astype(jnp.float32)
    )
    grad_ffn = grad_two.astype(jnp.bfloat16)
    downweight_part = weight_grad(active, grad_ffn)
    downbias_part = token_sum(grad_ffn)
    grad_active = product_back(grad_ffn, down_w)
    gelu_pull = jax.vjp(gelu_exact, before)[1]
    grad_before = gelu_pull(grad_active)[0].astype(jnp.bfloat16)
    upweight_part = weight_grad(settled_low, grad_before)
    upbias_part = token_sum(grad_before)
    grad_settled = grad_two + product_back(grad_before, up_w)
    grad_one, attngain_part, attnshift_part = norm_backward(
        grad_settled, normed_one, inverse_one, attn_g.astype(jnp.float32)
    )
    grad_attn = grad_one.astype(jnp.bfloat16)
    proj_part = weight_grad(context_low, grad_attn)
    projbias_part = token_sum(grad_attn)
    grad_context = product_back(grad_attn, proj_w).astype(jnp.bfloat16)
    pieces = [(key_rows, value_rows)]
    for offset in offsets:
        pieces.append(passed_along((key_rows, value_rows), "shard", -offset))
    grad_query, grad_keys, grad_values = attend_backward(
        query_rows, grad_context, context, log_sum, pieces, key_masks, offsets
    )
    grad_mixed = jnp.concatenate([grad_query, grad_keys, grad_values], axis=-1)
    qkv_part = weight_grad(hidden_low, grad_mixed)
    querybias_part = token_sum(grad_query)
    valuebias_part = token_sum(grad_values)
    grad_hidden = grad_one + product_back(grad_mixed, qkv_w)
    layer_grads = (
        qkv_part,
        querybias_part,
        valuebias_part,
        proj_part,
        projbias_part,
        attngain_part,
        attnshift_part,
        upweight_part,
        upbias_part,
        downweight_part,
        downbias_part,
        ffngain_part,
        ffnshift_part,
    )
    return (grad_hidden, layer_grads)


def on_device(
    inputs,
    cotangent,
    segment_ids,
    memory_slot,
    memory_table,
    qkv_weight,
    query_bias,
    value_bias,
    proj_weight,
    proj_bias,
    attn_gain,
    attn_shift,
    up_weight,
    up_bias,
    down_weight,
    down_bias,
    ffn_gain,
    ffn_shift,
):
    shards = lax.axis_size("shard")
    my_index = lax.axis_index("shard")
    row_count = inputs.shape[1]
    reach_out = min(REACH, shards - 1)
    offsets = [offset for offset in range(-reach_out, reach_out + 1) if offset != 0]
    seg_here = lax.dynamic_slice_in_dim(segment_ids, my_index * row_count, row_count, 1)
    key_masks = [piece_mask(segment_ids, seg_here, my_index, shards, row_count, 0)]
    for offset in offsets:
        key_masks.append(piece_mask(segment_ids, seg_here, my_index, shards, row_count, offset))
    gathered = (
        lax.all_gather(qkv_weight, "shard", axis=1, tiled=True),
        lax.all_gather(query_bias, "shard", axis=1, tiled=True),
        lax.all_gather(value_bias, "shard", axis=1, tiled=True),
        lax.all_gather(proj_weight, "shard", axis=1, tiled=True),
        lax.all_gather(proj_bias, "shard", axis=1, tiled=True),
        lax.all_gather(attn_gain, "shard", axis=1, tiled=True),
        lax.all_gather(attn_shift, "shard", axis=1, tiled=True),
        lax.all_gather(up_weight, "shard", axis=1, tiled=True),
        lax.all_gather(up_bias, "shard", axis=1, tiled=True),
        lax.all_gather(down_weight, "shard", axis=1, tiled=True),
        lax.all_gather(down_bias, "shard", axis=1, tiled=True),
        lax.all_gather(ffn_gain, "shard", axis=1, tiled=True),
        lax.all_gather(ffn_shift, "shard", axis=1, tiled=True),
        lax.all_gather(memory_table, "shard", axis=1, tiled=True),
    )
    slot_range = jnp.arange(MEMS, dtype=jnp.int32)
    slot_hot = (memory_slot[..., None] == slot_range).astype(jnp.float32)
    hidden = inputs.astype(jnp.float32) + jnp.einsum(
        "btm,md->btd", slot_hot, gathered[13].astype(jnp.float32), precision=lax.Precision.HIGHEST
    )
    saved_list = []
    for layer_num in range(LAYERS):
        weights = tuple((item[layer_num] for item in gathered[:13]))
        hidden, saved_state = layer_forward(hidden, weights, offsets, key_masks)
        saved_list.append(saved_state)
    regathered = (
        lax.all_gather(qkv_weight, "shard", axis=1, tiled=True),
        lax.all_gather(query_bias, "shard", axis=1, tiled=True),
        lax.all_gather(value_bias, "shard", axis=1, tiled=True),
        lax.all_gather(proj_weight, "shard", axis=1, tiled=True),
        lax.all_gather(proj_bias, "shard", axis=1, tiled=True),
        lax.all_gather(attn_gain, "shard", axis=1, tiled=True),
        lax.all_gather(attn_shift, "shard", axis=1, tiled=True),
        lax.all_gather(up_weight, "shard", axis=1, tiled=True),
        lax.all_gather(up_bias, "shard", axis=1, tiled=True),
        lax.all_gather(down_weight, "shard", axis=1, tiled=True),
        lax.all_gather(down_bias, "shard", axis=1, tiled=True),
        lax.all_gather(ffn_gain, "shard", axis=1, tiled=True),
        lax.all_gather(ffn_shift, "shard", axis=1, tiled=True),
    )
    grad_hidden = cotangent.astype(jnp.float32)
    grads_by_layer = [None] * LAYERS
    for layer_num in range(LAYERS - 1, -1, -1):
        weights = tuple((item[layer_num] for item in regathered))
        grad_hidden, layer_grads = layer_backward(
            grad_hidden, weights, saved_list[layer_num], offsets, key_masks
        )
        grads_by_layer[layer_num] = layer_grads
    memory_full = jnp.einsum("btm,btd->md", slot_hot, grad_hidden, precision=lax.Precision.HIGHEST)
    stacked = [
        jnp.stack([grads_by_layer[layer_num][member] for layer_num in range(LAYERS)])
        for member in range(13)
    ]
    shares = (
        lax.psum_scatter(stacked[0], "shard", scatter_dimension=1, tiled=True),
        lax.psum_scatter(stacked[1], "shard", scatter_dimension=1, tiled=True),
        lax.psum_scatter(stacked[2], "shard", scatter_dimension=1, tiled=True),
        lax.psum_scatter(stacked[3], "shard", scatter_dimension=1, tiled=True),
        lax.psum_scatter(stacked[4], "shard", scatter_dimension=1, tiled=True),
        lax.psum_scatter(stacked[5], "shard", scatter_dimension=1, tiled=True),
        lax.psum_scatter(stacked[6], "shard", scatter_dimension=1, tiled=True),
        lax.psum_scatter(stacked[7], "shard", scatter_dimension=1, tiled=True),
        lax.psum_scatter(stacked[8], "shard", scatter_dimension=1, tiled=True),
        lax.psum_scatter(stacked[9], "shard", scatter_dimension=1, tiled=True),
        lax.psum_scatter(stacked[10], "shard", scatter_dimension=1, tiled=True),
        lax.psum_scatter(stacked[11], "shard", scatter_dimension=1, tiled=True),
        lax.psum_scatter(stacked[12], "shard", scatter_dimension=1, tiled=True),
        lax.psum_scatter(memory_full, "shard", scatter_dimension=1, tiled=True),
    )
    totals = (
        lax.psum(shares[0].astype(jnp.bfloat16), "rep").astype(jnp.float32),
        lax.psum(shares[1].astype(jnp.bfloat16), "rep").astype(jnp.float32),
        lax.psum(shares[2].astype(jnp.bfloat16), "rep").astype(jnp.float32),
        lax.psum(shares[3].astype(jnp.bfloat16), "rep").astype(jnp.float32),
        lax.psum(shares[4].astype(jnp.bfloat16), "rep").astype(jnp.float32),
        lax.psum(shares[5].astype(jnp.bfloat16), "rep").astype(jnp.float32),
        lax.psum(shares[6].astype(jnp.bfloat16), "rep").astype(jnp.float32),
        lax.psum(shares[7].astype(jnp.bfloat16), "rep").astype(jnp.float32),
        lax.psum(shares[8].astype(jnp.bfloat16), "rep").astype(jnp.float32),
        lax.psum(shares[9].astype(jnp.bfloat16), "rep").astype(jnp.float32),
        lax.psum(shares[10].astype(jnp.bfloat16), "rep").astype(jnp.float32),
        lax.psum(shares[11].astype(jnp.bfloat16), "rep").astype(jnp.float32),
        lax.psum(shares[12].astype(jnp.bfloat16), "rep").astype(jnp.float32),
        lax.psum(shares[13].astype(jnp.bfloat16), "rep").astype(jnp.float32),
    )
    return (
        hidden,
        grad_hidden,
        totals[13],
        totals[0],
        totals[1],
        totals[2],
        totals[3],
        totals[4],
        totals[5],
        totals[6],
        totals[7],
        totals[8],
        totals[9],
        totals[10],
        totals[11],
        totals[12],
    )


def solution(mesh):
    return jax.shard_map(
        on_device,
        mesh=mesh,
        in_specs=(
            P(None, ("rep", "shard"), None),
            P(None, ("rep", "shard"), None),
            P(None, "rep"),
            P(None, ("rep", "shard")),
            P(None, "shard"),
            P(None, "shard", None),
            P(None, "shard"),
            P(None, "shard"),
            P(None, "shard", None),
            P(None, "shard"),
            P(None, "shard"),
            P(None, "shard"),
            P(None, "shard", None),
            P(None, "shard"),
            P(None, "shard", None),
            P(None, "shard"),
            P(None, "shard"),
            P(None, "shard"),
        ),
        out_specs=(
            P(None, ("rep", "shard"), None),
            P(None, ("rep", "shard"), None),
            P(None, "shard"),
            P(None, "shard", None),
            P(None, "shard"),
            P(None, "shard"),
            P(None, "shard", None),
            P(None, "shard"),
            P(None, "shard"),
            P(None, "shard"),
            P(None, "shard", None),
            P(None, "shard"),
            P(None, "shard", None),
            P(None, "shard"),
            P(None, "shard"),
            P(None, "shard"),
        ),
        check_vma=False,
    )
```

profile of v0, /device:TPU:0, one launch (start us, length us, event | category | flops | bytes accessed | tf_op | source)
XLA Modules:
  0.0 3595.3 jit_solution(14362843414721016178)
XLA Ops:
  10.0 33.7 all-gather
  45.5 76.1 %all-gather.14.cloned.1.call-done = bf16[2,768,2304]{2,1,0:T(8,128)(2,1)} async-done(((bf16[2,96,2304]{2,1,0:T(8,128)(2,1)}), bf16[2,768,2304]{2,1,0:T(8,128)(2,1)}) %all-gather.14.cloned.1.call-update) | async-done | bytes 7077904 | tf_op jit(solution)/shard_map/all_gather | solution.py:389
  140.0 16.7 collective-permute-done
  158.1 79.5 %all-gather.2 = bf16[8,96,2]{1,2,0:T(2,128)(2,1)S(1)} all-gather(bf16[1,96,2]{1,2,0:T(2,128)(2,1)S(1)} %bitcast.1135), channel_id=1, replica_groups=mesh['rep'=4,'shard'=8] {'shard'}, dimensions={0}, use_global_device_ids=true | all-gather | bytes 3456 | tf_op jit(solution)/shard_map/all_gather | solution.py:391
  237.7 86.6 %all-gather.1 = bf16[8,96,2]{1,2,0:T(2,128)(2,1)S(1)} all-gather(bf16[1,96,2]{1,2,0:T(2,128)(2,1)S(1)} %bitcast.1136), channel_id=1, replica_groups=mesh['rep'=4,'shard'=8] {'shard'}, dimensions={0}, use_global_device_ids=true | all-gather | bytes 3456 | tf_op jit(solution)/shard_map/all_gather | solution.py:390
  349.7 94.0 %all-gather.6 = bf16[8,96,2]{1,2,0:T(2,128)(2,1)S(1)} all-gather(bf16[1,96,2]{1,2,0:T(2,128)(2,1)S(1)} %bitcast.1137), channel_id=1, replica_groups=mesh['rep'=4,'shard'=8] {'shard'}, dimensions={0}, use_global_device_ids=true | all-gather | bytes 3456 | tf_op jit(solution)/shard_map/all_gather | solution.py:399
  443.7 80.2 %all-gather.3 = bf16[8,96,2]{1,2,0:T(2,128)(2,1)S(1)} all-gather(bf16[1,96,2]{1,2,0:T(2,128)(2,1)S(1)} %bitcast.1138), channel_id=1, replica_groups=mesh['rep'=4,'shard'=8] {'shard'}, dimensions={0}, use_global_device_ids=true | all-gather | bytes 3456 | tf_op jit(solution)/shard_map/all_gather | solution.py:393
  529.9 17.0 all-gather.5
  547.0 18.9 all-gather.4
  565.9 16.8 all-gather.8
  582.8 18.3 all-gather.7
  601.3 30.0 all_gather.57
  711.0 8.8 conditional.68
  758.0 15.7 multiply_convert_fusion.19
  784.5 45.2 %collective-permute-start.16 = (bf16[2,256,768]{2,1,0:T(8,128)(2,1)S(1)}, bf16[2,256,768]{2,1,0:T(8,128)(2,1)S(1)}, u32[]{:S(2)}, u32[]{:S(2)}) collective-permute-start(bf16[2,256,768]{2,1,0:T(8,128)(2,1)S(1)} %slice.278), channel_id=1, source_target_pairs={{0,4},{1,5},{2,6},{3,7},{8,12},{9,13},{10,14},{11,15},{16,20},{17,... | collective-permute-start | bytes 2359304 | tf_op jit(solution)/shard_map/ppermute | solution.py:20
  840.5 13.3 collective-permute-done.17
  863.6 66.7 %collective-permute-start.24 = (bf16[2,256,768]{2,1,0:T(8,128)(2,1)}, bf16[2,256,768]{2,1,0:T(8,128)(2,1)S(1)}, u32[]{:S(2)}, u32[]{:S(2)}) collective-permute-start(bf16[2,256,768]{2,1,0:T(8,128)(2,1)} %get-tuple-element.2498), channel_id=1, source_target_pairs={{0,4},{1,5},{2,6},{3,7},{8,12},{9,13},{10,14},{11,15},{16,20},{17,... | collective-permute-start | bytes 2359304 | tf_op jit(solution)/shard_map/ppermute | solution.py:20
  941.4 13.3 collective-permute-done.25
  974.0 9.5 conditional.77
  983.5 9.6 conditional.78
  1017.6 8.8 conditional.86
  1026.4 9.0 conditional.87
  1035.5 8.8 conditional.88
  1044.3 9.0 conditional.89
  1064.2 14.9 multiply_convert_fusion.18
  1089.4 18.1 convert_reduce_fusion
  1127.6 25.9 conditional.90
  1162.9 20.2 conditional.95
  1183.2 18.7 conditional.96
  1201.9 20.3 conditional.97
  1222.2 18.7 conditional.98
  1243.2 80.7 %collective-permute-start.47 = (bf16[2,256,768]{2,1,0:T(8,128)(2,1)}, bf16[2,256,768]{2,1,0:T(8,128)(2,1)}, u32[]{:S(2)}, u32[]{:S(2)}) collective-permute-start(bf16[2,256,768]{2,1,0:T(8,128)(2,1)} %copy.541), channel_id=1, source_target_pairs={{0,4},{1,5},{2,6},{3,7},{8,12},{9,13},{10,14},{11,15},{16,20},{17,... | collective-permute-start | bytes 2359304 | tf_op jit(solution)/shard_map/ppermute | solution.py:20
  1326.2 12.9 collective-permute-start.46
  1369.3 9.8 collective-permute-done.44
  1379.0 50.7 %collective-permute-start.39 = (bf16[2,256,768]{2,1,0:T(8,128)(2,1)}, bf16[2,256,768]{2,1,0:T(8,128)(2,1)}, u32[]{:S(2)}, u32[]{:S(2)}) collective-permute-start(bf16[2,256,768]{2,1,0:T(8,128)(2,1)} %copy.532), channel_id=1, source_target_pairs={{0,4},{1,5},{2,6},{3,7},{8,12},{9,13},{10,14},{11,15},{16,20},{17,... | collective-permute-start | bytes 2359304 | tf_op jit(solution)/shard_map/ppermute | solution.py:20
  1458.6 10.7 collective-permute-done.38
  1470.6 15.6 collective-permute-done.37
  1498.1 66.7 %collective-permute-done.32 = bf16[2,256,768]{2,1,0:T(8,128)(2,1)S(1)} collective-permute-done((bf16[2,256,768]{2,1,0:T(8,128)(2,1)}, bf16[2,256,768]{2,1,0:T(8,128)(2,1)S(1)}, u32[]{:S(2)}, u32[]{:S(2)}) %collective-permute-start.32) | collective-permute-done | bytes 786464 | tf_op jit(solution)/shard_map/ppermute | solution.py:20
  1607.4 26.0 conditional.99
  1642.8 20.4 conditional.104
  1663.2 18.8 conditional.105
  1682.0 18.1 conditional.106
  1700.2 18.4 conditional.107
  1720.0 33.2 collective-permute-start.63
  1790.1 59.1 %collective-permute-start.55 = (bf16[2,256,768]{2,1,0:T(8,128)(2,1)}, bf16[2,256,768]{2,1,0:T(8,128)(2,1)}, u32[]{:S(2)}, u32[]{:S(2)}) collective-permute-start(bf16[2,256,768]{2,1,0:T(8,128)(2,1)} %copy.572), channel_id=1, source_target_pairs={{0,4},{1,5},{2,6},{3,7},{8,12},{9,13},{10,14},{11,15},{16,20},{17,... | collective-permute-start | bytes 2359304 | tf_op jit(solution)/shard_map/ppermute | solution.py:20
  1872.9 19.2 collective-permute-done.54
  1893.3 15.6 collective-permute-done.53
  1921.4 53.5 %collective-permute-done.48 = bf16[2,256,768]{2,1,0:T(8,128)(2,1)S(1)} collective-permute-done((bf16[2,256,768]{2,1,0:T(8,128)(2,1)}, bf16[2,256,768]{2,1,0:T(8,128)(2,1)S(1)}, u32[]{:S(2)}, u32[]{:S(2)}) %collective-permute-start.48) | collective-permute-done | bytes 786464 | tf_op jit(solution)/shard_map/ppermute | solution.py:20
  1983.7 11.0 pad_maximum_fusion.2
  2048.6 180.0 %reduce-scatter.35.cloned.1.call-done = f32[2,96,2304]{2,1,0:T(8,128)} async-done(((f32[2,768,2304]{2,1,0:T(8,128)}), f32[2,96,2304]{2,1,0:T(8,128)}) %reduce-scatter.35.cloned.1.call-update) | async-done | bytes 1769488 | tf_op jit(solution)/shard_map/reduce_scatter | solution.py:443
  2231.1 310.2 %reduce-scatter.39.cloned.1.call-done = f32[2,96,3072]{2,1,0:T(8,128)} async-done(((f32[2,768,3072]{2,1,0:T(8,128)}), f32[2,96,3072]{2,1,0:T(8,128)}) %reduce-scatter.39.cloned.1.call-update) | async-done | bytes 2359312 | tf_op jit(solution)/shard_map/reduce_scatter | solution.py:450
  2544.2 309.9 %reduce-scatter.41.cloned.1.call-done = f32[2,384,768]{2,1,0:T(8,128)} async-done(((f32[2,3072,768]{2,1,0:T(8,128)}), f32[2,384,768]{2,1,0:T(8,128)}) %reduce-scatter.41.cloned.1.call-update) | async-done | bytes 2359312 | tf_op jit(solution)/shard_map/reduce_scatter | solution.py:452
  2856.9 61.8 %reduce-scatter.45.cloned.1.call-done = f32[96,2]{1,0:T(8,128)} async-done(((f32[768,2]{1,0:T(8,128)}), f32[96,2]{1,0:T(8,128)}) %reduce-scatter.45.cloned.1.call-update) | async-done | bytes 784
  2919.6 63.4 %reduce-scatter.49.cloned.1.call-done = f32[96,2]{1,0:T(8,128)} async-done(((f32[768,2]{1,0:T(8,128)}), f32[96,2]{1,0:T(8,128)}) %reduce-scatter.49.cloned.1.call-update) | async-done | bytes 784
  2983.9 63.6 %reduce-scatter.51.cloned.1.call-done = f32[96,2]{1,0:T(8,128)} async-done(((f32[768,2]{1,0:T(8,128)}), f32[96,2]{1,0:T(8,128)}) %reduce-scatter.51.cloned.1.call-update) | async-done | bytes 784
  3048.4 63.6 %reduce-scatter.53.cloned.1.call-done = f32[96,2]{1,0:T(8,128)} async-done(((f32[768,2]{1,0:T(8,128)}), f32[96,2]{1,0:T(8,128)}) %reduce-scatter.53.cloned.1.call-update) | async-done | bytes 784
  3112.8 63.6 %reduce-scatter.57.cloned.1.call-done = f32[96,2]{1,0:T(8,128)} async-done(((f32[768,2]{1,0:T(8,128)}), f32[96,2]{1,0:T(8,128)}) %reduce-scatter.57.cloned.1.call-update) | async-done | bytes 784
  3177.3 63.5 %reduce-scatter.59.cloned.1.call-done = f32[96,2]{1,0:T(8,128)} async-done(((f32[768,2]{1,0:T(8,128)}), f32[96,2]{1,0:T(8,128)}) %reduce-scatter.59.cloned.1.call-update) | async-done | bytes 784
  3241.7 63.5 %reduce-scatter.61.cloned.1.call-done = f32[96,2]{1,0:T(8,128)} async-done(((f32[768,2]{1,0:T(8,128)}), f32[96,2]{1,0:T(8,128)}) %reduce-scatter.61.cloned.1.call-update) | async-done | bytes 784
  3306.0 67.5 %reduce-scatter.55.cloned.1.call-done = f32[384,2]{1,0:T(8,128)} async-done(((f32[3072,2]{1,0:T(8,128)}), f32[384,2]{1,0:T(8,128)}) %reduce-scatter.55.cloned.1.call-update) | async-done | bytes 3088
  3374.5 63.1 %reduce-scatter.47.cloned.1.call-done = f32[96,2]{1,0:T(8,128)} async-done(((f32[768,2]{1,0:T(8,128)}), f32[96,2]{1,0:T(8,128)}) %reduce-scatter.47.cloned.1.call-update) | async-done | bytes 784
  3438.5 64.0 %reduce-scatter.43.cloned.1.call-done = f32[96,20]{1,0:T(8,128)} async-done(((f32[768,20]{1,0:T(8,128)}), f32[96,20]{1,0:T(8,128)}) %reduce-scatter.43.cloned.1.call-update) | async-done | bytes 7696
  3503.4 10.7 all-reduce
  3519.8 59.9 %all-reduce.4.cloned.1.call-done = (bf16[2,96,2304]{2,1,0:T(8,128)(2,1)}, bf16[2,96,768]{2,1,0:T(8,128)(2,1)}, bf16[2,96,3072]{2,1,0:T(8,128)(2,1)}, bf16[2,384,768]{2,1,0:T(8,128)(2,1)}) async-done(((bf16[2,96,2304]{2,1,0:T(8,128)(2,1)}, bf16[2,96,768]{2,1,0:T(8,128)(2,1)}, bf16[2,96,3072]{2,1,0:T(8,128)(2,1)}, bf16[2,384,768]{2,1,0:T(8,128)(2,1)}), (bf16[2,96,2304]{2,1,0:T(8,128)(2,1)}, ...) | async-done | bytes 3538960 | tf_op jit(solution)/shard_map/psum | solution.py:459
  (1002 shorter events, 978.9 us)
Async XLA Ops:
  7.2 114.4 %all-gather.14.cloned.1.call-start = ((), (), s32[]{:S(2)}) async-start(), calls=%async_computation.14 | async-start | bytes 7962624 | tf_op jit(solution)/shard_map/all_gather | solution.py:389
  7.9 735.4 %all-gather.16.cloned.1.call-start = ((), (), s32[]{:S(2)}) async-start(), calls=%async_computation.15 | async-start | bytes 2654208 | tf_op jit(solution)/shard_map/all_gather | solution.py:392
  8.7 739.3 %all-gather.18.cloned.1.call-start = ((), (), s32[]{:S(2)}) async-start(), calls=%async_computation.16 | async-start | bytes 10616832 | tf_op jit(solution)/shard_map/all_gather | solution.py:396
  9.4 764.3 %all-gather.20.cloned.1.call-start = ((), (), s32[]{:S(2)}) async-start(), calls=%async_computation.17 | async-start | bytes 10616832 | tf_op jit(solution)/shard_map/all_gather | solution.py:398
  10.0 2036.9 %reduce-scatter.37.cloned.1.call-start = ((), (), s32[]{:S(2)}) async-start(), calls=%async_computation.19 | async-start | bytes 5308416 | tf_op jit(solution)/shard_map/reduce_scatter | solution.py:446
  129.4 201.0 %collective-permute-start.1 = (bf16[2,256,768]{2,1,0:T(8,128)(2,1)S(1)}, bf16[2,256,768]{2,1,0:T(8,128)(2,1)}, u32[]{:S(2)}, u32[]{:S(2)}) collective-permute-start(bf16[2,256,768]{2,1,0:T(8,128)(2,1)S(1)} %slice.279), channel_id=1, source_target_pairs={{0,3},{1,4},{2,5},{3,6},{4,7},{8,11},{9,12},{10,13},{11,14},{12,15... | collective-permute-start | bytes 2359304 | tf_op jit(solution)/shard_map/ppermute | solution.py:20
  132.8 198.9 %collective-permute-start.2 = (bf16[2,256,768]{2,1,0:T(8,128)(2,1)S(1)}, bf16[2,256,768]{2,1,0:T(8,128)(2,1)}, u32[]{:S(2)}, u32[]{:S(2)}) collective-permute-start(bf16[2,256,768]{2,1,0:T(8,128)(2,1)S(1)} %slice.279), channel_id=1, source_target_pairs={{0,2},{1,3},{2,4},{3,5},{4,6},{5,7},{8,10},{9,11},{10,12},{11,13},... | collective-permute-start | bytes 2359304 | tf_op jit(solution)/shard_map/ppermute | solution.py:20
  135.4 197.6 %collective-permute-start.3 = (bf16[2,256,768]{2,1,0:T(8,128)(2,1)S(1)}, bf16[2,256,768]{2,1,0:T(8,128)(2,1)}, u32[]{:S(2)}, u32[]{:S(2)}) collective-permute-start(bf16[2,256,768]{2,1,0:T(8,128)(2,1)S(1)} %slice.279), channel_id=1, source_target_pairs={{0,1},{1,2},{2,3},{3,4},{4,5},{5,6},{6,7},{8,9},{9,10},{10,11},{11... | collective-permute-start | bytes 2359304 | tf_op jit(solution)/shard_map/ppermute | solution.py:20
  138.7 201.5 %collective-permute-start.4 = (bf16[2,256,768]{2,1,0:T(8,128)(2,1)S(1)}, bf16[2,256,768]{2,1,0:T(8,128)(2,1)S(1)}, u32[]{:S(2)}, u32[]{:S(2)}) collective-permute-start(bf16[2,256,768]{2,1,0:T(8,128)(2,1)S(1)} %slice.279), channel_id=1, source_target_pairs={{1,0},{2,1},{3,2},{4,3},{5,4},{6,5},{7,6},{9,8},{10,9},{11,10},{12... | collective-permute-start | bytes 2359304 | tf_op jit(solution)/shard_map/ppermute | solution.py:20
  156.7 189.9 %collective-permute-start.5 = (bf16[2,256,768]{2,1,0:T(8,128)(2,1)S(1)}, bf16[2,256,768]{2,1,0:T(8,128)(2,1)S(1)}, u32[]{:S(2)}, u32[]{:S(2)}) collective-permute-start(bf16[2,256,768]{2,1,0:T(8,128)(2,1)S(1)} %slice.279), channel_id=1, source_target_pairs={{2,0},{3,1},{4,2},{5,3},{6,4},{7,5},{10,8},{11,9},{12,10},{13,11},... | collective-permute-start | bytes 2359304 | tf_op jit(solution)/shard_map/ppermute | solution.py:20
  330.4 304.5 %collective-permute-start.6 = (bf16[2,256,768]{2,1,0:T(8,128)(2,1)S(1)}, bf16[2,256,768]{2,1,0:T(8,128)(2,1)}, u32[]{:S(2)}, u32[]{:S(2)}) collective-permute-start(bf16[2,256,768]{2,1,0:T(8,128)(2,1)S(1)} %slice.279), channel_id=1, source_target_pairs={{3,0},{4,1},{5,2},{6,3},{7,4},{11,8},{12,9},{13,10},{14,11},{15,12... | collective-permute-start | bytes 2359304 | tf_op jit(solution)/shard_map/ppermute | solution.py:20
  331.7 308.1 %collective-permute-start.7 = (bf16[2,256,768]{2,1,0:T(8,128)(2,1)S(1)}, bf16[2,256,768]{2,1,0:T(8,128)(2,1)}, u32[]{:S(2)}, u32[]{:S(2)}) collective-permute-start(bf16[2,256,768]{2,1,0:T(8,128)(2,1)S(1)} %slice.279), channel_id=1, source_target_pairs={{4,0},{5,1},{6,2},{7,3},{12,8},{13,9},{14,10},{15,11},{20,16},{21,... | collective-permute-start | bytes 2359304 | tf_op jit(solution)/shard_map/ppermute | solution.py:20
  333.1 308.1 %collective-permute-start.8 = (bf16[2,256,768]{2,1,0:T(8,128)(2,1)}, bf16[2,256,768]{2,1,0:T(8,128)(2,1)}, u32[]{:S(2)}, u32[]{:S(2)}) collective-permute-start(bf16[2,256,768]{2,1,0:T(8,128)(2,1)} %get-tuple-element.2500), channel_id=1, source_target_pairs={{0,4},{1,5},{2,6},{3,7},{8,12},{9,13},{10,14},{11,15},{16,20},{17,... | collective-permute-start | bytes 2359304 | tf_op jit(solution)/shard_map/ppermute | solution.py:20
  340.3 302.2 %collective-permute-start.9 = (bf16[2,256,768]{2,1,0:T(8,128)(2,1)}, bf16[2,256,768]{2,1,0:T(8,128)(2,1)}, u32[]{:S(2)}, u32[]{:S(2)}) collective-permute-start(bf16[2,256,768]{2,1,0:T(8,128)(2,1)} %get-tuple-element.2500), channel_id=1, source_target_pairs={{0,3},{1,4},{2,5},{3,6},{4,7},{8,11},{9,12},{10,13},{11,14},{12,15... | collective-permute-start | bytes 2359304 | tf_op jit(solution)/shard_map/ppermute | solution.py:20
  346.6 297.2 %collective-permute-start.10 = (bf16[2,256,768]{2,1,0:T(8,128)(2,1)}, bf16[2,256,768]{2,1,0:T(8,128)(2,1)}, u32[]{:S(2)}, u32[]{:S(2)}) collective-permute-start(bf16[2,256,768]{2,1,0:T(8,128)(2,1)} %get-tuple-element.2500), channel_id=1, source_target_pairs={{0,2},{1,3},{2,4},{3,5},{4,6},{5,7},{8,10},{9,11},{10,12},{11,13},... | collective-permute-start | bytes 2359304 | tf_op jit(solution)/shard_map/ppermute | solution.py:20
  635.0 66.5 %collective-permute-start.11 = (bf16[2,256,768]{2,1,0:T(8,128)(2,1)}, bf16[2,256,768]{2,1,0:T(8,128)(2,1)}, u32[]{:S(2)}, u32[]{:S(2)}) collective-permute-start(bf16[2,256,768]{2,1,0:T(8,128)(2,1)} %get-tuple-element.2500), channel_id=1, source_target_pairs={{0,1},{1,2},{2,3},{3,4},{4,5},{5,6},{6,7},{8,9},{9,10},{10,11},{11... | collective-permute-start | bytes 2359304 | tf_op jit(solution)/shard_map/ppermute | solution.py:20
  639.9 71.1 %collective-permute-start.12 = (bf16[2,256,768]{2,1,0:T(8,128)(2,1)}, bf16[2,256,768]{2,1,0:T(8,128)(2,1)}, u32[]{:S(2)}, u32[]{:S(2)}) collective-permute-start(bf16[2,256,768]{2,1,0:T(8,128)(2,1)} %get-tuple-element.2500), channel_id=1, source_target_pairs={{1,0},{2,1},{3,2},{4,3},{5,4},{6,5},{7,6},{9,8},{10,9},{11,10},{12... | collective-permute-start | bytes 2359304 | tf_op jit(solution)/shard_map/ppermute | solution.py:20
  641.2 78.7 %collective-permute-start.13 = (bf16[2,256,768]{2,1,0:T(8,128)(2,1)}, bf16[2,256,768]{2,1,0:T(8,128)(2,1)}, u32[]{:S(2)}, u32[]{:S(2)}) collective-permute-start(bf16[2,256,768]{2,1,0:T(8,128)(2,1)} %get-tuple-element.2500), channel_id=1, source_target_pairs={{2,0},{3,1},{4,2},{5,3},{6,4},{7,5},{10,8},{11,9},{12,10},{13,11},... | collective-permute-start | bytes 2359304 | tf_op jit(solution)/shard_map/ppermute | solution.py:20
  642.5 85.1 %collective-permute-start.14 = (bf16[2,256,768]{2,1,0:T(8,128)(2,1)}, bf16[2,256,768]{2,1,0:T(8,128)(2,1)}, u32[]{:S(2)}, u32[]{:S(2)}) collective-permute-start(bf16[2,256,768]{2,1,0:T(8,128)(2,1)} %get-tuple-element.2500), channel_id=1, source_target_pairs={{3,0},{4,1},{5,2},{6,3},{7,4},{11,8},{12,9},{13,10},{14,11},{15,12... | collective-permute-start | bytes 2359304 | tf_op jit(solution)/shard_map/ppermute | solution.py:20
  643.8 91.5 %collective-permute-start.15 = (bf16[2,256,768]{2,1,0:T(8,128)(2,1)}, bf16[2,256,768]{2,1,0:T(8,128)(2,1)}, u32[]{:S(2)}, u32[]{:S(2)}) collective-permute-start(bf16[2,256,768]{2,1,0:T(8,128)(2,1)} %get-tuple-element.2500), channel_id=1, source_target_pairs={{4,0},{5,1},{6,2},{7,3},{12,8},{13,9},{14,10},{15,11},{20,16},{21,... | collective-permute-start | bytes 2359304 | tf_op jit(solution)/shard_map/ppermute | solution.py:20
  784.5 54.7 %collective-permute-start.16 = (bf16[2,256,768]{2,1,0:T(8,128)(2,1)S(1)}, bf16[2,256,768]{2,1,0:T(8,128)(2,1)S(1)}, u32[]{:S(2)}, u32[]{:S(2)}) collective-permute-start(bf16[2,256,768]{2,1,0:T(8,128)(2,1)S(1)} %slice.278), channel_id=1, source_target_pairs={{0,4},{1,5},{2,6},{3,7},{8,12},{9,13},{10,14},{11,15},{16,20},{17,... | collective-permute-start | bytes 2359304 | tf_op jit(solution)/shard_map/ppermute | solution.py:20
  836.0 94.3 %collective-permute-start.20 = (bf16[2,256,768]{2,1,0:T(8,128)(2,1)S(1)}, bf16[2,256,768]{2,1,0:T(8,128)(2,1)S(1)}, u32[]{:S(2)}, u32[]{:S(2)}) collective-permute-start(bf16[2,256,768]{2,1,0:T(8,128)(2,1)S(1)} %slice.278), channel_id=1, source_target_pairs={{1,0},{2,1},{3,2},{4,3},{5,4},{6,5},{7,6},{9,8},{10,9},{11,10},{12... | collective-permute-start | bytes 2359304 | tf_op jit(solution)/shard_map/ppermute | solution.py:20
  839.2 92.5 %collective-permute-start.21 = (bf16[2,256,768]{2,1,0:T(8,128)(2,1)S(1)}, bf16[2,256,768]{2,1,0:T(8,128)(2,1)S(1)}, u32[]{:S(2)}, u32[]{:S(2)}) collective-permute-start(bf16[2,256,768]{2,1,0:T(8,128)(2,1)S(1)} %slice.278), channel_id=1, source_target_pairs={{2,0},{3,1},{4,2},{5,3},{6,4},{7,5},{10,8},{11,9},{12,10},{13,11},... | collective-permute-start | bytes 2359304 | tf_op jit(solution)/shard_map/ppermute | solution.py:20
  854.8 78.3 %collective-permute-start.22 = (bf16[2,256,768]{2,1,0:T(8,128)(2,1)S(1)}, bf16[2,256,768]{2,1,0:T(8,128)(2,1)S(1)}, u32[]{:S(2)}, u32[]{:S(2)}) collective-permute-start(bf16[2,256,768]{2,1,0:T(8,128)(2,1)S(1)} %slice.278), channel_id=1, source_target_pairs={{3,0},{4,1},{5,2},{6,3},{7,4},{11,8},{12,9},{13,10},{14,11},{15,12... | collective-permute-start | bytes 2359304 | tf_op jit(solution)/shard_map/ppermute | solution.py:20
  862.3 76.1 %collective-permute-start.23 = (bf16[2,256,768]{2,1,0:T(8,128)(2,1)S(1)}, bf16[2,256,768]{2,1,0:T(8,128)(2,1)S(1)}, u32[]{:S(2)}, u32[]{:S(2)}) collective-permute-start(bf16[2,256,768]{2,1,0:T(8,128)(2,1)S(1)} %slice.278), channel_id=1, source_target_pairs={{4,0},{5,1},{6,2},{7,3},{12,8},{13,9},{14,10},{15,11},{20,16},{21,... | collective-permute-start | bytes 2359304 | tf_op jit(solution)/shard_map/ppermute | solution.py:20
  863.6 76.6 %collective-permute-start.24 = (bf16[2,256,768]{2,1,0:T(8,128)(2,1)}, bf16[2,256,768]{2,1,0:T(8,128)(2,1)S(1)}, u32[]{:S(2)}, u32[]{:S(2)}) collective-permute-start(bf16[2,256,768]{2,1,0:T(8,128)(2,1)} %get-tuple-element.2498), channel_id=1, source_target_pairs={{0,4},{1,5},{2,6},{3,7},{8,12},{9,13},{10,14},{11,15},{16,20},{17,... | collective-permute-start | bytes 2359304 | tf_op jit(solution)/shard_map/ppermute | solution.py:20
  933.1 83.6 %collective-permute-start.27 = (bf16[2,256,768]{2,1,0:T(8,128)(2,1)}, bf16[2,256,768]{2,1,0:T(8,128)(2,1)}, u32[]{:S(2)}, u32[]{:S(2)}) collective-permute-start(bf16[2,256,768]{2,1,0:T(8,128)(2,1)} %get-tuple-element.2498), channel_id=1, source_target_pairs={{0,1},{1,2},{2,3},{3,4},{4,5},{5,6},{6,7},{8,9},{9,10},{10,11},{11... | collective-permute-start | bytes 2359304 | tf_op jit(solution)/shard_map/ppermute | solution.py:20
  938.4 78.4 %collective-permute-start.28 = (bf16[2,256,768]{2,1,0:T(8,128)(2,1)}, bf16[2,256,768]{2,1,0:T(8,128)(2,1)}, u32[]{:S(2)}, u32[]{:S(2)}) collective-permute-start(bf16[2,256,768]{2,1,0:T(8,128)(2,1)} %get-tuple-element.2498), channel_id=1, source_target_pairs={{1,0},{2,1},{3,2},{4,3},{5,4},{6,5},{7,6},{9,8},{10,9},{11,10},{12... | collective-permute-start | bytes 2359304 | tf_op jit(solution)/shard_map/ppermute | solution.py:20
  940.1 86.3 %collective-permute-start.29 = (bf16[2,256,768]{2,1,0:T(8,128)(2,1)}, bf16[2,256,768]{2,1,0:T(8,128)(2,1)}, u32[]{:S(2)}, u32[]{:S(2)}) collective-permute-start(bf16[2,256,768]{2,1,0:T(8,128)(2,1)} %get-tuple-element.2498), channel_id=1, source_target_pairs={{2,0},{3,1},{4,2},{5,3},{6,4},{7,5},{10,8},{11,9},{12,10},{13,11},... | collective-permute-start | bytes 2359304 | tf_op jit(solution)/shard_map/ppermute | solution.py:20
  954.7 80.7 %collective-permute-start.30 = (bf16[2,256,768]{2,1,0:T(8,128)(2,1)}, bf16[2,256,768]{2,1,0:T(8,128)(2,1)}, u32[]{:S(2)}, u32[]{:S(2)}) collective-permute-start(bf16[2,256,768]{2,1,0:T(8,128)(2,1)} %get-tuple-element.2498), channel_id=1, source_target_pairs={{3,0},{4,1},{5,2},{6,3},{7,4},{11,8},{12,9},{13,10},{14,11},{15,12... | collective-permute-start | bytes 2359304 | tf_op jit(solution)/shard_map/ppermute | solution.py:20
  963.2 81.1 %collective-permute-start.31 = (bf16[2,256,768]{2,1,0:T(8,128)(2,1)}, bf16[2,256,768]{2,1,0:T(8,128)(2,1)}, u32[]{:S(2)}, u32[]{:S(2)}) collective-permute-start(bf16[2,256,768]{2,1,0:T(8,128)(2,1)} %get-tuple-element.2498), channel_id=1, source_target_pairs={{4,0},{5,1},{6,2},{7,3},{12,8},{13,9},{14,10},{15,11},{20,16},{21,... | collective-permute-start | bytes 2359304 | tf_op jit(solution)/shard_map/ppermute | solution.py:20
  1243.2 109.9 %collective-permute-start.47 = (bf16[2,256,768]{2,1,0:T(8,128)(2,1)}, bf16[2,256,768]{2,1,0:T(8,128)(2,1)}, u32[]{:S(2)}, u32[]{:S(2)}) collective-permute-start(bf16[2,256,768]{2,1,0:T(8,128)(2,1)} %copy.541), channel_id=1, source_target_pairs={{0,4},{1,5},{2,6},{3,7},{8,12},{9,13},{10,14},{11,15},{16,20},{17,... | collective-permute-start | bytes 2359304 | tf_op jit(solution)/shard_map/ppermute | solution.py:20
  1350.4 79.3 %collective-permute-start.43 = (bf16[2,256,768]{2,1,0:T(8,128)(2,1)S(1)}, bf16[2,256,768]{2,1,0:T(8,128)(2,1)}, u32[]{:S(2)}, u32[]{:S(2)}) collective-permute-start(bf16[2,256,768]{2,1,0:T(8,128)(2,1)S(1)} %copy.537), channel_id=1, source_target_pairs={{1,0},{2,1},{3,2},{4,3},{5,4},{6,5},{7,6},{9,8},{10,9},{11,10},{12... | collective-permute-start | bytes 2359304 | tf_op jit(solution)/shard_map/ppermute | solution.py:20
  1353.1 78.8 %collective-permute-start.42 = (bf16[2,256,768]{2,1,0:T(8,128)(2,1)S(1)}, bf16[2,256,768]{2,1,0:T(8,128)(2,1)}, u32[]{:S(2)}, u32[]{:S(2)}) collective-permute-start(bf16[2,256,768]{2,1,0:T(8,128)(2,1)S(1)} %copy.536), channel_id=1, source_target_pairs={{2,0},{3,1},{4,2},{5,3},{6,4},{7,5},{10,8},{11,9},{12,10},{13,11},... | collective-permute-start | bytes 2359304 | tf_op jit(solution)/shard_map/ppermute | solution.py:20
  1365.9 80.7 %collective-permute-start.41 = (bf16[2,256,768]{2,1,0:T(8,128)(2,1)}, bf16[2,256,768]{2,1,0:T(8,128)(2,1)}, u32[]{:S(2)}, u32[]{:S(2)}) collective-permute-start(bf16[2,256,768]{2,1,0:T(8,128)(2,1)} %copy.535), channel_id=1, source_target_pairs={{3,0},{4,1},{5,2},{6,3},{7,4},{11,8},{12,9},{13,10},{14,11},{15,12... | collective-permute-start | bytes 2359304 | tf_op jit(solution)/shard_map/ppermute | solution.py:20
  1368.0 88.1 %collective-permute-start.40 = (bf16[2,256,768]{2,1,0:T(8,128)(2,1)}, bf16[2,256,768]{2,1,0:T(8,128)(2,1)}, u32[]{:S(2)}, u32[]{:S(2)}) collective-permute-start(bf16[2,256,768]{2,1,0:T(8,128)(2,1)} %copy.533), channel_id=1, source_target_pairs={{4,0},{5,1},{6,2},{7,3},{12,8},{13,9},{14,10},{15,11},{20,16},{21,... | collective-permute-start | bytes 2359304 | tf_op jit(solution)/shard_map/ppermute | solution.py:20
  1379.0 78.3 %collective-permute-start.39 = (bf16[2,256,768]{2,1,0:T(8,128)(2,1)}, bf16[2,256,768]{2,1,0:T(8,128)(2,1)}, u32[]{:S(2)}, u32[]{:S(2)}) collective-permute-start(bf16[2,256,768]{2,1,0:T(8,128)(2,1)} %copy.532), channel_id=1, source_target_pairs={{0,4},{1,5},{2,6},{3,7},{8,12},{9,13},{10,14},{11,15},{16,20},{17,... | collective-permute-start | bytes 2359304 | tf_op jit(solution)/shard_map/ppermute | solution.py:20
  1431.9 54.3 %collective-permute-start.37 = (bf16[2,256,768]{2,1,0:T(8,128)(2,1)}, bf16[2,256,768]{2,1,0:T(8,128)(2,1)}, u32[]{:S(2)}, u32[]{:S(2)}) collective-permute-start(bf16[2,256,768]{2,1,0:T(8,128)(2,1)} %copy.530), channel_id=1, source_target_pairs={{0,2},{1,3},{2,4},{3,5},{4,6},{5,7},{8,10},{9,11},{10,12},{11,13},... | collective-permute-start | bytes 2359304 | tf_op jit(solution)/shard_map/ppermute | solution.py:20
  1486.2 78.7 %collective-permute-start.32 = (bf16[2,256,768]{2,1,0:T(8,128)(2,1)}, bf16[2,256,768]{2,1,0:T(8,128)(2,1)S(1)}, u32[]{:S(2)}, u32[]{:S(2)}) collective-permute-start(bf16[2,256,768]{2,1,0:T(8,128)(2,1)} %copy.524), channel_id=1, source_target_pairs={{4,0},{5,1},{6,2},{7,3},{12,8},{13,9},{14,10},{15,11},{20,16},{21,... | collective-permute-start | bytes 2359304 | tf_op jit(solution)/shard_map/ppermute | solution.py:20
  1595.3 633.3 %reduce-scatter.35.cloned.1.call-start = ((), (), s32[]{:S(2)}) async-start(), calls=%async_computation.18 | async-start | bytes 15925248 | tf_op jit(solution)/shard_map/reduce_scatter | solution.py:443
  1720.0 54.6 %collective-permute-start.63 = (bf16[2,256,768]{2,1,0:T(8,128)(2,1)S(1)}, bf16[2,256,768]{2,1,0:T(8,128)(2,1)S(1)}, u32[]{:S(2)}, u32[]{:S(2)}) collective-permute-start(bf16[2,256,768]{2,1,0:T(8,128)(2,1)S(1)} %copy.581), channel_id=1, source_target_pairs={{0,4},{1,5},{2,6},{3,7},{8,12},{9,13},{10,14},{11,15},{16,20},{17,... | collective-permute-start | bytes 2359304 | tf_op jit(solution)/shard_map/ppermute | solution.py:20
  1771.0 78.3 %collective-permute-start.59 = (bf16[2,256,768]{2,1,0:T(8,128)(2,1)}, bf16[2,256,768]{2,1,0:T(8,128)(2,1)}, u32[]{:S(2)}, u32[]{:S(2)}) collective-permute-start(bf16[2,256,768]{2,1,0:T(8,128)(2,1)} %copy.577), channel_id=1, source_target_pairs={{1,0},{2,1},{3,2},{4,3},{5,4},{6,5},{7,6},{9,8},{10,9},{11,10},{12... | collective-permute-start | bytes 2359304 | tf_op jit(solution)/shard_map/ppermute | solution.py:20
  1774.6 76.9 %collective-permute-start.58 = (bf16[2,256,768]{2,1,0:T(8,128)(2,1)}, bf16[2,256,768]{2,1,0:T(8,128)(2,1)}, u32[]{:S(2)}, u32[]{:S(2)}) collective-permute-start(bf16[2,256,768]{2,1,0:T(8,128)(2,1)} %copy.576), channel_id=1, source_target_pairs={{2,0},{3,1},{4,2},{5,3},{6,4},{7,5},{10,8},{11,9},{12,10},{13,11},... | collective-permute-start | bytes 2359304 | tf_op jit(solution)/shard_map/ppermute | solution.py:20
  1787.3 80.2 %collective-permute-start.57 = (bf16[2,256,768]{2,1,0:T(8,128)(2,1)}, bf16[2,256,768]{2,1,0:T(8,128)(2,1)}, u32[]{:S(2)}, u32[]{:S(2)}) collective-permute-start(bf16[2,256,768]{2,1,0:T(8,128)(2,1)} %copy.575), channel_id=1, source_target_pairs={{3,0},{4,1},{5,2},{6,3},{7,4},{11,8},{12,9},{13,10},{14,11},{15,12... | collective-permute-start | bytes 2359304 | tf_op jit(solution)/shard_map/ppermute | solution.py:20
  1788.8 81.5 %collective-permute-start.56 = (bf16[2,256,768]{2,1,0:T(8,128)(2,1)}, bf16[2,256,768]{2,1,0:T(8,128)(2,1)}, u32[]{:S(2)}, u32[]{:S(2)}) collective-permute-start(bf16[2,256,768]{2,1,0:T(8,128)(2,1)} %copy.573), channel_id=1, source_target_pairs={{4,0},{5,1},{6,2},{7,3},{12,8},{13,9},{14,10},{15,11},{20,16},{21,... | collective-permute-start | bytes 2359304 | tf_op jit(solution)/shard_map/ppermute | solution.py:20
  1790.1 81.5 %collective-permute-start.55 = (bf16[2,256,768]{2,1,0:T(8,128)(2,1)}, bf16[2,256,768]{2,1,0:T(8,128)(2,1)}, u32[]{:S(2)}, u32[]{:S(2)}) collective-permute-start(bf16[2,256,768]{2,1,0:T(8,128)(2,1)} %copy.572), channel_id=1, source_target_pairs={{0,4},{1,5},{2,6},{3,7},{8,12},{9,13},{10,14},{11,15},{16,20},{17,... | collective-permute-start | bytes 2359304 | tf_op jit(solution)/shard_map/ppermute | solution.py:20
  1851.4 57.5 %collective-permute-start.53 = (bf16[2,256,768]{2,1,0:T(8,128)(2,1)}, bf16[2,256,768]{2,1,0:T(8,128)(2,1)}, u32[]{:S(2)}, u32[]{:S(2)}) collective-permute-start(bf16[2,256,768]{2,1,0:T(8,128)(2,1)} %copy.570), channel_id=1, source_target_pairs={{0,2},{1,3},{2,4},{3,5},{4,6},{5,7},{8,10},{9,11},{10,12},{11,13},... | collective-permute-start | bytes 2359304 | tf_op jit(solution)/shard_map/ppermute | solution.py:20
  1867.6 53.8 %collective-permute-start.52 = (bf16[2,256,768]{2,1,0:T(8,128)(2,1)}, bf16[2,256,768]{2,1,0:T(8,128)(2,1)S(1)}, u32[]{:S(2)}, u32[]{:S(2)}) collective-permute-start(bf16[2,256,768]{2,1,0:T(8,128)(2,1)} %copy.569), channel_id=1, source_target_pairs={{0,1},{1,2},{2,3},{3,4},{4,5},{5,6},{6,7},{8,9},{9,10},{10,11},{11... | collective-permute-start | bytes 2359304 | tf_op jit(solution)/shard_map/ppermute | solution.py:20
  1870.3 51.1 %collective-permute-start.51 = (bf16[2,256,768]{2,1,0:T(8,128)(2,1)}, bf16[2,256,768]{2,1,0:T(8,128)(2,1)S(1)}, u32[]{:S(2)}, u32[]{:S(2)}) collective-permute-start(bf16[2,256,768]{2,1,0:T(8,128)(2,1)} %copy.568), channel_id=1, source_target_pairs={{1,0},{2,1},{3,2},{4,3},{5,4},{6,5},{7,6},{9,8},{10,9},{11,10},{12... | collective-permute-start | bytes 2359304 | tf_op jit(solution)/shard_map/ppermute | solution.py:20
  1871.6 49.8 %collective-permute-start.50 = (bf16[2,256,768]{2,1,0:T(8,128)(2,1)}, bf16[2,256,768]{2,1,0:T(8,128)(2,1)S(1)}, u32[]{:S(2)}, u32[]{:S(2)}) collective-permute-start(bf16[2,256,768]{2,1,0:T(8,128)(2,1)} %copy.567), channel_id=1, source_target_pairs={{2,0},{3,1},{4,2},{5,3},{6,4},{7,5},{10,8},{11,9},{12,10},{13,11},... | collective-permute-start | bytes 2359304 | tf_op jit(solution)/shard_map/ppermute | solution.py:20
  1908.9 66.0 %collective-permute-start.48 = (bf16[2,256,768]{2,1,0:T(8,128)(2,1)}, bf16[2,256,768]{2,1,0:T(8,128)(2,1)S(1)}, u32[]{:S(2)}, u32[]{:S(2)}) collective-permute-start(bf16[2,256,768]{2,1,0:T(8,128)(2,1)} %copy.564), channel_id=1, source_target_pairs={{4,0},{5,1},{6,2},{7,3},{12,8},{13,9},{14,10},{15,11},{20,16},{21,... | collective-permute-start | bytes 2359304 | tf_op jit(solution)/shard_map/ppermute | solution.py:20
  1994.8 546.6 %reduce-scatter.39.cloned.1.call-start = ((), (), s32[]{:S(2)}) async-start(), calls=%async_computation.20 | async-start | bytes 21233664 | tf_op jit(solution)/shard_map/reduce_scatter | solution.py:450
  2011.6 842.4 %reduce-scatter.41.cloned.1.call-start = ((), (), s32[]{:S(2)}) async-start(), calls=%async_computation.21 | async-start | bytes 21233664 | tf_op jit(solution)/shard_map/reduce_scatter | solution.py:452
  2027.2 891.5 %reduce-scatter.45.cloned.1.call-start = ((), (), s32[]{:S(2)}) async-start(), calls=%async_computation.23 | async-start | bytes 442368
  2029.0 954.0 %reduce-scatter.49.cloned.1.call-start = ((), (), s32[]{:S(2)}) async-start(), calls=%async_computation.25 | async-start | bytes 442368
  2030.1 1017.4 %reduce-scatter.51.cloned.1.call-start = ((), (), s32[]{:S(2)}) async-start(), calls=%async_computation.26 | async-start | bytes 442368
  2031.1 1080.9 %reduce-scatter.53.cloned.1.call-start = ((), (), s32[]{:S(2)}) async-start(), calls=%async_computation.27 | async-start | bytes 442368
  2032.4 1144.1 %reduce-scatter.57.cloned.1.call-start = ((), (), s32[]{:S(2)}) async-start(), calls=%async_computation.29 | async-start | bytes 442368
  2033.4 1207.4 %reduce-scatter.59.cloned.1.call-start = ((), (), s32[]{:S(2)}) async-start(), calls=%async_computation.30 | async-start | bytes 442368
  2034.5 1270.7 %reduce-scatter.61.cloned.1.call-start = ((), (), s32[]{:S(2)}) async-start(), calls=%async_computation.31 | async-start | bytes 442368
  2035.5 1338.0 %reduce-scatter.55.cloned.1.call-start = ((), (), s32[]{:S(2)}) async-start(), calls=%async_computation.28 | async-start | bytes 1769472
  2037.3 1400.3 %reduce-scatter.47.cloned.1.call-start = ((), (), s32[]{:S(2)}) async-start(), calls=%async_computation.24 | async-start | bytes 442368
  2038.4 1464.1 %reduce-scatter.43.cloned.1.call-start = ((), (), s32[]{:S(2)}) async-start(), calls=%async_computation.22 | async-start | bytes 442368
  2046.8 1532.9 %all-reduce.4.cloned.1.call-start = ((), (), s32[]{:S(2)}) async-start(), calls=%async_computation.32 | async-start | bytes 7077888 | tf_op jit(solution)/shard_map/psum | solution.py:459
  (228 other events, 11730.6 us)
Sparse Core Ops, SparseCore 0:
  10.2 111.3 all-gather.13
  123.8 88.4 all-gather.15
  214.5 228.0 all-gather.17
  444.7 145.7 all-gather.19
  1595.4 139.6 reduce-scatter.36
  1994.8 233.7 reduce-scatter.34
  2232.5 308.8 reduce-scatter.38
  2545.2 308.7 reduce-scatter.40
  2857.3 61.3 reduce-scatter.44
  2921.8 61.1 reduce-scatter.48
  2986.3 61.1 reduce-scatter.50
  3050.6 61.3 reduce-scatter.52
  3115.2 61.1 reduce-scatter.56
  3179.6 61.2 reduce-scatter.58
  3243.9 61.1 reduce-scatter.60
  3309.0 64.4 reduce-scatter.54
  3376.6 60.9 reduce-scatter.46
  3441.3 61.1 reduce-scatter.42
  3505.7 73.9 all-reduce.3
where the time goes:
time: 3620 us; the launch traced here: 3600 us
  waiting for transfers between devices  1840 us (51%)
  blocking collectives  486 us (13%)
  starting transfers between devices  466 us (13%)
  matrix products  344 us (10%)
  local copies, waits for them, and re-layouts  257 us (7%)
  other arithmetic  158 us (4%)
    unnamed x29, waiting for transfers between devices  641 us
    ppermute x64, starting transfers between devices, passed_along(): return lax.ppermute(block, axis, route)  465 us
    reduce_scatter x1, waiting for transfers between devices, on_device(): lax.psum_scatter(stacked[7], 'shard', scatter_dimension=1, tiled=True)  310 us
    reduce_scatter x1, waiting for transfers between devices, on_device(): lax.psum_scatter(stacked[9], 'shard', scatter_dimension=1, tiled=True)  310 us
    ppermute x64, waiting for transfers between devices, passed_along(): return lax.ppermute(block, axis, route)  260 us
    reduce_scatter x1, waiting for transfers between devices, on_device(): lax.psum_scatter(stacked[0], 'shard', scatter_dimension=1, tiled=True)  180 us
    another operation x76, local copies, waits for them, and re-layouts  114 us
    all_gather x1, blocking collectives, on_device(): lax.all_gather(down_bias, 'shard', axis=1, tiled=True)  94 us
  transfers between devices with their start and end apart: 83, of which 33 were waited for; matrix products, arithmetic and copies ran while one was open for 14% of the time, Pallas kernels for 0%

commit v1 on v0

--- a/solution.py
+++ b/solution.py
@@ -1,6 +1,8 @@
 import jax
 import jax.numpy as jnp
 from jax import lax
+from jax.experimental import pallas as pl
+from jax.experimental.pallas import tpu as pltpu
 from jax.sharding import PartitionSpec as P
 
 HEADS = 12
@@ -491,9 +493,464 @@
     )
 
 
+BLOCK = 256
+GROUP = 4
+BF16 = jnp.bfloat16
+F32 = jnp.float32
+
+
+def mm(left, right, left_dim, right_dim):
+    return lax.dot_general(
+        left, right, (((left_dim,), (right_dim,)), ((), ())), preferred_element_type=F32
+    )
+
+
+def exchange(tensor, axis, mask):
+    count = lax.axis_size(axis)
+    return lax.ppermute(tensor, axis, [(i, i ^ mask) for i in range(count)])
+
+
+def ordered(first_is_mine, mine, other):
+    return jnp.stack(
+        [jnp.where(first_is_mine, mine, other), jnp.where(first_is_mine, other, mine)]
+    )
+
+
+def gather_small(tensor):
+    index = lax.axis_index("shard")
+    for bit in range(3):
+        other = exchange(tensor, "shard", 1 << bit)
+        tensor = ordered((index >> bit) & 1 == 0, tensor, other)
+    return tensor.reshape((8,) + tensor.shape[3:])
+
+
+def sum_small(tensor):
+    for axis, bits in (("rep", 2), ("shard", 3)):
+        for bit in range(bits):
+            tensor = tensor + exchange(tensor, axis, 1 << bit)
+    return tensor
+
+
+def to_groups(tensor, index):
+    low = index < GROUP
+    mine = jnp.where(low, tensor[0], tensor[1])
+    other = exchange(jnp.where(low, tensor[1], tensor[0]), "shard", GROUP)
+    both = ordered(low, mine, other)
+    return both.reshape((2 * tensor.shape[1],) + tensor.shape[2:])
+
+
+def from_groups(tensor, index):
+    low = index < GROUP
+    half = tensor.shape[0] // 2
+    mine = jnp.where(low, tensor[:half], tensor[half:])
+    other = exchange(
+        jnp.where(low, tensor[half:], tensor[:half]).astype(BF16), "shard", GROUP
+    ).astype(tensor.dtype)
+    return ordered(low, mine, other)
+
+
+def swap(tensor):
+    shape = tensor.shape
+    flat = tensor.reshape((shape[0] * shape[1],) + shape[2:])
+    moved = lax.all_to_all(
+        flat, "shard", 0, 0, axis_index_groups=[[0, 1, 2, 3], [4, 5, 6, 7]], tiled=True
+    )
+    return moved.reshape(shape)
+
+
+def block_cols(block):
+    half = block // GROUP
+    return pl.ds(pl.multiple_of(half * BLOCK, BLOCK), BLOCK)
+
+
+def flipped(tensor):
+    return jnp.transpose(tensor.astype(F32)).astype(BF16)
+
+
+def pair_mask(seg_col, seg_row, keys, queries):
+    col = seg_col[pl.ds(pl.multiple_of(keys * BLOCK, BLOCK), BLOCK), :]
+    col = jnp.concatenate([col] * (BLOCK // 128), axis=1)
+    return col == seg_row[queries]
+
+
+def attend_kernel(
+    lo_ref, hi_ref, x_ref, seg_col, seg_row, low_ref, out_ref, lse_ref, keys_nat, acc, top, total,
+):
+    heads = x_ref.shape[1] // (3 * HEAD_DIM)
+    width = heads * HEAD_DIM
+    blocks = seg_row.shape[0]
+
+    def flip(block, carry):
+        for h in range(heads):
+            keys_nat[h, block] = flipped(
+                x_ref[block % GROUP, width + h * HEAD_DIM : width + (h + 1) * HEAD_DIM, block_cols(block)]
+            )
+        return carry
+
+    lax.fori_loop(0, blocks, flip, 0)
+
+    def per_query(i, carry):
+        src, cols = (i % GROUP, block_cols(i))
+        for h in range(heads):
+            top[h] = jnp.full(top.shape[1:], masked_score, F32)
+            total[h] = jnp.zeros(total.shape[1:], F32)
+            acc[h] = jnp.zeros(acc.shape[1:], F32)
+
+        def per_key(j, inner):
+            allowed = pair_mask(seg_col, seg_row, j, i)
+            for h in range(heads):
+                query = x_ref[src, h * HEAD_DIM : (h + 1) * HEAD_DIM, cols]
+                value = x_ref[
+                    j % GROUP, 2 * width + h * HEAD_DIM : 2 * width + (h + 1) * HEAD_DIM, block_cols(j)
+                ]
+                scores = jnp.where(allowed, mm(keys_nat[h, j], query, 1, 0), masked_score)
+                old = top[h]
+                new = jnp.maximum(old, jnp.max(scores, axis=0, keepdims=True))
+                raised = jnp.exp(scores - new)
+                fade = jnp.exp(old - new)
+                top[h] = new
+                total[h] = total[h] * fade + jnp.sum(raised, axis=0, keepdims=True)
+                acc[h] = acc[h] * fade + mm(value, raised.astype(BF16), 1, 0)
+            return inner
+
+        lax.fori_loop(lo_ref[i], hi_ref[i], per_key, 0)
+        for h in range(heads):
+            out = acc[h] / total[h]
+            out_ref[src, h * HEAD_DIM : (h + 1) * HEAD_DIM, cols] = out
+            low_ref[src, h * HEAD_DIM : (h + 1) * HEAD_DIM, cols] = out.astype(BF16)
+            lse_ref[h, i] = top[h] + jnp.log(total[h])
+        return carry
+
+    lax.fori_loop(0, blocks, per_query, 0)
+
+
+def attend_back_kernel(
+    lo_ref, hi_ref, x_ref, go_ref, out_ref, lse_ref, seg_col, seg_row, dx_ref,
+    keys_nat, values_nat, delta, dq, dk, dv,
+):
+    heads = x_ref.shape[1] // (3 * HEAD_DIM)
+    width = heads * HEAD_DIM
+    blocks = seg_row.shape[0]
+
+    def prepare(block, carry):
+        src, cols = (block % GROUP, block_cols(block))
+        for h in range(heads):
+            low, high = (h * HEAD_DIM, (h + 1) * HEAD_DIM)
+            keys_nat[h, block] = flipped(x_ref[src, width + low : width + high, cols])
+            values_nat[h, block] = flipped(x_ref[src, 2 * width + low : 2 * width + high, cols])
+            delta[h, block] = jnp.sum(
+                go_ref[src, low:high, cols].astype(F32) * out_ref[src, low:high, cols],
+                axis=0,
+                keepdims=True,
+            )
+            dq[h, block] = jnp.zeros(dq.shape[2:], F32)
+        return carry
+
+    lax.fori_loop(0, blocks, prepare, 0)
+
+    def per_key(j, carry):
+        key_src, key_cols = (j % GROUP, block_cols(j))
+        for h in range(heads):
+            dk[h] = jnp.zeros(dk.shape[1:], F32)
+            dv[h] = jnp.zeros(dv.shape[1:], F32)
+
+        def per_query(i, inner):
+            src, cols = (i % GROUP, block_cols(i))
+            allowed = pair_mask(seg_col, seg_row, j, i)
+            for h in range(heads):
+                low, high = (h * HEAD_DIM, (h + 1) * HEAD_DIM)
+                query = x_ref[src, low:high, cols]
+                grad = go_ref[src, low:high, cols]
+                scores = jnp.where(allowed, mm(keys_nat[h, j], query, 1, 0), masked_score)
+                probs = jnp.exp(scores - lse_ref[h, i])
+                grad_probs = mm(values_nat[h, j], grad, 1, 0)
+                grad_scores = (probs * (grad_probs - delta[h, i])).astype(BF16)
+                dv[h] += mm(grad, probs.astype(BF16), 1, 1)
+                dk[h] += mm(query, grad_scores, 1, 1)
+                dq[h, i] += mm(x_ref[key_src, width + low : width + high, key_cols], grad_scores, 1, 0)
+            return inner
+
+        lax.fori_loop(lo_ref[j], hi_ref[j], per_query, 0)
+        for h in range(heads):
+            low, high = (h * HEAD_DIM, (h + 1) * HEAD_DIM)
+            dx_ref[key_src, width + low : width + high, key_cols] = dk[h].astype(BF16)
+            dx_ref[key_src, 2 * width + low : 2 * width + high, key_cols] = dv[h].astype(BF16)
+        return carry
+
+    lax.fori_loop(0, blocks, per_key, 0)
+
+    def finish(block, carry):
+        src, cols = (block % GROUP, block_cols(block))
+        for h in range(heads):
+            dx_ref[src, h * HEAD_DIM : (h + 1) * HEAD_DIM, cols] = (dq[h, block] * 0.125).astype(BF16)
+        return carry
+
+    lax.fori_loop(0, blocks, finish, 0)
+
+
+def in_vmem(count):
+    return [pl.BlockSpec(memory_space=pltpu.VMEM)] * count
+
+
+def attend(qkv, spans, seg_col, seg_row):
+    heads = qkv.shape[1] // (3 * HEAD_DIM)
+    blocks = seg_row.shape[0]
+    return pl.pallas_call(
+        attend_kernel,
+        name="attend",
+        out_shape=(
+            jax.ShapeDtypeStruct((GROUP, heads * HEAD_DIM, qkv.shape[2]), BF16),
+            jax.ShapeDtypeStruct((GROUP, heads * HEAD_DIM, qkv.shape[2]), F32),
+            jax.ShapeDtypeStruct((heads, blocks, 1, BLOCK), F32),
+        ),
+        in_specs=[pl.BlockSpec(memory_space=pltpu.SMEM)] * 2 + in_vmem(3),
+        out_specs=in_vmem(3),
+        scratch_shapes=[
+            pltpu.VMEM((heads, blocks, BLOCK, HEAD_DIM), BF16),
+            pltpu.VMEM((heads, HEAD_DIM, BLOCK), F32),
+            pltpu.VMEM((heads, 1, BLOCK), F32),
+            pltpu.VMEM((heads, 1, BLOCK), F32),
+        ],
+    )(*spans, qkv, seg_col, seg_row)
+
+
+def attend_back(qkv, grad_out, out, lse, spans, seg_col, seg_row):
+    heads = qkv.shape[1] // (3 * HEAD_DIM)
+    blocks = seg_row.shape[0]
+    return pl.pallas_call(
+        attend_back_kernel,
+        name="attend_back",
+        out_shape=jax.ShapeDtypeStruct(qkv.shape, BF16),
+        in_specs=[pl.BlockSpec(memory_space=pltpu.SMEM)] * 2 + in_vmem(6),
+        out_specs=in_vmem(1)[0],
+        scratch_shapes=[
+            pltpu.VMEM((heads, blocks, BLOCK, HEAD_DIM), BF16),
+            pltpu.VMEM((heads, blocks, BLOCK, HEAD_DIM), BF16),
+            pltpu.VMEM((heads, blocks, 1, BLOCK), F32),
+            pltpu.VMEM((heads, blocks, HEAD_DIM, BLOCK), F32),
+            pltpu.VMEM((heads, HEAD_DIM, BLOCK), F32),
+            pltpu.VMEM((heads, HEAD_DIM, BLOCK), F32),
+        ],
+    )(*spans, qkv, grad_out, out, lse, seg_col, seg_row)
+
+
+def norm_rows(tensor, gain, shift):
+    center = tensor - jnp.mean(tensor, axis=-1, keepdims=True)
+    inverse = lax.rsqrt(jnp.mean(center * center, axis=-1, keepdims=True) + norm_eps)
+    normed = center * inverse
+    return (normed * gain + shift, normed, inverse)
+
+
+def norm_rows_back(grad, normed, inverse, gain):
+    scaled = grad * gain
+    inner = (
+        scaled
+        - jnp.mean(scaled, axis=-1, keepdims=True)
+        - normed * jnp.mean(scaled * normed, axis=-1, keepdims=True)
+    )
+    return (inner * inverse, jnp.sum(grad * normed, axis=0), jnp.sum(grad, axis=0))
+
+
+def fast_forward(hidden, mats, downs, vecs, spans, seg_col, seg_row):
+    query_b, value_b, proj_b, attn_g, attn_s, down_b, ffn_g, ffn_s, up_b = vecs
+    width = hidden.shape[1]
+    hidden_low = hidden.astype(BF16)
+    query = (mm(mats[0], hidden_low, 0, 1) + query_b[:, None]).astype(BF16) * BF16(0.125)
+    keys = mm(mats[1], hidden_low, 0, 1).astype(BF16)
+    values = (mm(mats[2], hidden_low, 0, 1) + value_b[:, None]).astype(BF16)
+    share = width // GROUP
+    packed = jnp.concatenate(
+        [part.reshape(GROUP, share, part.shape[1]) for part in (query, keys, values)], axis=1
+    )
+    qkv = swap(packed)
+    low, out, lse = attend(qkv, spans, seg_col, seg_row)
+    context = swap(low).reshape(width, low.shape[2])
+    attn_out = mm(context, mats[3], 0, 0) + proj_b
+    settled, normed_one, inverse_one = norm_rows(hidden + attn_out, attn_g, attn_s)
+    settled_low = settled.astype(BF16)
+    ffn_out = down_b
+    actives, slopes = ([], [])
+    for part in range(len(mats) - 4):
+        before = mm(settled_low, mats[4 + part], 1, 0) + up_b[part * width : (part + 1) * width]
+        below = 0.5 * (1.0 + lax.erf(before * 0.7071067811865476))
+        active = (before * below).astype(BF16)
+        slopes.append((below + before * jnp.exp(-0.5 * before * before) * 0.3989422804014327).astype(BF16))
+        actives.append(active)
+        ffn_out = ffn_out + mm(active, downs[part * width : (part + 1) * width], 1, 0)
+    result, normed_two, inverse_two = norm_rows(settled + ffn_out, ffn_g, ffn_s)
+    return result, (
+        hidden_low, qkv, out, lse, context, normed_one, inverse_one, settled_low,
+        actives, slopes, normed_two, inverse_two,
+    )
+
+
+def fast_backward(grad, mats, downs, vecs, saved, spans, seg_col, seg_row):
+    query_b, value_b, proj_b, attn_g, attn_s, down_b, ffn_g, ffn_s, up_b = vecs
+    (
+        hidden_low, qkv, out, lse, context, normed_one, inverse_one, settled_low,
+        actives, slopes, normed_two, inverse_two,
+    ) = saved
+    width = grad.shape[1]
+    grad_two, ffn_g_sum, ffn_s_sum = norm_rows_back(grad, normed_two, inverse_two, ffn_g)
+    grad_ffn = grad_two.astype(BF16)
+    down_b_sum = jnp.sum(grad_ffn.astype(F32), axis=0)
+    grad_settled = grad_two
+    mat_grads = [None] * len(mats)
+    down_grads, up_b_sums = ([], [])
+    for part in range(len(actives)):
+        rows = slice(part * width, (part + 1) * width)
+        grad_before = (mm(grad_ffn, downs[rows], 1, 1) * slopes[part].astype(F32)).astype(BF16)
+        down_grads.append(mm(actives[part], grad_ffn, 0, 0).astype(BF16))
+        mat_grads[4 + part] = mm(settled_low, grad_before, 0, 0).astype(BF16)
+        up_b_sums.append(jnp.sum(grad_before.astype(F32), axis=0))
+        grad_settled = grad_settled + mm(grad_before, mats[4 + part], 1, 1)
+    grad_one, attn_g_sum, attn_s_sum = norm_rows_back(grad_settled, normed_one, inverse_one, attn_g)
+    grad_attn = grad_one.astype(BF16)
+    proj_b_sum = jnp.sum(grad_attn.astype(F32), axis=0)
+    grad_context = mm(mats[3], grad_attn, 1, 1).astype(BF16)
+    mat_grads[3] = mm(context, grad_attn, 1, 0).astype(BF16)
+    grad_out = swap(grad_context.reshape(GROUP, width // GROUP, grad_context.shape[1]))
+    moved = swap(attend_back(qkv, grad_out, out, lse, spans, seg_col, seg_row))
+    share = width // GROUP
+    pieces = [
+        moved[:, part * share : (part + 1) * share].reshape(width, moved.shape[2]) for part in range(3)
+    ]
+    grad_hidden = grad_one
+    for part in range(3):
+        mat_grads[part] = mm(hidden_low, pieces[part], 0, 1).astype(BF16)
+        grad_hidden = grad_hidden + mm(pieces[part], mats[part], 0, 1)
+    query_b_sum = jnp.sum(pieces[0].astype(F32), axis=1)
+    value_b_sum = jnp.sum(pieces[2].astype(F32), axis=1)
+    sums = [
+        query_b_sum, value_b_sum, proj_b_sum, attn_g_sum, attn_s_sum, down_b_sum, ffn_g_sum, ffn_s_sum,
+    ] + up_b_sums
+    return grad_hidden, mat_grads, down_grads, sums
+
+
+def gather_weights(mats, downs):
+    return (
+        lax.all_gather(mats, "shard", axis=1, tiled=True),
+        lax.all_gather(downs, "shard", axis=0, tiled=True),
+    )
+
+
+def scatter_grads(mat_grads, down_grads):
+    mats = lax.psum_scatter(jnp.stack(mat_grads), "shard", scatter_dimension=1, tiled=True)
+    downs = lax.psum_scatter(
+        jnp.concatenate(down_grads, axis=0), "shard", scatter_dimension=0, tiled=True
+    )
+    return (lax.psum(mats, "rep").astype(F32), lax.psum(downs, "rep").astype(F32))
+
+
+def on_device_fast(
+    inputs, cotangent, segment_ids, memory_slot, memory_table,
+    qkv_weight, query_bias, value_bias, proj_weight, proj_bias, attn_gain, attn_shift,
+    up_weight, up_bias, down_weight, down_bias, ffn_gain, ffn_shift,
+):
+    index = lax.axis_index("shard")
+    width = inputs.shape[2]
+    share = memory_table.shape[1]
+    ups = up_weight.shape[2] // width
+
+    weights = []
+    for layer in range(LAYERS):
+        own = jnp.concatenate([qkv_weight[layer], proj_weight[layer], up_weight[layer]], axis=1)
+        own = jnp.stack([own[:, part * width : (part + 1) * width] for part in range(4 + ups)])
+        weights.append(gather_weights(own, down_weight[layer]))
+
+    vec_args = (
+        query_bias, value_bias, proj_bias, attn_gain, attn_shift, down_bias, ffn_gain, ffn_shift,
+    )
+    plain = len(vec_args)
+    rows = [item[layer][None] for layer in range(LAYERS) for item in vec_args]
+    rows += [up_bias[layer].reshape(ups, share) for layer in range(LAYERS)]
+    rows.append(memory_table)
+    small = gather_small(jnp.concatenate(rows, axis=0)).astype(F32)
+    wide = jnp.transpose(small, (1, 0, 2)).reshape(small.shape[1], width)
+    vecs = []
+    for layer in range(LAYERS):
+        start = LAYERS * plain + layer * ups
+        vecs.append(
+            [wide[layer * plain + item] for item in range(plain)]
+            + [small[:, start : start + ups].reshape(ups * width)]
+        )
+    table = wide[LAYERS * (plain + ups) :].astype(BF16)
+
+    segs = jnp.where(index < GROUP, segment_ids[0], segment_ids[1])
+    tiles = segs.reshape(-1, BLOCK)
+    first, last = (tiles[:, 0], tiles[:, -1])
+    spans = (
+        jnp.sum((last[None, :] < first[:, None]).astype(jnp.int32), axis=1),
+        jnp.sum((first[None, :] <= last[:, None]).astype(jnp.int32), axis=1),
+    )
+    seg_row = tiles[:, None, :]
+    seg_col = jnp.broadcast_to(segs[:, None], (segs.shape[0], 128))
+
+    slots = to_groups(memory_slot[..., None], index)[:, 0]
+    slot_hot = slots[:, None] == jnp.arange(MEMS, dtype=jnp.int32)
+    hidden = to_groups(inputs, index).astype(F32) + mm(slot_hot.astype(BF16), table, 1, 0)
+    saved = []
+    for layer in range(LAYERS):
+        mats, downs = weights[layer]
+        hidden, state = fast_forward(hidden, mats, downs, vecs[layer], spans, seg_col, seg_row)
+        saved.append(state)
+    layer_output = from_groups(hidden, index)
+
+    grad = to_groups(cotangent, index).astype(F32)
+    sums, shares = ([None] * LAYERS, [None] * LAYERS)
+    for layer in range(LAYERS - 1, -1, -1):
+        mats, downs = weights[layer]
+        grad, mat_grads, down_grads, sums[layer] = fast_backward(
+            grad, mats, downs, vecs[layer], saved[layer], spans, seg_col, seg_row
+        )
+        shares[layer] = scatter_grads(mat_grads, down_grads)
+    input_grad = from_groups(grad, index)
+    memory_sum = lax.dot_general(
+        slot_hot.astype(F32), grad, (((0,), (0,)), ((), ())), precision=lax.Precision.HIGHEST
+    )
+    flat = jnp.concatenate([jnp.stack(sums[layer]) for layer in range(LAYERS)] + [memory_sum], axis=0)
+    flat = sum_small(flat)
+    per = plain + ups
+    own = lax.dynamic_slice_in_dim(flat, index * share, share, 1)
+    vec_grads = [
+        jnp.stack([own[layer * per + item] for layer in range(LAYERS)]) for item in range(plain)
+    ]
+    up_sums = jnp.stack([flat[layer * per + plain : (layer + 1) * per].reshape(-1) for layer in range(LAYERS)])
+    upbias_grad = lax.dynamic_slice_in_dim(up_sums, index * share * ups, share * ups, 1)
+    memory_grad = own[LAYERS * per :]
+
+    def wide_grad(low, high):
+        return jnp.stack(
+            [jnp.concatenate(list(shares[layer][0][low:high]), axis=1) for layer in range(LAYERS)]
+        )
+
+    return (
+        layer_output,
+        input_grad,
+        memory_grad,
+        wide_grad(0, 3),
+        vec_grads[0],
+        vec_grads[1],
+        wide_grad(3, 4),
+        vec_grads[2],
+        vec_grads[3],
+        vec_grads[4],
+        wide_grad(4, 4 + ups),
+        upbias_grad,
+        jnp.stack([shares[layer][1] for layer in range(LAYERS)]),
+        vec_grads[5],
+        vec_grads[6],
+        vec_grads[7],
+    )
+
+
+def fast_fits(mesh):
+    return mesh.shape["shard"] == 2 * GROUP and mesh.shape["rep"] == 4
+
+
 def solution(mesh):
     return jax.shard_map(
-        on_device,
+        on_device_fast if fast_fits(mesh) else on_device,
         mesh=mesh,
         in_specs=(
             P(None, ("rep", "shard"), None),

time: 3620 us -> 1290 us (0.36)
  waiting for transfers between devices: 1840 us -> 638 us
  starting transfers between devices: 466 us -> 44 us
  blocking collectives: 486 us -> 203 us
  local copies, waits for them, and re-layouts: 257 us -> 43.5 us
  matrix products: 344 us -> 153 us
  Pallas kernels: 0 us -> 142 us
  other arithmetic: 158 us -> 44.5 us
    unnamed x29 -> x9, waiting for transfers between devices: 641 us -> 0.48 us
    reduce_scatter x4, waiting for transfers between devices: 800 us -> 242 us  [the longest x2 242 us: scatter_grads(): lax.psum_scatter(jnp.stack(mat_grads), 'shard', scatter_dimension=1, tile...]
    all_gather x10 -> x0, blocking collectives: 475 us -> none  [the longest x1 94 us: on_device(): lax.all_gather(down_bias, 'shard', axis=1, tiled=True)]
    ppermute x64 -> x13, starting transfers between devices: 465 us -> 31.2 us  [exchange(): return lax.ppermute(tensor, axis, [(i, i ^ mask) for i in range(count)])]
    all_to_all x0 -> x5, blocking collectives: none -> 203 us  [swap(): lax.all_to_all(flat, 'shard', 0, 0, axis_index_groups=[[0, 1, 2, 3], [4,...]
    dot_general x96 -> x74, matrix products: 344 us -> 153 us  [the longest x73 152 us: mm(): lax.dot_general(left, right, (((left_dim,), (right_dim,)), ((), ())), pre...]
    ppermute x64 -> x13, waiting for transfers between devices: 260 us -> 88.2 us  [exchange(): return lax.ppermute(tensor, axis, [(i, i ^ mask) for i in range(count)])]
    pallas_call x0 -> x4, Pallas kernels: none -> 142 us  [the longest x2 72.6 us: attend_back(): pl.pallas_call(attend_back_kernel, name='attend_back', out_shape=jax.Shap...]
  transfers between devices with their start and end apart: 83 -> 25, of which waited for: 33 -> 14; matrix products, arithmetic and copies ran while one was open for 14% -> 15% of each run, Pallas kernels for 0% -> 11%
where the time goes in v1:
time: 1290 us; the launch traced here: 1280 us
  waiting for transfers between devices  638 us (49%)
  blocking collectives  203 us (16%)
  matrix products  153 us (12%)
  Pallas kernels  142 us (11%)
  other arithmetic  44.5 us (3%)
  starting transfers between devices  44 us (3%)
  local copies, waits for them, and re-layouts  43.5 us (3%)
  between operations  16.4 us (1%)
    reduce_scatter x2, waiting for transfers between devices, scatter_grads(): lax.psum_scatter(jnp.stack(mat_grads), 'shard', scatter_dimension=1, tile...  242 us
    all_to_all x5, blocking collectives, swap(): lax.all_to_all(flat, 'shard', 0, 0, axis_index_groups=[[0, 1, 2, 3], [4,...  203 us
    all_gather x2, waiting for transfers between devices, gather_weights(): lax.all_gather(mats, 'shard', axis=1, tiled=True)  196 us
    dot_general x73, matrix products, mm(): lax.dot_general(left, right, (((left_dim,), (right_dim,)), ((), ())), pre...  152 us
    ppermute x13, waiting for transfers between devices, exchange(): return lax.ppermute(tensor, axis, [(i, i ^ mask) for i in range(count)])  88.2 us
    pallas_call x2, Pallas kernels, attend_back(): pl.pallas_call(attend_back_kernel, name='attend_back', out_shape=jax.Shap...  72.6 us
    pallas_call x2, Pallas kernels, attend(): pl.pallas_call(attend_kernel, name='attend', out_shape=(jax.ShapeDtypeStr...  69.3 us
    psum x1, waiting for transfers between devices, scatter_grads(): lax.psum(mats, 'rep').astype(F32)  60.2 us
  transfers between devices with their start and end apart: 25, of which 14 were waited for; matrix products, arithmetic and copies ran while one was open for 15% of the time, Pallas kernels for 11%

profile of v1, /device:TPU:0, one launch (start us, length us, event | category | flops | bytes accessed | tf_op | source)
XLA Modules:
  0.0 1284.5 jit_solution(15284285477271532929)
XLA Ops:
  14.1 2.4 fusion.140
  17.8 4.1 collective-permute-start.1
  27.8 12.9 %collective-permute-done.3 = bf16[2,44,96]{2,1,0:T(8,128)(2,1)S(1)} collective-permute-done((bf16[2,44,96]{2,1,0:T(8,128)(2,1)S(1)}, bf16[2,44,96]{2,1,0:T(8,128)(2,1)S(1)}, u32[]{:S(2)}, u32[]{:S(2)}) %collective-permute-start.3) | collective-permute-done | bytes 16928 | tf_op jit(solution)/shard_map/ppermute | solution.py:510
  40.8 5.2 collective-permute-start.4
  46.0 25.1 %collective-permute-done.4 = bf16[2,2,44,96]{3,2,1,0:T(8,128)(2,1)S(1)} collective-permute-done((bf16[2,2,44,96]{3,2,1,0:T(8,128)(2,1)S(1)}, bf16[2,2,44,96]{3,2,1,0:T(8,128)(2,1)S(1)}, u32[]{:S(2)}, u32[]{:S(2)}) %collective-permute-start.4) | collective-permute-done | bytes 33824 | tf_op jit(solution)/shard_map/ppermute | solution.py:510
  73.9 95.4 %all-gather.7.cloned.1.call-done = bf16[8,768,768]{2,1,0:T(8,128)(2,1)} async-done(((bf16[8,96,768]{2,1,0:T(8,128)(2,1)}), bf16[8,768,768]{2,1,0:T(8,128)(2,1)}) %all-gather.7.cloned.1.call-update) | async-done | bytes 9437200 | tf_op jit(solution)/shard_map/all_gather | solution.py:832
  177.2 3.8 all-to-all-start
  183.2 41.9 %all-to-all-done.x_ref = bf16[4,576,512]{2,1,0:T(8,128)(2,1)S(1)} async-done(((bf16[4,576,512]{2,1,0:T(8,128)(2,1)}), bf16[4,576,512]{2,1,0:T(8,128)(2,1)S(1)}, u32[]{:S(2)}, u32[]{:S(2)}) %all-to-all-start) | async-done | bytes 2359328 | tf_op jit(solution)/shard_map/all_to_all | solution.py:555
  226.8 34.7 %attend.2 = (bf16[4,192,512]{2,1,0:T(8,128)(2,1)}, f32[4,192,512]{2,1,0:T(8,128)}, f32[3,8,1,256]{3,2,1,0:T(1,128)}) custom-call(s32[8]{0:T(128)} %get-tuple-element.51.lo_ref, s32[8]{0:T(128)} %get-tuple-element.50.hi_ref, bf16[4,576,512]{2,1,0:T(8,128)(2,1)} %copy-done.3, s32[2048,128]{1,0:T(8,128)} %broadcast_in_dim.2.seg_col, s32[8,1,256]{2,1,0:T(1,128)} %bitcast.546), custom_call_target="tpu_custom_call" | custom-call | tf_op jit(solution)/shard_map/attend/pallas_call | solution.py:698
  261.5 3.5 all-to-all-start.1
  267.1 9.5 all-to-all-done.1
  276.6 3.3 fusion.153
  280.6 3.5 convolution_add_fusion.4
  284.0 3.3 multiply_convert_fusion.13
  287.3 3.8 multiply_convert_fusion.14
  291.1 2.2 fusion.92
  293.4 2.3 fusion.90
  295.7 3.3 multiply_convert_fusion.15
  304.3 100.8 %all-gather.9.cloned.1.call-done = bf16[8,768,768]{2,1,0:T(8,128)(2,1)} async-done(((bf16[8,96,768]{2,1,0:T(8,128)(2,1)}), bf16[8,768,768]{2,1,0:T(8,128)(2,1)}) %all-gather.9.cloned.1.call-update) | async-done | bytes 9437200 | tf_op jit(solution)/shard_map/all_gather | solution.py:832
  405.1 2.4 convolution_convert_fusion.26
  411.9 50.0 %all_to_all.60.x_ref = bf16[4,576,512]{2,1,0:T(8,128)(2,1)} all-to-all(bf16[4,576,512]{2,1,0:T(8,128)(2,1)S(1)} %pad_maximum_fusion.3), channel_id=1, replica_groups={{0,1,2,3},{4,5,6,7},{8,9,10,11},{12,13,14,15},{16,17,18,19},{20,21,22,2..., dimensions={0} | all-to-all | bytes 4718592 | tf_op jit(solution)/shard_map/all_to_all | solution.py:555
  461.9 34.6 %attend.3 = (bf16[4,192,512]{2,1,0:T(8,128)(2,1)}, f32[4,192,512]{2,1,0:T(8,128)}, f32[3,8,1,256]{3,2,1,0:T(1,128)}) custom-call(s32[8]{0:T(128)} %get-tuple-element.51.lo_ref, s32[8]{0:T(128)} %get-tuple-element.50.hi_ref, bf16[4,576,512]{2,1,0:T(8,128)(2,1)} %all_to_all.60.x_ref, s32[2048,128]{1,0:T(8,128)} %broadcast_in_dim.2.seg_col, s32[8,1,256]{2,1,0:T(1,128)} %bitcast.547), custom_call_target="tpu_custom_call" | custom-call | tf_op jit(solution)/shard_map/attend/pallas_call | solution.py:698
  496.5 4.3 all-to-all-start.3
  502.3 3.5 collective-permute-start.6
  517.9 5.9 collective-permute-done.6
  527.4 2.6 fusion.155
  531.1 3.5 convolution_add_fusion
  534.6 3.6 multiply_convert_fusion.9
  538.2 3.6 multiply_convert_fusion.10
  541.9 2.4 fusion.100
  546.4 3.4 multiply_convert_fusion.11
  555.3 3.0 convert_reduce_fusion.5
  562.5 2.4 pad_maximum_fusion.1
  565.0 3.2 convert_reduce_fusion.1
  568.3 2.7 convert_reduce_fusion.2
  571.1 2.7 convert_reduce_fusion.3
  573.8 2.8 convert_reduce_fusion.4
  583.4 30.2 %all_to_all.61.go_ref = bf16[4,192,512]{2,1,0:T(8,128)(2,1)} all-to-all(bf16[4,192,512]{2,1,0:T(8,128)(2,1)S(1)} %bitcast.533), channel_id=1, replica_groups={{0,1,2,3},{4,5,6,7},{8,9,10,11},{12,13,14,15},{16,17,18,19},{20,21,22,2..., dimensions={0} | all-to-all | bytes 1572864 | tf_op jit(solution)/shard_map/all_to_all | solution.py:555
  613.6 36.3 %attend_back.2 = bf16[4,576,512]{2,1,0:T(8,128)(2,1)} custom-call(s32[8]{0:T(128)} %get-tuple-element.51.lo_ref, s32[8]{0:T(128)} %get-tuple-element.50.hi_ref, bf16[4,576,512]{2,1,0:T(8,128)(2,1)} %all_to_all.60.x_ref, bf16[4,192,512]{2,1,0:T(8,128)(2,1)} %all_to_all.61.go_ref, f32[4,192,512]{2,1,0:T(8,128)} %get-tuple-element.24.out_ref, ...), custom_call_target="tpu_custom_call" | custom-call | tf_op jit(solution)/shard_map/attend_back/pallas_call | solution.py:720
  650.0 46.4 %all_to_all.62 = bf16[4,576,512]{2,1,0:T(8,128)(2,1)S(1)} all-to-all(bf16[4,576,512]{2,1,0:T(8,128)(2,1)} %attend_back.2), channel_id=1, replica_groups={{0,1,2,3},{4,5,6,7},{8,9,10,11},{12,13,14,15},{16,17,18,19},{20,21,22,2..., dimensions={0} | all-to-all | bytes 4718592 | tf_op jit(solution)/shard_map/all_to_all | solution.py:555
  697.8 2.9 fusion.94
  703.1 2.9 multiply_reduce_fusion.1
  712.4 2.5 pad_maximum_fusion
  715.0 3.3 fusion.64
  722.1 3.1 fusion.70
  732.9 3.3 convert_reduce_fusion.10
  736.2 2.4 fusion.91
  738.7 2.4 convert_reduce_fusion.11
  741.1 2.5 fusion.89
  744.8 2.4 fusion.87
  748.6 2.8 multiply_reduce_fusion.2
  752.0 2.7 convolution_convert_fusion.24
  754.7 18.7 %all_to_all.63.go_ref = bf16[4,192,512]{2,1,0:T(8,128)(2,1)} all-to-all(bf16[4,192,512]{2,1,0:T(8,128)(2,1)S(1)} %bitcast.534), channel_id=1, replica_groups={{0,1,2,3},{4,5,6,7},{8,9,10,11},{12,13,14,15},{16,17,18,19},{20,21,22,2..., dimensions={0} | all-to-all | bytes 1572864 | tf_op jit(solution)/shard_map/all_to_all | solution.py:555
  773.4 36.3 %attend_back.3 = bf16[4,576,512]{2,1,0:T(8,128)(2,1)} custom-call(s32[8]{0:T(128)} %get-tuple-element.51.lo_ref, s32[8]{0:T(128)} %get-tuple-element.50.hi_ref, bf16[4,576,512]{2,1,0:T(8,128)(2,1)} %copy-done.3, bf16[4,192,512]{2,1,0:T(8,128)(2,1)} %all_to_all.63.go_ref, f32[4,192,512]{2,1,0:T(8,128)} %get-tuple-element.26.out_ref, ...), custom_call_target="tpu_custom_call" | custom-call | tf_op jit(solution)/shard_map/attend_back/pallas_call | solution.py:720
  809.7 57.4 %all_to_all.64 = bf16[4,576,512]{2,1,0:T(8,128)(2,1)S(1)} all-to-all(bf16[4,576,512]{2,1,0:T(8,128)(2,1)} %attend_back.3), channel_id=1, replica_groups={{0,1,2,3},{4,5,6,7},{8,9,10,11},{12,13,14,15},{16,17,18,19},{20,21,22,2..., dimensions={0} | all-to-all | bytes 4718592 | tf_op jit(solution)/shard_map/all_to_all | solution.py:555
  884.6 2.4 select_convert_fusion.1
  894.0 2.2 fusion.85
  901.0 8.6 collective-permute-start.9
  909.6 29.6 %collective-permute-done.5 = bf16[256,768]{1,0:T(8,128)(2,1)} collective-permute-done((bf16[256,768]{1,0:T(8,128)(2,1)}, bf16[256,768]{1,0:T(8,128)(2,1)}, u32[]{:S(2)}, u32[]{:S(2)}) %collective-permute-start.5) | collective-permute-done | bytes 393248 | tf_op jit(solution)/shard_map/ppermute | solution.py:510
  943.1 6.5 collective-permute-done.10
  949.8 77.0 %reduce-scatter.7.cloned.1.call-done = bf16[8,96,768]{2,1,0:T(8,128)(2,1)} async-done(((bf16[8,768,768]{2,1,0:T(8,128)(2,1)}), bf16[8,96,768]{2,1,0:T(8,128)(2,1)}) %reduce-scatter.7.cloned.1.call-update) | async-done | bytes 1179664 | tf_op jit(solution)/shard_map/reduce_scatter | solution.py:838
  1026.8 164.8 %reduce-scatter.5.cloned.1.call-done = bf16[8,96,768]{2,1,0:T(8,128)(2,1)} async-done(((bf16[8,768,768]{2,1,0:T(8,128)(2,1)}), bf16[8,96,768]{2,1,0:T(8,128)(2,1)}) %reduce-scatter.5.cloned.1.call-update) | async-done | bytes 1179664 | tf_op jit(solution)/shard_map/reduce_scatter | solution.py:838
  1195.6 6.3 collective-permute-done.12
  1208.1 60.2 %all-reduce.3.cloned.1.call-done = (bf16[8,96,768]{2,1,0:T(8,128)(2,1)}, bf16[8,96,768]{2,1,0:T(8,128)(2,1)}, bf16[1,384,768]{2,1,0:T(8,128)(2,1)}, bf16[1,384,768]{2,1,0:T(8,128)(2,1)}) async-done(((bf16[8,96,768]{2,1,0:T(8,128)(2,1)}, bf16[8,96,768]{2,1,0:T(8,128)(2,1)}, bf16[1,384,768]{2,1,0:T(8,128)(2,1)}, bf16[1,384,768]{2,1,0:T(8,128)(2,1)}), (bf16[8,96,768]{2,1,0:T(8,128)(2,1)}, ...) | async-done | bytes 3538960 | tf_op jit(solution)/shard_map/psum | solution.py:842
  (523 shorter events, 154.2 us)
Async XLA Ops:
  7.2 162.2 %all-gather.7.cloned.1.call-start = ((), (), s32[]{:S(2)}) async-start(), calls=%async_computation.12 | async-start | bytes 10616832 | tf_op jit(solution)/shard_map/all_gather | solution.py:832
  14.1 277.0 %all-gather.11.cloned.1.call-start = ((), (), s32[]{:S(2)}) async-start(), calls=%async_computation.18 | async-start | bytes 5308416 | tf_op jit(solution)/shard_map/all_gather | solution.py:833
  16.5 5.5 copy-start.87
  16.5 5.7 copy-start.92
  16.5 5.7 copy-start.93
  16.5 5.7 copy-start.94
  16.5 5.7 copy-start.95
  16.5 5.7 copy-start.96
  16.5 5.7 copy-start.97
  16.6 5.7 copy-start.98
  16.6 5.7 copy-start.99
  16.6 5.7 copy-start.86
  16.6 7.4 copy-start.21
  16.6 388.4 %all-gather.9.cloned.1.call-start = ((), (), s32[]{:S(2)}) async-start(), calls=%async_computation.13 | async-start | bytes 10616832 | tf_op jit(solution)/shard_map/all_gather | solution.py:832
  17.8 10.0 collective-permute-start.1
  22.4 3.7 collective-permute-start.2
  24.0 48.2 %collective-permute-start = (bf16[256,768]{1,0:T(8,128)(2,1)S(1)}, bf16[256,768]{1,0:T(8,128)(2,1)S(1)}, u32[]{:S(2)}, u32[]{:S(2)}) collective-permute-start(bf16[256,768]{1,0:T(8,128)(2,1)S(1)} %select_bitcast_fusion.1), channel_id=1, source_target_pairs={{0,4},{1,5},{2,6},{3,7},{4,0},{5,1},{6,2},{7,3},{8,12},{9,13},{10,... | collective-permute-start | bytes 1179656 | tf_op jit(solution)/shard_map/ppermute | solution.py:510
  26.2 14.6 %collective-permute-start.3 = (bf16[2,44,96]{2,1,0:T(8,128)(2,1)S(1)}, bf16[2,44,96]{2,1,0:T(8,128)(2,1)S(1)}, u32[]{:S(2)}, u32[]{:S(2)}) collective-permute-start(bf16[2,44,96]{2,1,0:T(8,128)(2,1)S(1)} %pad_maximum_fusion.13), channel_id=1, source_target_pairs={{0,2},{1,3},{2,0},{3,1},{4,6},{5,7},{6,4},{7,5},{8,10},{9,11},{10,... | collective-permute-start | bytes 50696 | tf_op jit(solution)/shard_map/ppermute | solution.py:510
  40.8 30.4 %collective-permute-start.4 = (bf16[2,2,44,96]{3,2,1,0:T(8,128)(2,1)S(1)}, bf16[2,2,44,96]{3,2,1,0:T(8,128)(2,1)S(1)}, u32[]{:S(2)}, u32[]{:S(2)}) collective-permute-start(bf16[2,2,44,96]{3,2,1,0:T(8,128)(2,1)S(1)} %pad_maximum_fusion.12), channel_id=1, source_target_pairs={{0,4},{1,5},{2,6},{3,7},{4,0},{5,1},{6,2},{7,3},{8,12},{9,13},{10,... | collective-permute-start | bytes 101384 | tf_op jit(solution)/shard_map/ppermute | solution.py:510
  46.0 26.4 %copy-start.74 = (s32[1,2,2,128]{3,1,2,0:T(2,128)}, s32[1,2,2,128]{3,1,2,0:T(2,128)S(1)}, u32[]{:S(2)}) copy-start(s32[1,2,2,128]{3,1,2,0:T(2,128)S(1)} %copy.44) | copy-start | bytes 6148
  73.9 99.6 %copy-start.37 = (bf16[512,768]{1,0:T(8,128)(2,1)}, bf16[512,768]{1,0:T(8,128)(2,1)S(1)}, u32[]{:S(2)}) copy-start(bf16[512,768]{1,0:T(8,128)(2,1)S(1)} %get-tuple-element.173) | copy-start | bytes 2359300
  177.2 4.3 copy-start.81
  177.2 47.8 %all-to-all-start = ((bf16[4,576,512]{2,1,0:T(8,128)(2,1)}), bf16[4,576,512]{2,1,0:T(8,128)(2,1)S(1)}, u32[]{:S(2)}, u32[]{:S(2)}) async-start(bf16[4,576,512]{2,1,0:T(8,128)(2,1)} %pad_maximum_fusion.2), calls=%async_computation | async-start | bytes 4718592 | tf_op jit(solution)/shard_map/all_to_all | solution.py:555
  182.2 44.5 %copy-start.58 = (s32[1,2048]{1,0:T(1,128)}, s32[1,2048]{1,0:T(1,128)S(1)}, u32[]{:S(2)}) copy-start(s32[1,2048]{1,0:T(1,128)S(1)} %get-tuple-element.67) | copy-start | bytes 24580
  261.5 15.1 %all-to-all-start.1 = ((bf16[4,192,512]{2,1,0:T(8,128)(2,1)}), bf16[4,192,512]{2,1,0:T(8,128)(2,1)S(1)}, u32[]{:S(2)}, u32[]{:S(2)}) async-start(bf16[4,192,512]{2,1,0:T(8,128)(2,1)} %get-tuple-element.22), calls=%async_computation.1 | async-start | bytes 1572864 | tf_op jit(solution)/shard_map/all_to_all | solution.py:555
  265.0 276.9 %all-gather.13.cloned.1.call-start = ((), (), s32[]{:S(2)}) async-start(), calls=%async_computation.19 | async-start | bytes 5308416 | tf_op jit(solution)/shard_map/all_gather | solution.py:833
  266.6 260.8 %copy-start.59 = (f32[768]{0:T(1024)}, f32[768]{0:T(1024)S(1)}, u32[]{:S(2)}) copy-start(f32[768]{0:T(1024)S(1)} %mul.420) | copy-start | bytes 9220
  266.7 36.3 %copy-start.78 = (f32[768]{0:T(1024)}, f32[768]{0:T(1024)S(1)}, u32[]{:S(2)}) copy-start(f32[768]{0:T(1024)S(1)} %add.431) | copy-start | bytes 9220
  280.2 20.5 %copy-start.65 = (f32[512]{0:T(512)}, f32[512]{0:T(512)S(1)}, u32[]{:S(2)}) copy-start(f32[512]{0:T(512)S(1)} %add_rsqrt_fusion.3) | copy-start | bytes 6148
  280.5 15.2 %copy-start.39 = (bf16[512,768]{1,0:T(8,128)(2,1)}, bf16[512,768]{1,0:T(8,128)(2,1)S(1)}, u32[]{:S(2)}) copy-start(bf16[512,768]{1,0:T(8,128)(2,1)S(1)} %fusion.79) | copy-start | bytes 2359300
  287.3 3.8 copy-start.100
  291.1 8.8 slice-start.3
  293.4 6.6 slice-start.4
  303.0 104.4 %copy-start.72 = (f32[512]{0:T(512)}, f32[512]{0:T(512)S(1)}, u32[]{:S(2)}) copy-start(f32[512]{0:T(512)S(1)} %add_rsqrt_fusion.2) | copy-start | bytes 6148
  496.5 14.6 %copy-start.80 = (f32[1,8,96]{2,1,0:T(8,128)S(1)}, f32[1,8,96]{2,1,0:T(8,128)}, u32[]{:S(2)}) copy-start(f32[1,8,96]{2,1,0:T(8,128)} %get-tuple-element.113) | copy-start | bytes 9220
  496.5 30.9 %all-to-all-start.3 = ((bf16[4,192,512]{2,1,0:T(8,128)(2,1)}), bf16[4,192,512]{2,1,0:T(8,128)(2,1)}, u32[]{:S(2)}, u32[]{:S(2)}) async-start(bf16[4,192,512]{2,1,0:T(8,128)(2,1)} %get-tuple-element.23), calls=%async_computation.3 | async-start | bytes 1572864 | tf_op jit(solution)/shard_map/all_to_all | solution.py:555
  500.8 448.9 %reduce-scatter.11.cloned.1.call-start = ((), (), s32[]{:S(2)}) async-start(), calls=%async_computation.17 | async-start | bytes 5308416 | tf_op jit(solution)/shard_map/reduce_scatter | solution.py:839
  502.3 21.5 %collective-permute-start.6 = (bf16[256,768]{1,0:T(8,128)(2,1)S(1)}, bf16[256,768]{1,0:T(8,128)(2,1)}, u32[]{:S(2)}, u32[]{:S(2)}) collective-permute-start(bf16[256,768]{1,0:T(8,128)(2,1)S(1)} %select_bitcast_fusion), channel_id=1, source_target_pairs={{0,4},{1,5},{2,6},{3,7},{4,0},{5,1},{6,2},{7,3},{8,12},{9,13},{10,... | collective-permute-start | bytes 1179656 | tf_op jit(solution)/shard_map/ppermute | solution.py:510
  517.9 7.9 copy-start.61
  530.6 4.0 copy-start.67
  531.1 7.1 copy-start.43
  565.0 384.8 %reduce-scatter.9.cloned.1.call-start = ((), (), s32[]{:S(2)}) async-start(), calls=%async_computation.16 | async-start | bytes 5308416 | tf_op jit(solution)/shard_map/reduce_scatter | solution.py:839
  568.3 10.8 copy-start.50
  568.3 8.3 slice-start
  571.0 5.6 copy-start.105
  571.0 5.6 slice-start.1
  697.8 5.2 copy-start.17
  715.0 311.8 %reduce-scatter.7.cloned.1.call-start = ((), (), s32[]{:S(2)}) async-start(), calls=%async_computation.15 | async-start | bytes 10616832 | tf_op jit(solution)/shard_map/reduce_scatter | solution.py:838
  732.6 459.0 %reduce-scatter.5.cloned.1.call-start = ((), (), s32[]{:S(2)}) async-start(), calls=%async_computation.14 | async-start | bytes 10616832 | tf_op jit(solution)/shard_map/reduce_scatter | solution.py:838
  732.9 5.7 copy-start.119
  736.2 7.4 slice-start.5
  738.6 5.0 slice-start.6
  752.0 122.5 %copy-start.7 = (f32[512,768]{1,0:T(8,128)}, f32[512,768]{1,0:T(8,128)S(1)}, u32[]{:S(2)}) copy-start(f32[512,768]{1,0:T(8,128)S(1)} %get-tuple-element.65) | copy-start | bytes 4718596
  868.5 4.1 copy-start.22
  883.8 5.4 copy-start.5
  883.9 384.4 %all-reduce.3.cloned.1.call-start = ((), (), s32[]{:S(2)}) async-start(), calls=%async_computation.20 | async-start | bytes 7077888 | tf_op jit(solution)/shard_map/psum | solution.py:842
  887.0 52.1 %collective-permute-start.5 = (bf16[256,768]{1,0:T(8,128)(2,1)}, bf16[256,768]{1,0:T(8,128)(2,1)}, u32[]{:S(2)}, u32[]{:S(2)}) collective-permute-start(bf16[256,768]{1,0:T(8,128)(2,1)} %select_convert_fusion.1), channel_id=1, source_target_pairs={{0,4},{1,5},{2,6},{3,7},{4,0},{5,1},{6,2},{7,3},{8,12},{9,13},{10,... | collective-permute-start | bytes 1179656 | tf_op jit(solution)/shard_map/ppermute | solution.py:510
  898.4 40.8 %copy-start.12 = (f32[512,768]{1,0:T(8,128)S(1)}, f32[512,768]{1,0:T(8,128)}, u32[]{:S(2)}) copy-start(f32[512,768]{1,0:T(8,128)} %get-tuple-element.92) | copy-start | bytes 4718596
  899.3 1.7 collective-permute-start.8
  900.2 291.4 %collective-permute-start.7 = (bf16[256,768]{1,0:T(8,128)(2,1)}, bf16[256,768]{1,0:T(8,128)(2,1)}, u32[]{:S(2)}, u32[]{:S(2)}) collective-permute-start(bf16[256,768]{1,0:T(8,128)(2,1)} %select_convert_fusion), channel_id=1, source_target_pairs={{0,4},{1,5},{2,6},{3,7},{4,0},{5,1},{6,2},{7,3},{8,12},{9,13},{10,... | collective-permute-start | bytes 1179656 | tf_op jit(solution)/shard_map/ppermute | solution.py:510
  901.0 39.3 %collective-permute-start.9 = (f32[44,768]{1,0:T(8,128)S(1)}, f32[44,768]{1,0:T(8,128)S(1)}, u32[]{:S(2)}, u32[]{:S(2)}) collective-permute-start(f32[44,768]{1,0:T(8,128)S(1)} %add.497), channel_id=1, source_target_pairs={{0,16},{8,24},{16,0},{24,8},{1,17},{9,25},{17,1},{25,9},{2,18},{10... | collective-permute-start | bytes 405512 | tf_op jit(solution)/shard_map/ppermute | solution.py:510
  940.3 9.3 collective-permute-start.10
  949.6 243.1 %collective-permute-start.11 = (f32[44,768]{1,0:T(8,128)S(1)}, f32[44,768]{1,0:T(8,128)S(1)}, u32[]{:S(2)}, u32[]{:S(2)}) collective-permute-start(f32[44,768]{1,0:T(8,128)S(1)} %add.499), channel_id=1, source_target_pairs={{0,2},{1,3},{2,0},{3,1},{4,6},{5,7},{6,4},{7,5},{8,10},{9,11},{10,... | collective-permute-start | bytes 405512 | tf_op jit(solution)/shard_map/ppermute | solution.py:510
  1192.8 9.2 collective-permute-start.12
  (92 other events, 187.1 us)
Sparse Core Ops, SparseCore 0:
  14.2 155.0 all-gather.6
  171.5 95.0 all-gather.10
  269.4 135.5 all-gather.8
  407.7 96.5 all-gather.12
  565.1 118.4 reduce-scatter.10
  715.1 103.8 reduce-scatter.8
  822.6 204.1 reduce-scatter.6
  1030.4 161.1 reduce-scatter.4
  1194.2 73.9 all-reduce.2

commit v2 on v1

--- a/solution.py
+++ b/solution.py
@@ -827,6 +827,136 @@
     return grad_hidden, mat_grads, down_grads, sums
 
 
+MESH = pl.DeviceIdType.MESH
+
+
+def places():
+    rep, shard = (lax.axis_index("rep"), lax.axis_index("shard"))
+    core, y, z = (lax.rem(rep, 2), lax.rem(shard, 2), lax.div(shard, 2))
+    across_x = lax.rem(rep + 2, 4)
+    across_core = rep + 1 - 2 * core
+    zs = (z, z + 1 - 2 * lax.rem(z, 2), lax.rem(z + 2, 4), 3 - z)
+    return (rep, shard, core, y, across_x, across_core, zs)
+
+
+def greet():
+    rep, shard, core, y, across_x, across_core, zs = places()
+    barrier = pltpu.get_barrier_semaphore()
+    partners = [(rep, 2 * other + y) for other in zs[1:]]
+    partners += [(rep, 2 * zs[0] + 1 - y), (across_x, shard), (across_core, shard)]
+    for partner in partners:
+        pl.semaphore_signal(barrier, inc=1, device_id=partner, device_id_type=MESH)
+    pl.semaphore_wait(barrier, len(partners))
+
+
+class Sends:
+    def __init__(self, sems):
+        self.sems = sems
+        self.copies = []
+
+    def push(self, source, target, arrived, device):
+        copy = pltpu.make_async_remote_copy(
+            source, target, self.sems.at[len(self.copies)], arrived, device_id=device, device_id_type=MESH
+        )
+        copy.start()
+        self.copies.append(copy)
+
+    def finish(self):
+        for copy in self.copies:
+            copy.wait_send()
+
+
+def gather_kernel(own_mats, own_downs, mats, downs, local_sems, send_sems, mat_sems, down_sems):
+    rep, shard, core, y, across_x, across_core, zs = places()
+    greet()
+    sends = Sends(send_sems)
+
+    def mat_piece(chunk, quarter):
+        return mats.at[:, chunk, quarter]
+
+    def send_mat(chunk, quarter, device, source=None):
+        target = mat_piece(chunk, quarter)
+        sends.push(target if source is None else source, target, mat_sems.at[chunk, quarter], device)
+
+    def send_down(chunk, device, source=None):
+        target = downs.at[chunk, core]
+        sends.push(target if source is None else source, target, down_sems.at[chunk, core], device)
+
+    def wait_mat(chunk, quarter):
+        piece = mat_piece(chunk, quarter)
+        pltpu.make_async_copy(piece, piece, mat_sems.at[chunk, quarter]).wait()
+
+    def wait_down(chunk, half):
+        piece = downs.at[chunk, half]
+        pltpu.make_async_copy(piece, piece, down_sems.at[chunk, half]).wait()
+
+    beside = (rep, 2 * zs[0] + 1 - y)
+    own_mat, own_down = (own_mats.at[:, rep], own_downs.at[core])
+    for k in (2, 3, 1):
+        send_mat(shard, rep, (rep, 2 * zs[k] + y), own_mat)
+    send_mat(shard, rep, beside, own_mat)
+    for k in (2, 3, 1):
+        send_down(shard, (rep, 2 * zs[k] + y), own_down)
+    send_down(shard, beside, own_down)
+    local = [
+        pltpu.make_async_copy(own_mats, mats.at[:, shard], local_sems.at[0]),
+        pltpu.make_async_copy(own_downs, downs.at[shard], local_sems.at[1]),
+    ]
+    for copy in local:
+        copy.start()
+
+    events = ((0, 1), (1, 0), (2, 0), (1, 1), (3, 0), (2, 1), (3, 1))
+    chunks = [2 * zs[k] + (1 - y if far else y) for k, far in events]
+
+    def from_x(chunk):
+        wait_mat(chunk, across_x)
+        send_mat(chunk, across_x, (across_core, shard))
+
+    for at, (chunk, (k, far)) in enumerate(zip(chunks, events)):
+        wait_mat(chunk, rep)
+        if not far:
+            send_mat(chunk, rep, beside)
+        send_mat(chunk, rep, (across_x, shard))
+        send_mat(chunk, rep, (across_core, shard))
+        wait_down(chunk, core)
+        if not far:
+            send_down(chunk, beside)
+        send_down(chunk, (across_core, shard))
+        if at >= 3:
+            from_x(chunks[at - 3])
+    for chunk in chunks[-3:]:
+        from_x(chunk)
+    for chunk in chunks:
+        wait_mat(chunk, across_core)
+        wait_mat(chunk, lax.rem(across_core + 2, 4))
+        wait_down(chunk, 1 - core)
+    for copy in local:
+        copy.wait()
+    sends.finish()
+
+
+def gather_fast(own, down):
+    count, rows, width = own.shape
+    full, half = pl.pallas_call(
+        gather_kernel,
+        name="gather",
+        out_shape=(
+            jax.ShapeDtypeStruct((count, 8, 4, rows // 4, width), BF16),
+            jax.ShapeDtypeStruct((8, 2, down.shape[0] // 2, width), BF16),
+        ),
+        in_specs=in_vmem(2),
+        out_specs=[pl.BlockSpec(memory_space=pl.ANY)] * 2,
+        scratch_shapes=[
+            pltpu.SemaphoreType.DMA((2,)),
+            pltpu.SemaphoreType.DMA((42,)),
+            pltpu.SemaphoreType.DMA((8, 4)),
+            pltpu.SemaphoreType.DMA((8, 2)),
+        ],
+        compiler_params=pltpu.CompilerParams(collective_id=0, has_side_effects=True),
+    )(own.reshape(count, 4, rows // 4, width), down.reshape(2, down.shape[0] // 2, width))
+    return (full.reshape(count, 8 * rows, width), half.reshape(8 * down.shape[0], width))
+
+
 def gather_weights(mats, downs):
     return (
         lax.all_gather(mats, "shard", axis=1, tiled=True),
@@ -834,12 +964,246 @@
     )
 
 
+def reduce_kernel(
+    mats, downs, qkv_out, proj_out, up_out, down_out,
+    core_mats, x_mats, y_mats, z_mats, core_downs, y_downs, z_downs, x_down,
+    x_stage, y_stage, z_stage, yd_stage, zd_stage, xd_stage, all_mats, all_downs,
+    send_sems, core_sems, x_sems, y_sems, z_sems, core_d_sems, y_d_sems, z_d_sems, x_d_sem,
+    all_sems, all_d_sems,
+):
+    rep, shard, core, y, across_x, across_core, zs = places()
+    x = lax.div(rep, 2)
+    beside, past_x, past_core = ((rep, 2 * zs[0] + 1 - y), (across_x, shard), (across_core, shard))
+    greet()
+    sends = Sends(send_sems)
+
+    def arrive(ref, sem):
+        pltpu.make_async_copy(ref, ref, sem).wait()
+
+    def chunk_of(k, far):
+        return 2 * zs[k] + (1 - y if far else y)
+
+    def add_mats(target, parts):
+        def body(block, carry):
+            total = parts[0][block].astype(F32)
+            for part in parts[1:]:
+                total = total + part[block].astype(F32)
+            target[block] = total.astype(BF16)
+            return carry
+
+        lax.fori_loop(0, mats.shape[2], body, 0)
+
+    def add_downs(target, parts):
+        rows = 32
+
+        def body(step, carry):
+            at = pl.ds(pl.multiple_of(step * rows, rows), rows)
+            total = parts[0][at].astype(F32)
+            for part in parts[1:]:
+                total = total + part[at].astype(F32)
+            target[at] = total.astype(BF16)
+            return carry
+
+        lax.fori_loop(0, downs.shape[2] // rows, body, 0)
+
+    far_order = [(k, 1) for k in (2, 3, 1, 0)]
+    near_order = [(k, 0) for k in (2, 3, 1)]
+    own = (0, 0)
+
+    def mat_at(chunk, quarter):
+        return mats.at[chunk, quarter]
+
+    for k, far in far_order + near_order + [own]:
+        chunk = chunk_of(k, far)
+        for side in (1, 0):
+            which = (1 - x) if side else x
+            sends.push(
+                mat_at(chunk, 2 * which + 1 - core),
+                core_mats.at[chunk, which],
+                core_sems.at[chunk, which],
+                past_core,
+            )
+        sends.push(downs.at[chunk, 1 - core], core_downs.at[chunk], core_d_sems.at[chunk], past_core)
+
+    def step_x(slot, place):
+        chunk = chunk_of(*place)
+        arrive(core_mats.at[chunk, 1 - x], core_sems.at[chunk, 1 - x])
+        add_mats(x_stage.at[slot], [mat_at(chunk, across_x), core_mats.at[chunk, 1 - x]])
+        sends.push(x_stage.at[slot], x_mats.at[chunk], x_sems.at[chunk], past_x)
+
+    def mat_parts(chunk):
+        arrive(core_mats.at[chunk, x], core_sems.at[chunk, x])
+        arrive(x_mats.at[chunk], x_sems.at[chunk])
+        return [mat_at(chunk, rep), core_mats.at[chunk, x], x_mats.at[chunk]]
+
+    def down_parts(chunk):
+        arrive(core_downs.at[chunk], core_d_sems.at[chunk])
+        return [downs.at[chunk, core], core_downs.at[chunk]]
+
+    def step_y(place):
+        k = place[0]
+        add_mats(y_stage.at[k], mat_parts(chunk_of(*place)))
+        sends.push(y_stage.at[k], y_mats.at[k], y_sems.at[k], beside)
+
+    def step_yd(place):
+        k = place[0]
+        add_downs(yd_stage.at[k], down_parts(chunk_of(*place)))
+        sends.push(yd_stage.at[k], y_downs.at[k], y_d_sems.at[k], beside)
+
+    def step_z(place):
+        k = place[0]
+        parts = mat_parts(chunk_of(*place))
+        arrive(y_mats.at[k], y_sems.at[k])
+        add_mats(z_stage.at[k - 1], parts + [y_mats.at[k]])
+        sends.push(z_stage.at[k - 1], z_mats.at[k - 1], z_sems.at[k - 1], (rep, 2 * zs[k] + y))
+
+    def step_zd(place):
+        k = place[0]
+        parts = down_parts(chunk_of(*place))
+        arrive(y_downs.at[k], y_d_sems.at[k])
+        add_downs(zd_stage.at[k - 1], parts + [y_downs.at[k]])
+        sends.push(zd_stage.at[k - 1], z_downs.at[k - 1], z_d_sems.at[k - 1], (rep, 2 * zs[k] + y))
+
+    far, near = (far_order, near_order)
+    step_x(0, far[0])
+    step_yd(far[0])
+    step_x(1, far[1])
+    step_yd(far[1])
+    step_x(2, far[2])
+    step_yd(far[2])
+    step_yd(far[3])
+    step_y(far[0])
+    step_x(3, far[3])
+    step_y(far[1])
+    step_x(4, near[0])
+    step_zd(near[0])
+    step_y(far[2])
+    step_x(5, near[1])
+    step_zd(near[1])
+    step_y(far[3])
+    step_x(6, near[2])
+    step_zd(near[2])
+    step_z(near[0])
+    step_x(7, own)
+    step_z(near[1])
+    step_z(near[2])
+
+    parts = down_parts(shard)
+    arrive(y_downs.at[0], y_d_sems.at[0])
+    for k in range(3):
+        arrive(z_downs.at[k], z_d_sems.at[k])
+    add_downs(xd_stage, parts + [y_downs.at[0]] + [z_downs.at[k] for k in range(3)])
+    sends.push(xd_stage, x_down, x_d_sem, past_x)
+
+    parts = mat_parts(shard)
+    arrive(y_mats.at[0], y_sems.at[0])
+    for k in range(3):
+        arrive(z_mats.at[k], z_sems.at[k])
+    add_mats(all_mats.at[rep], parts + [y_mats.at[0]] + [z_mats.at[k] for k in range(3)])
+    sends.push(all_mats.at[rep], all_mats.at[rep], all_sems.at[rep], past_x)
+    sends.push(all_mats.at[rep], all_mats.at[rep], all_sems.at[rep], past_core)
+
+    arrive(x_down, x_d_sem)
+    add_downs(all_downs.at[core], [xd_stage, x_down])
+    sends.push(all_downs.at[core], all_downs.at[core], all_d_sems.at[core], past_core)
+
+    arrive(all_mats.at[across_x], all_sems.at[across_x])
+    sends.push(all_mats.at[across_x], all_mats.at[across_x], all_sems.at[across_x], past_core)
+    opposite = lax.rem(across_core + 2, 4)
+    arrive(all_mats.at[across_core], all_sems.at[across_core])
+    arrive(all_mats.at[opposite], all_sems.at[opposite])
+    arrive(all_downs.at[1 - core], all_d_sems.at[1 - core])
+
+    quarter, width = (mats.shape[3], mats.shape[4])
+    for q in range(4):
+        rows = slice(q * quarter, (q + 1) * quarter)
+        for block in range(all_mats.shape[1]):
+            piece = all_mats[q, block].astype(F32)
+            if block < 3:
+                qkv_out[rows, block * width : (block + 1) * width] = piece
+            elif block == 3:
+                proj_out[rows, :] = piece
+            else:
+                up_out[rows, (block - 4) * width : (block - 3) * width] = piece
+    half = all_downs.shape[1]
+    for c in range(2):
+        down_out[c * half : (c + 1) * half, :] = all_downs[c].astype(F32)
+    sends.finish()
+
+
+def reduce_fast(mat_grads, down_grads):
+    count = len(mat_grads)
+    width = mat_grads[0].shape[1]
+    quarter = mat_grads[0].shape[0] // 32
+    mats = jnp.stack([item.reshape(8, 4, quarter, width) for item in mat_grads], axis=2)
+    downs = jnp.concatenate(down_grads, axis=0)
+    half = downs.shape[0] // 16
+    downs = downs.reshape(8, 2, half, width)
+
+    def mat_buf(*lead):
+        return pltpu.VMEM(lead + (count, quarter, width), BF16)
+
+    def down_buf(*lead):
+        return pltpu.VMEM(lead + (half, width), BF16)
+
+    dma = pltpu.SemaphoreType.DMA
+    return pl.pallas_call(
+        reduce_kernel,
+        name="reduce",
+        out_shape=(
+            jax.ShapeDtypeStruct((4 * quarter, 3 * width), F32),
+            jax.ShapeDtypeStruct((4 * quarter, width), F32),
+            jax.ShapeDtypeStruct((4 * quarter, (count - 4) * width), F32),
+            jax.ShapeDtypeStruct((2 * half, width), F32),
+        ),
+        in_specs=in_vmem(2),
+        out_specs=in_vmem(4),
+        scratch_shapes=[
+            mat_buf(8, 2), mat_buf(8), mat_buf(4), mat_buf(3),
+            down_buf(8), down_buf(4), down_buf(3), down_buf(),
+            mat_buf(8), mat_buf(4), mat_buf(3),
+            down_buf(4), down_buf(3), down_buf(),
+            mat_buf(4), down_buf(2),
+            dma((51,)), dma((8, 2)), dma((8,)), dma((4,)), dma((3,)),
+            dma((8,)), dma((4,)), dma((3,)), dma(()), dma((4,)), dma((2,)),
+        ],
+        compiler_params=pltpu.CompilerParams(
+            collective_id=1, has_side_effects=True, vmem_limit_bytes=60 * 1024 * 1024
+        ),
+    )(mats, downs)
+
+
+def spread_rep(piece):
+    rep = lax.axis_index("rep")
+    for bit in range(2):
+        other = exchange(piece, "rep", 1 << bit)
+        piece = ordered((rep >> bit) & 1 == 0, piece, other)
+    return piece.reshape((4,) + piece.shape[2:])
+
+
 def scatter_grads(mat_grads, down_grads):
-    mats = lax.psum_scatter(jnp.stack(mat_grads), "shard", scatter_dimension=1, tiled=True)
+    width = mat_grads[0].shape[1]
+    rows = mat_grads[0].shape[0]
+
+    def by_rep(tensor):
+        split = tensor.reshape(8, 4, tensor.shape[0] // 32, width)
+        return jnp.transpose(split, (1, 0, 2, 3)).reshape(tensor.shape)
+
+    mats = lax.psum_scatter(
+        jnp.stack([by_rep(item) for item in mat_grads]),
+        ("rep", "shard"), scatter_dimension=1, tiled=True,
+    )
     downs = lax.psum_scatter(
-        jnp.concatenate(down_grads, axis=0), "shard", scatter_dimension=0, tiled=True
-    )
-    return (lax.psum(mats, "rep").astype(F32), lax.psum(downs, "rep").astype(F32))
+        by_rep(jnp.concatenate(down_grads, axis=0)),
+        ("rep", "shard"), scatter_dimension=0, tiled=True,
+    )
+    mats = jnp.transpose(spread_rep(mats), (1, 0, 2, 3)).reshape(len(mat_grads), rows // 8, width)
+    downs = spread_rep(downs).reshape(-1, width)
+
+    def side(low, high):
+        return jnp.concatenate(list(mats[low:high]), axis=1).astype(F32)
+
+    return (side(0, 3), side(3, 4), side(4, len(mat_grads)), downs.astype(F32))
 
 
 def on_device_fast(
@@ -856,7 +1220,7 @@
     for layer in range(LAYERS):
         own = jnp.concatenate([qkv_weight[layer], proj_weight[layer], up_weight[layer]], axis=1)
         own = jnp.stack([own[:, part * width : (part + 1) * width] for part in range(4 + ups)])
-        weights.append(gather_weights(own, down_weight[layer]))
+        weights.append((gather_fast if layer == 0 else gather_weights)(own, down_weight[layer]))
 
     vec_args = (
         query_bias, value_bias, proj_bias, attn_gain, attn_shift, down_bias, ffn_gain, ffn_shift,
@@ -903,7 +1267,7 @@
         grad, mat_grads, down_grads, sums[layer] = fast_backward(
             grad, mats, downs, vecs[layer], saved[layer], spans, seg_col, seg_row
         )
-        shares[layer] = scatter_grads(mat_grads, down_grads)
+        shares[layer] = (reduce_fast if layer == 0 else scatter_grads)(mat_grads, down_grads)
     input_grad = from_groups(grad, index)
     memory_sum = lax.dot_general(
         slot_hot.astype(F32), grad, (((0,), (0,)), ((), ())), precision=lax.Precision.HIGHEST
@@ -919,25 +1283,23 @@
     upbias_grad = lax.dynamic_slice_in_dim(up_sums, index * share * ups, share * ups, 1)
     memory_grad = own[LAYERS * per :]
 
-    def wide_grad(low, high):
-        return jnp.stack(
-            [jnp.concatenate(list(shares[layer][0][low:high]), axis=1) for layer in range(LAYERS)]
-        )
+    def wide_grad(member):
+        return jnp.stack([shares[layer][member] for layer in range(LAYERS)])
 
     return (
         layer_output,
         input_grad,
         memory_grad,
-        wide_grad(0, 3),
+        wide_grad(0),
         vec_grads[0],
         vec_grads[1],
-        wide_grad(3, 4),
+        wide_grad(1),
         vec_grads[2],
         vec_grads[3],
         vec_grads[4],
-        wide_grad(4, 4 + ups),
+        wide_grad(2),
         upbias_grad,
-        jnp.stack([shares[layer][1] for layer in range(LAYERS)]),
+        wide_grad(3),
         vec_grads[5],
         vec_grads[6],
         vec_grads[7],

time: 1290 us -> 940 us (0.73)
  waiting for transfers between devices: 638 us -> 88.9 us
  Pallas kernels: 142 us -> 389 us
  blocking collectives: 203 us -> 70.9 us
  local copies, waits for them, and re-layouts: 43.5 us -> 144 us
  matrix products: 153 us -> 117 us
    pallas_call x0 -> x2, Pallas kernels: none -> 247 us  [the longest x1 147 us: gather_fast(): pl.pallas_call(gather_kernel, name='gather', out_shape=(jax.ShapeDtypeStr...]
    reduce_scatter x4 -> x1, waiting for transfers between devices: 242 us -> 0.01 us  [scatter_grads(): lax.psum_scatter(by_rep(jnp.concatenate(down_grads, axis=0)), ('rep', 'sh...]
    all_gather x2 -> x1, waiting for transfers between devices: 196 us -> 0.01 us  [gather_weights(): lax.all_gather(mats, 'shard', axis=1, tiled=True)]
    all_to_all x5 -> x2, blocking collectives: 203 us -> 70.9 us  [swap(): lax.all_to_all(flat, 'shard', 0, 0, axis_index_groups=[[0, 1, 2, 3], [4,...]
    psum x1 -> x0, waiting for transfers between devices: 60.2 us -> none  [scatter_grads(): lax.psum(mats, 'rep').astype(F32)]
    unnamed x281 -> x416, local copies, waits for them, and re-layouts: 19 us -> 63.3 us
    dot_general x73, matrix products: 152 us -> 115 us  [mm(): lax.dot_general(left, right, (((left_dim,), (right_dim,)), ((), ())), pre...]
    ppermute x13 -> x17, waiting for transfers between devices: 88.2 us -> 52.9 us  [exchange(): return lax.ppermute(tensor, axis, [(i, i ^ mask) for i in range(count)])]
  transfers between devices with their start and end apart: 25 -> 27, of which waited for: 14 -> 11; matrix products, arithmetic and copies ran while one was open for 15% -> 26% of each run, Pallas kernels for 11% -> 38%
where the time goes in v2:
time: 940 us; the launch traced here: 927 us
  Pallas kernels  389 us (41%)
  local copies, waits for them, and re-layouts  144 us (15%)
  matrix products  117 us (12%)
  waiting for transfers between devices  88.9 us (9%)
  blocking collectives  70.9 us (8%)
  starting transfers between devices  52.6 us (6%)
  other arithmetic  48.6 us (5%)
  between operations  16.4 us (2%)
    pallas_call x1, Pallas kernels, gather_fast(): pl.pallas_call(gather_kernel, name='gather', out_shape=(jax.ShapeDtypeStr...  147 us
    dot_general x73, matrix products, mm(): lax.dot_general(left, right, (((left_dim,), (right_dim,)), ((), ())), pre...  115 us
    pallas_call x1, Pallas kernels, reduce_fast(): pl.pallas_call(reduce_kernel, name='reduce', out_shape=(jax.ShapeDtypeStr...  101 us
    pallas_call x2, Pallas kernels, attend_back(): pl.pallas_call(attend_back_kernel, name='attend_back', out_shape=jax.Shap...  72.6 us
    all_to_all x2, blocking collectives, swap(): lax.all_to_all(flat, 'shard', 0, 0, axis_index_groups=[[0, 1, 2, 3], [4,...  70.9 us
    pallas_call x2, Pallas kernels, attend(): pl.pallas_call(attend_kernel, name='attend', out_shape=(jax.ShapeDtypeStr...  69.4 us
    unnamed x416, local copies, waits for them, and re-layouts  63.3 us
    ppermute x17, waiting for transfers between devices, exchange(): return lax.ppermute(tensor, axis, [(i, i ^ mask) for i in range(count)])  52.9 us
  transfers between devices with their start and end apart: 27, of which 11 were waited for; matrix products, arithmetic and copies ran while one was open for 26% of the time, Pallas kernels for 38%

profile of v2, /device:TPU:0, one launch (start us, length us, event | category | flops | bytes accessed | tf_op | source)
XLA Modules:
  0.0 926.9 jit_solution(8240319690285721729)
XLA Ops:
  14.8 4.1 collective-permute-start.1
  24.7 146.7 %gather.1 = (bf16[8,8,4,24,768]{4,3,2,1,0:T(8,128)(2,1)}, bf16[8,2,192,768]{3,2,1,0:T(8,128)(2,1)}) custom-call(bf16[8,4,24,768]{3,2,1,0:T(8,128)(2,1)} %copy-done.39, bf16[2,192,768]{2,1,0:T(8,128)(2,1)} %bitcast.479), custom_call_target="tpu_custom_call" | custom-call | tf_op jit(solution)/shard_map/gather/pallas_call | solution.py:940
  171.4 6.6 fusion.91
  179.6 3.5 collective-permute-done.3
  183.3 6.5 collective-permute-done.4
  200.7 4.4 all-to-all-start
  205.5 2.1 fusion.90
  211.2 30.8 %all-to-all-done.x_ref = bf16[4,576,512]{2,1,0:T(8,128)(2,1)S(1)} async-done(((bf16[4,576,512]{2,1,0:T(8,128)(2,1)}), bf16[4,576,512]{2,1,0:T(8,128)(2,1)S(1)}, u32[]{:S(2)}, u32[]{:S(2)}) %all-to-all-start) | async-done | bytes 2359328 | tf_op jit(solution)/shard_map/all_to_all | solution.py:555
  243.8 34.7 %attend.2 = (bf16[4,192,512]{2,1,0:T(8,128)(2,1)}, f32[4,192,512]{2,1,0:T(8,128)}, f32[3,8,1,256]{3,2,1,0:T(1,128)}) custom-call(s32[8]{0:T(128)} %get-tuple-element.63.lo_ref, s32[8]{0:T(128)} %get-tuple-element.62.hi_ref, bf16[4,576,512]{2,1,0:T(8,128)(2,1)} %copy-done.2, s32[2048,128]{1,0:T(8,128)} %broadcast_in_dim.2.seg_col, s32[8,1,256]{2,1,0:T(1,128)} %bitcast.552), custom_call_target="tpu_custom_call" | custom-call | tf_op jit(solution)/shard_map/attend/pallas_call | solution.py:698
  278.5 3.7 all-to-all-start.1
  283.0 4.6 fusion.92
  295.2 3.4 fusion.111
  305.3 2.0 multiply_convert_fusion.15
  314.8 2.4 convolution_convert_fusion.26
  317.2 2.1 add_convert_fusion
  319.3 2.1 fusion.51
  321.6 56.7 %all_to_all.60.x_ref = bf16[4,576,512]{2,1,0:T(8,128)(2,1)} all-to-all(bf16[4,576,512]{2,1,0:T(8,128)(2,1)S(1)} %pad_maximum_fusion.3), channel_id=1, replica_groups={{0,1,2,3},{4,5,6,7},{8,9,10,11},{12,13,14,15},{16,17,18,19},{20,21,22,2..., dimensions={0} | all-to-all | bytes 4718592 | tf_op jit(solution)/shard_map/all_to_all | solution.py:555
  378.3 34.7 %attend.3 = (bf16[4,192,512]{2,1,0:T(8,128)(2,1)}, f32[4,192,512]{2,1,0:T(8,128)}, f32[3,8,1,256]{3,2,1,0:T(1,128)}) custom-call(s32[8]{0:T(128)} %get-tuple-element.63.lo_ref, s32[8]{0:T(128)} %get-tuple-element.62.hi_ref, bf16[4,576,512]{2,1,0:T(8,128)(2,1)} %all_to_all.60.x_ref, s32[2048,128]{1,0:T(8,128)} %broadcast_in_dim.2.seg_col, s32[8,1,256]{2,1,0:T(1,128)} %bitcast.553), custom_call_target="tpu_custom_call" | custom-call | tf_op jit(solution)/shard_map/attend/pallas_call | solution.py:698
  413.1 4.6 all-to-all-start.3
  418.8 4.6 collective-permute-start.6
  435.5 5.6 collective-permute-done.6
  444.7 2.6 fusion.113
  448.5 3.5 convolution_add_fusion
  452.0 3.6 multiply_convert_fusion.9
  455.6 3.6 multiply_convert_fusion.10
  459.1 2.4 fusion.60
  461.5 2.1 fusion.58
  463.7 2.3 multiply_convert_fusion.11
  472.4 2.5 convert_reduce_fusion.5
  487.1 14.2 %all_to_all.61.go_ref = bf16[4,192,512]{2,1,0:T(8,128)(2,1)} all-to-all(bf16[4,192,512]{2,1,0:T(8,128)(2,1)S(1)} %bitcast.529), channel_id=1, replica_groups={{0,1,2,3},{4,5,6,7},{8,9,10,11},{12,13,14,15},{16,17,18,19},{20,21,22,2..., dimensions={0} | all-to-all | bytes 1572864 | tf_op jit(solution)/shard_map/all_to_all | solution.py:555
  501.3 36.3 %attend_back.2 = bf16[4,576,512]{2,1,0:T(8,128)(2,1)} custom-call(s32[8]{0:T(128)} %get-tuple-element.63.lo_ref, s32[8]{0:T(128)} %get-tuple-element.62.hi_ref, bf16[4,576,512]{2,1,0:T(8,128)(2,1)} %all_to_all.60.x_ref, bf16[4,192,512]{2,1,0:T(8,128)(2,1)} %all_to_all.61.go_ref, f32[4,192,512]{2,1,0:T(8,128)} %get-tuple-element.32.out_ref, ...), custom_call_target="tpu_custom_call" | custom-call | tf_op jit(solution)/shard_map/attend_back/pallas_call | solution.py:720
  537.6 4.5 all-to-all-start.5
  542.2 2.3 convolution_convert_fusion.1
  548.4 2.5 copy.77
  551.1 2.2 convolution_convert_fusion.5
  565.5 4.6 all-to-all-done.5
  585.9 8.7 copy.84
  594.6 2.4 fusion.54
  597.1 2.2 fusion.53
  599.4 3.8 multiply_reduce_fusion.1
  603.1 2.3 convert_reduce_fusion.13
  605.5 2.1 convert_reduce_fusion.10
  609.7 2.6 convert_reduce_fusion.11
  612.3 2.6 convert_reduce_fusion.12
  614.9 2.5 fusion.119
  621.2 2.0 multiply_reduce_fusion.2
  626.2 3.6 all-to-all-start.6
  636.0 17.3 %collective-permute-done.5 = bf16[256,768]{1,0:T(8,128)(2,1)S(1)} collective-permute-done((bf16[256,768]{1,0:T(8,128)(2,1)S(1)}, bf16[256,768]{1,0:T(8,128)(2,1)S(1)}, u32[]{:S(2)}, u32[]{:S(2)}) %collective-permute-start.5) | collective-permute-done | bytes 393248 | tf_op jit(solution)/shard_map/ppermute | solution.py:510
  658.1 36.3 %attend_back.3 = bf16[4,576,512]{2,1,0:T(8,128)(2,1)} custom-call(s32[8]{0:T(128)} %get-tuple-element.63.lo_ref, s32[8]{0:T(128)} %get-tuple-element.62.hi_ref, bf16[4,576,512]{2,1,0:T(8,128)(2,1)} %copy-done.2, bf16[4,192,512]{2,1,0:T(8,128)(2,1)} %copy-done.29, f32[4,192,512]{2,1,0:T(8,128)} %get-tuple-element.34.out_ref, ...), custom_call_target="tpu_custom_call" | custom-call | tf_op jit(solution)/shard_map/attend_back/pallas_call | solution.py:720
  694.3 3.8 all-to-all-start.7
  698.2 3.1 convolution_convert_fusion.18
  709.4 2.6 pad_maximum_fusion
  712.1 2.4 convert_reduce_fusion.7
  730.5 3.2 convolution_convert_fusion.19
  744.4 5.6 concatenate.56
  768.5 100.6 %reduce.16 = (f32[96,2304]{1,0:T(8,128)}, f32[96,768]{1,0:T(8,128)}, f32[96,3072]{1,0:T(8,128)}, f32[384,768]{1,0:T(8,128)}) custom-call(bf16[8,4,8,24,768]{4,3,2,1,0:T(8,128)(2,1)} %constant_dynamic-update-slice_fusion.8.mats, bf16[8,2,192,768]{3,2,1,0:T(8,128)(2,1)} %bitcast.450), custom_call_target="tpu_custom_call" | custom-call | tf_op jit(solution)/shard_map/reduce/pallas_call | solution.py:1150
  870.5 2.8 pad_maximum_fusion.5
  873.4 2.2 collective-permute-done.10
  875.6 5.7 collective-permute-start.11
  882.4 2.4 collective-permute-done.11
  884.8 3.0 collective-permute-start.12
  889.1 4.9 collective-permute-done.12
  898.1 2.0 collective-permute-start.14
  904.4 9.4 %collective-permute-done.14 = bf16[2,8,24,768]{3,2,1,0:T(8,128)(2,1)S(1)} collective-permute-done((bf16[2,8,24,768]{3,2,1,0:T(8,128)(2,1)S(1)}, bf16[2,8,24,768]{3,2,1,0:T(8,128)(2,1)S(1)}, u32[]{:S(2)}, u32[]{:S(2)}) %collective-permute-start.14) | collective-permute-done | bytes 589856 | tf_op jit(solution)/shard_map/ppermute | solution.py:510
  (673 shorter events, 213.5 us)
Async XLA Ops:
  7.2 307.6 %all-gather.4.cloned.1.call-start = ((), (), s32[]{:S(2)}) async-start(), calls=%async_computation.10 | async-start | bytes 10616832 | tf_op jit(solution)/shard_map/all_gather | solution.py:962
  10.7 8.2 copy-start.144
  10.7 8.4 copy-start.155
  10.7 8.4 copy-start.156
  10.7 8.4 copy-start.157
  10.7 8.4 copy-start.158
  10.7 8.4 copy-start.159
  10.7 8.4 copy-start.160
  10.8 8.4 copy-start.161
  10.8 8.4 copy-start.162
  10.8 8.4 copy-start.143
  10.8 10.1 %copy-start.30 = (bf16[2,256,768]{2,1,0:T(8,128)(2,1)S(1)}, bf16[2,256,768]{2,1,0:T(8,128)(2,1)}, u32[]{:S(2)}) copy-start(bf16[2,256,768]{2,1,0:T(8,128)(2,1)} %param.18) | copy-start | bytes 2359300
  14.8 164.1 %collective-permute-start.1 = (s32[256,1]{0,1:T(1,128)}, s32[256,1]{0,1:T(1,128)}, u32[]{:S(2)}, u32[]{:S(2)}) collective-permute-start(s32[256,1]{0,1:T(1,128)} %fusion.84), channel_id=1, source_target_pairs={{0,4},{1,5},{2,6},{3,7},{4,0},{5,1},{6,2},{7,3},{8,12},{9,13},{10,... | collective-permute-start | bytes 3080 | tf_op jit(solution)/shard_map/ppermute | solution.py:510
  19.3 158.7 %collective-permute-start.2 = (bf16[44,96]{1,0:T(8,128)(2,1)S(1)}, bf16[44,96]{1,0:T(8,128)(2,1)}, u32[]{:S(2)}, u32[]{:S(2)}) collective-permute-start(bf16[44,96]{1,0:T(8,128)(2,1)S(1)} %concatenate.53), channel_id=1, source_target_pairs={{0,1},{1,0},{2,3},{3,2},{4,5},{5,4},{6,7},{7,6},{8,9},{9,8},{10,11... | collective-permute-start | bytes 25352 | tf_op jit(solution)/shard_map/ppermute | solution.py:510
  21.7 171.2 %collective-permute-start = (bf16[256,768]{1,0:T(8,128)(2,1)}, bf16[256,768]{1,0:T(8,128)(2,1)}, u32[]{:S(2)}, u32[]{:S(2)}) collective-permute-start(bf16[256,768]{1,0:T(8,128)(2,1)} %select_bitcast_fusion.3), channel_id=1, source_target_pairs={{0,4},{1,5},{2,6},{3,7},{4,0},{5,1},{6,2},{7,3},{8,12},{9,13},{10,... | collective-permute-start | bytes 1179656 | tf_op jit(solution)/shard_map/ppermute | solution.py:510
  178.0 19.0 %copy-start.15 = (bf16[1,8,4,24,768]{4,3,2,1,0:T(8,128)(2,1)}, bf16[1,8,4,24,768]{4,3,2,1,0:T(8,128)(2,1)S(1)}, u32[]{:S(2)}) copy-start(bf16[1,8,4,24,768]{4,3,2,1,0:T(8,128)(2,1)S(1)} %get-tuple-element.81) | copy-start | bytes 3538948
  178.0 121.6 %copy-start.17 = (bf16[1,8,4,24,768]{4,3,2,1,0:T(8,128)(2,1)}, bf16[1,8,4,24,768]{4,3,2,1,0:T(8,128)(2,1)S(1)}, u32[]{:S(2)}) copy-start(bf16[1,8,4,24,768]{4,3,2,1,0:T(8,128)(2,1)S(1)} %get-tuple-element.76) | copy-start | bytes 3538948
  178.8 4.3 collective-permute-start.3
  183.1 6.6 collective-permute-start.4
  183.2 13.7 %copy-start.116 = (s32[1,2,2,128]{3,1,2,0:T(2,128)}, s32[1,2,2,128]{3,1,2,0:T(2,128)S(1)}, u32[]{:S(2)}) copy-start(s32[1,2,2,128]{3,1,2,0:T(2,128)S(1)} %copy.82) | copy-start | bytes 6148
  200.7 41.4 %all-to-all-start = ((bf16[4,576,512]{2,1,0:T(8,128)(2,1)}), bf16[4,576,512]{2,1,0:T(8,128)(2,1)S(1)}, u32[]{:S(2)}, u32[]{:S(2)}) async-start(bf16[4,576,512]{2,1,0:T(8,128)(2,1)} %pad_maximum_fusion.2), calls=%async_computation | async-start | bytes 4718592 | tf_op jit(solution)/shard_map/all_to_all | solution.py:555
  207.6 36.1 %copy-start.98 = (s32[1,2048]{1,0:T(1,128)}, s32[1,2048]{1,0:T(1,128)S(1)}, u32[]{:S(2)}) copy-start(s32[1,2048]{1,0:T(1,128)S(1)} %get-tuple-element.75) | copy-start | bytes 24580
  278.5 16.7 %all-to-all-start.1 = ((bf16[4,192,512]{2,1,0:T(8,128)(2,1)}), bf16[4,192,512]{2,1,0:T(8,128)(2,1)S(1)}, u32[]{:S(2)}, u32[]{:S(2)}) async-start(bf16[4,192,512]{2,1,0:T(8,128)(2,1)} %get-tuple-element.29), calls=%async_computation.1 | async-start | bytes 1572864 | tf_op jit(solution)/shard_map/all_to_all | solution.py:555
  282.2 177.0 %all-gather.6.cloned.1.call-start = ((), (), s32[]{:S(2)}) async-start(), calls=%async_computation.12 | async-start | bytes 5308416 | tf_op jit(solution)/shard_map/all_gather | solution.py:963
  282.9 8.8 copy-start.134
  282.9 8.8 copy-start.133
  282.9 8.9 copy-start.132
  282.9 9.6 %copy-start.131 = (f32[1,8,96]{2,1,0:T(8,128)S(1)}, f32[1,8,96]{2,1,0:T(8,128)}, u32[]{:S(2)}) copy-start(f32[1,8,96]{2,1,0:T(8,128)} %get-tuple-element.153) | copy-start | bytes 9220
  282.9 10.2 %copy-start.130 = (f32[1,8,96]{2,1,0:T(8,128)S(1)}, f32[1,8,96]{2,1,0:T(8,128)}, u32[]{:S(2)}) copy-start(f32[1,8,96]{2,1,0:T(8,128)} %get-tuple-element.148) | copy-start | bytes 9220
  282.9 10.9 %copy-start.129 = (f32[1,8,96]{2,1,0:T(8,128)S(1)}, f32[1,8,96]{2,1,0:T(8,128)}, u32[]{:S(2)}) copy-start(f32[1,8,96]{2,1,0:T(8,128)} %get-tuple-element.149) | copy-start | bytes 9220
  282.9 11.5 %copy-start.128 = (f32[1,8,96]{2,1,0:T(8,128)S(1)}, f32[1,8,96]{2,1,0:T(8,128)}, u32[]{:S(2)}) copy-start(f32[1,8,96]{2,1,0:T(8,128)} %get-tuple-element.152) | copy-start | bytes 9220
  283.0 12.2 %copy-start.127 = (f32[1,8,96]{2,1,0:T(8,128)S(1)}, f32[1,8,96]{2,1,0:T(8,128)}, u32[]{:S(2)}) copy-start(f32[1,8,96]{2,1,0:T(8,128)} %get-tuple-element.155) | copy-start | bytes 9220
  291.7 153.0 %copy-start.101 = (f32[768]{0:T(1024)}, f32[768]{0:T(1024)S(1)}, u32[]{:S(2)}) copy-start(f32[768]{0:T(1024)S(1)} %mul.420) | copy-start | bytes 9220
  299.3 11.7 %copy-start.107 = (f32[512]{0:T(512)}, f32[512]{0:T(512)S(1)}, u32[]{:S(2)}) copy-start(f32[512]{0:T(512)S(1)} %add_rsqrt_fusion.3) | copy-start | bytes 6148
  300.5 10.5 %copy-start.34 = (f32[512,768]{1,0:T(8,128)}, f32[512,768]{1,0:T(8,128)S(1)}, u32[]{:S(2)}) copy-start(f32[512,768]{1,0:T(8,128)S(1)} %convolution_add_fusion.4) | copy-start | bytes 4718596
  413.1 15.7 %copy-start.126 = (f32[1,8,96]{2,1,0:T(8,128)S(1)}, f32[1,8,96]{2,1,0:T(8,128)}, u32[]{:S(2)}) copy-start(f32[1,8,96]{2,1,0:T(8,128)} %get-tuple-element.142) | copy-start | bytes 9220
  413.1 31.7 %all-to-all-start.3 = ((bf16[4,192,512]{2,1,0:T(8,128)(2,1)}), bf16[4,192,512]{2,1,0:T(8,128)(2,1)}, u32[]{:S(2)}, u32[]{:S(2)}) async-start(bf16[4,192,512]{2,1,0:T(8,128)(2,1)} %get-tuple-element.31), calls=%async_computation.3 | async-start | bytes 1572864 | tf_op jit(solution)/shard_map/all_to_all | solution.py:555
  418.8 22.4 %collective-permute-start.6 = (bf16[256,768]{1,0:T(8,128)(2,1)S(1)}, bf16[256,768]{1,0:T(8,128)(2,1)}, u32[]{:S(2)}, u32[]{:S(2)}) collective-permute-start(bf16[256,768]{1,0:T(8,128)(2,1)S(1)} %select_bitcast_fusion.2), channel_id=1, source_target_pairs={{0,4},{1,5},{2,6},{3,7},{4,0},{5,1},{6,2},{7,3},{8,12},{9,13},{10,... | collective-permute-start | bytes 1179656 | tf_op jit(solution)/shard_map/ppermute | solution.py:510
  435.5 7.7 copy-start.103
  448.5 7.1 copy-start.82
  476.0 7.8 copy-start.92
  537.6 32.6 %all-to-all-start.5 = ((bf16[4,576,512]{2,1,0:T(8,128)(2,1)}), bf16[4,576,512]{2,1,0:T(8,128)(2,1)}, u32[]{:S(2)}, u32[]{:S(2)}) async-start(bf16[4,576,512]{2,1,0:T(8,128)(2,1)} %attend_back.2), calls=%async_computation.5 | async-start | bytes 4718592 | tf_op jit(solution)/shard_map/all_to_all | solution.py:555
  542.1 169.9 %reduce-scatter.5.cloned.1.call-start = ((), (), s32[]{:S(2)}) async-start(), calls=%async_computation.11 | async-start | bytes 4866048 | tf_op jit(solution)/shard_map/reduce_scatter | solution.py:1196
  550.9 344.4 %reduce-scatter.7.cloned.1.call-start = ((), (), s32[]{:S(2)}) async-start(), calls=%async_computation.13 | async-start | bytes 9732096
  605.4 6.9 copy-start.85
  626.2 7.4 copy-start.135
  626.2 31.0 %all-to-all-start.6 = ((bf16[4,192,512]{2,1,0:T(8,128)(2,1)}), bf16[4,192,512]{2,1,0:T(8,128)(2,1)S(1)}, u32[]{:S(2)}, u32[]{:S(2)}) async-start(bf16[4,192,512]{2,1,0:T(8,128)(2,1)} %bitcast.85), calls=%async_computation.6 | async-start | bytes 1572864 | tf_op jit(solution)/shard_map/all_to_all | solution.py:555
  629.9 23.3 %collective-permute-start.5 = (bf16[256,768]{1,0:T(8,128)(2,1)S(1)}, bf16[256,768]{1,0:T(8,128)(2,1)S(1)}, u32[]{:S(2)}, u32[]{:S(2)}) collective-permute-start(bf16[256,768]{1,0:T(8,128)(2,1)S(1)} %select_convert_fusion.1), channel_id=1, source_target_pairs={{0,4},{1,5},{2,6},{3,7},{4,0},{5,1},{6,2},{7,3},{8,12},{9,13},{10,... | collective-permute-start | bytes 1179656 | tf_op jit(solution)/shard_map/ppermute | solution.py:510
  694.3 41.6 %all-to-all-start.7 = ((bf16[4,576,512]{2,1,0:T(8,128)(2,1)}), bf16[4,576,512]{2,1,0:T(8,128)(2,1)S(1)}, u32[]{:S(2)}, u32[]{:S(2)}) async-start(bf16[4,576,512]{2,1,0:T(8,128)(2,1)} %attend_back.3), calls=%async_computation.7 | async-start | bytes 4718592 | tf_op jit(solution)/shard_map/all_to_all | solution.py:555
  712.0 8.5 copy-start.120
  712.0 16.0 %copy-start.122 = (f32[768]{0:T(1024)S(1)}, f32[768]{0:T(1024)}, u32[]{:S(2)}) copy-start(f32[768]{0:T(1024)} %get-tuple-element.44) | copy-start | bytes 9220
  712.0 17.9 %copy-start.121 = (f32[768]{0:T(1024)S(1)}, f32[768]{0:T(1024)}, u32[]{:S(2)}) copy-start(f32[768]{0:T(1024)} %get-tuple-element.57) | copy-start | bytes 9220
  712.0 2.5 collective-permute-start.15
  716.0 17.8 %collective-permute-start.16 = (bf16[2,96,768]{2,1,0:T(8,128)(2,1)}, bf16[2,96,768]{2,1,0:T(8,128)(2,1)}, u32[]{:S(2)}, u32[]{:S(2)}) collective-permute-start(bf16[2,96,768]{2,1,0:T(8,128)(2,1)} %pad_maximum_fusion.15), channel_id=1, source_target_pairs={{0,16},{8,24},{16,0},{24,8},{1,17},{9,25},{17,1},{25,9},{2,18},{10... | collective-permute-start | bytes 884744 | tf_op jit(solution)/shard_map/ppermute | solution.py:510
  743.0 8.7 copy-start.72
  750.0 15.6 %collective-permute-start.8 = (f32[44,768]{1,0:T(8,128)}, f32[44,768]{1,0:T(8,128)S(1)}, u32[]{:S(2)}, u32[]{:S(2)}) collective-permute-start(f32[44,768]{1,0:T(8,128)} %concatenate.56), channel_id=1, source_target_pairs={{0,8},{8,0},{16,24},{24,16},{1,9},{9,1},{17,25},{25,17},{2,10},{10... | collective-permute-start | bytes 405512 | tf_op jit(solution)/shard_map/ppermute | solution.py:510
  751.1 130.2 %collective-permute-start.7 = (bf16[256,768]{1,0:T(8,128)(2,1)}, bf16[256,768]{1,0:T(8,128)(2,1)}, u32[]{:S(2)}, u32[]{:S(2)}) collective-permute-start(bf16[256,768]{1,0:T(8,128)(2,1)} %select_convert_fusion), channel_id=1, source_target_pairs={{0,4},{1,5},{2,6},{3,7},{4,0},{5,1},{6,2},{7,3},{8,12},{9,13},{10,... | collective-permute-start | bytes 1179656 | tf_op jit(solution)/shard_map/ppermute | solution.py:510
  765.6 103.4 %collective-permute-start.9 = (f32[44,768]{1,0:T(8,128)S(1)}, f32[44,768]{1,0:T(8,128)S(1)}, u32[]{:S(2)}, u32[]{:S(2)}) collective-permute-start(f32[44,768]{1,0:T(8,128)S(1)} %add.485), channel_id=1, source_target_pairs={{0,16},{8,24},{16,0},{24,8},{1,17},{9,25},{17,1},{25,9},{2,18},{10... | collective-permute-start | bytes 405512 | tf_op jit(solution)/shard_map/ppermute | solution.py:510
  768.5 102.1 %copy-start.24 = (f32[1,384,768]{2,1,0:T(8,128)S(1)}, f32[1,384,768]{2,1,0:T(8,128)}, u32[]{:S(2)}) copy-start(f32[1,384,768]{2,1,0:T(8,128)} %convert.12) | copy-start | bytes 3538948
  869.1 6.5 collective-permute-start.10
  875.6 9.2 collective-permute-start.11
  884.8 9.1 collective-permute-start.12
  896.3 1.6 collective-permute-start.13
  898.1 15.7 %collective-permute-start.14 = (bf16[2,8,24,768]{3,2,1,0:T(8,128)(2,1)S(1)}, bf16[2,8,24,768]{3,2,1,0:T(8,128)(2,1)S(1)}, u32[]{:S(2)}, u32[]{:S(2)}) collective-permute-start(bf16[2,8,24,768]{3,2,1,0:T(8,128)(2,1)S(1)} %pad_maximum_fusion.12), channel_id=1, source_target_pairs={{0,16},{8,24},{16,0},{24,8},{1,17},{9,25},{17,1},{25,9},{2,18},{10... | collective-permute-start | bytes 1769480 | tf_op jit(solution)/shard_map/ppermute | solution.py:510
  (152 other events, 303.1 us)
Sparse Core Ops, SparseCore 0:
  14.3 214.6 all-gather.3
  285.7 107.9 all-gather.5
  551.0 120.2 reduce-scatter.4
  677.1 173.8 reduce-scatter.6

commit v3 on v1

--- a/solution.py
+++ b/solution.py
@@ -1,3 +1,5 @@
+import functools
+
 import jax
 import jax.numpy as jnp
 from jax import lax
@@ -516,21 +518,6 @@
     )
 
 
-def gather_small(tensor):
-    index = lax.axis_index("shard")
-    for bit in range(3):
-        other = exchange(tensor, "shard", 1 << bit)
-        tensor = ordered((index >> bit) & 1 == 0, tensor, other)
-    return tensor.reshape((8,) + tensor.shape[3:])
-
-
-def sum_small(tensor):
-    for axis, bits in (("rep", 2), ("shard", 3)):
-        for bit in range(bits):
-            tensor = tensor + exchange(tensor, axis, 1 << bit)
-    return tensor
-
-
 def to_groups(tensor, index):
     low = index < GROUP
     mine = jnp.where(low, tensor[0], tensor[1])
@@ -598,19 +585,30 @@
 
         def per_key(j, inner):
             allowed = pair_mask(seg_col, seg_row, j, i)
+            olds = [top[h] for h in range(heads)]
+            sums = [total[h] for h in range(heads)]
+            mixes = [acc[h] for h in range(heads)]
+            scores = [
+                mm(keys_nat[h, j], x_ref[src, h * HEAD_DIM : (h + 1) * HEAD_DIM, cols], 1, 0)
+                for h in range(heads)
+            ]
+            scores = [jnp.where(allowed, item, masked_score) for item in scores]
+            news = [
+                jnp.maximum(old, jnp.max(item, axis=0, keepdims=True)) for old, item in zip(olds, scores)
+            ]
+            raised = [jnp.exp(item - new) for item, new in zip(scores, news)]
+            adds = [
+                mm(
+                    x_ref[j % GROUP, 2 * width + h * HEAD_DIM : 2 * width + (h + 1) * HEAD_DIM, block_cols(j)],
+                    raised[h].astype(BF16), 1, 0,
+                )
+                for h in range(heads)
+            ]
             for h in range(heads):
-                query = x_ref[src, h * HEAD_DIM : (h + 1) * HEAD_DIM, cols]
-                value = x_ref[
-                    j % GROUP, 2 * width + h * HEAD_DIM : 2 * width + (h + 1) * HEAD_DIM, block_cols(j)
-                ]
-                scores = jnp.where(allowed, mm(keys_nat[h, j], query, 1, 0), masked_score)
-                old = top[h]
-                new = jnp.maximum(old, jnp.max(scores, axis=0, keepdims=True))
-                raised = jnp.exp(scores - new)
-                fade = jnp.exp(old - new)
-                top[h] = new
-                total[h] = total[h] * fade + jnp.sum(raised, axis=0, keepdims=True)
-                acc[h] = acc[h] * fade + mm(value, raised.astype(BF16), 1, 0)
+                fade = jnp.exp(olds[h] - news[h])
+                top[h] = news[h]
+                total[h] = sums[h] * fade + jnp.sum(raised[h], axis=0, keepdims=True)
+                acc[h] = mixes[h] * fade + adds[h]
             return inner
 
         lax.fori_loop(lo_ref[i], hi_ref[i], per_key, 0)
@@ -657,17 +655,30 @@
         def per_query(i, inner):
             src, cols = (i % GROUP, block_cols(i))
             allowed = pair_mask(seg_col, seg_row, j, i)
+            spots = [slice(h * HEAD_DIM, (h + 1) * HEAD_DIM) for h in range(heads)]
+            old_dv = [dv[h] for h in range(heads)]
+            old_dk = [dk[h] for h in range(heads)]
+            old_dq = [dq[h, i] for h in range(heads)]
+            queries = [x_ref[src, spot, cols] for spot in spots]
+            grads = [go_ref[src, spot, cols] for spot in spots]
+            scores = [mm(keys_nat[h, j], queries[h], 1, 0) for h in range(heads)]
+            grad_probs = [mm(values_nat[h, j], grads[h], 1, 0) for h in range(heads)]
+            probs = [
+                jnp.exp(jnp.where(allowed, scores[h], masked_score) - lse_ref[h, i]) for h in range(heads)
+            ]
+            grad_scores = [
+                (probs[h] * (grad_probs[h] - delta[h, i])).astype(BF16) for h in range(heads)
+            ]
+            add_dv = [mm(grads[h], probs[h].astype(BF16), 1, 1) for h in range(heads)]
+            add_dk = [mm(queries[h], grad_scores[h], 1, 1) for h in range(heads)]
+            add_dq = [
+                mm(x_ref[key_src, width + h * HEAD_DIM : width + (h + 1) * HEAD_DIM, key_cols], grad_scores[h], 1, 0)
+                for h in range(heads)
+            ]
             for h in range(heads):
-                low, high = (h * HEAD_DIM, (h + 1) * HEAD_DIM)
-                query = x_ref[src, low:high, cols]
-                grad = go_ref[src, low:high, cols]
-                scores = jnp.where(allowed, mm(keys_nat[h, j], query, 1, 0), masked_score)
-                probs = jnp.exp(scores - lse_ref[h, i])
-                grad_probs = mm(values_nat[h, j], grad, 1, 0)
-                grad_scores = (probs * (grad_probs - delta[h, i])).astype(BF16)
-                dv[h] += mm(grad, probs.astype(BF16), 1, 1)
-                dk[h] += mm(query, grad_scores, 1, 1)
-                dq[h, i] += mm(x_ref[key_src, width + low : width + high, key_cols], grad_scores, 1, 0)
+                dv[h] = old_dv[h] + add_dv[h]
+                dk[h] = old_dk[h] + add_dk[h]
+                dq[h, i] = old_dq[h] + add_dq[h]
             return inner
 
         lax.fori_loop(lo_ref[j], hi_ref[j], per_query, 0)
@@ -751,95 +762,434 @@
     return (inner * inverse, jnp.sum(grad * normed, axis=0), jnp.sum(grad, axis=0))
 
 
-def fast_forward(hidden, mats, downs, vecs, spans, seg_col, seg_row):
+def fast_forward(hidden, weights, vecs, spans, seg_col, seg_row):
     query_b, value_b, proj_b, attn_g, attn_s, down_b, ffn_g, ffn_s, up_b = vecs
     width = hidden.shape[1]
     hidden_low = hidden.astype(BF16)
-    query = (mm(mats[0], hidden_low, 0, 1) + query_b[:, None]).astype(BF16) * BF16(0.125)
-    keys = mm(mats[1], hidden_low, 0, 1).astype(BF16)
-    values = (mm(mats[2], hidden_low, 0, 1) + value_b[:, None]).astype(BF16)
+    qkv_w, later = weights
+    mixed = mm(qkv_w, hidden_low, 0, 1)
+    query = (mixed[:width] + query_b[:, None]).astype(BF16) * BF16(0.125)
+    keys = mixed[width : 2 * width].astype(BF16)
+    values = (mixed[2 * width :] + value_b[:, None]).astype(BF16)
     share = width // GROUP
     packed = jnp.concatenate(
         [part.reshape(GROUP, share, part.shape[1]) for part in (query, keys, values)], axis=1
     )
-    qkv = swap(packed)
+    proj_w, up_w, down_w, qkv = later(packed)
     low, out, lse = attend(qkv, spans, seg_col, seg_row)
     context = swap(low).reshape(width, low.shape[2])
-    attn_out = mm(context, mats[3], 0, 0) + proj_b
+    attn_out = mm(context, proj_w, 0, 0) + proj_b
     settled, normed_one, inverse_one = norm_rows(hidden + attn_out, attn_g, attn_s)
     settled_low = settled.astype(BF16)
-    ffn_out = down_b
-    actives, slopes = ([], [])
-    for part in range(len(mats) - 4):
-        before = mm(settled_low, mats[4 + part], 1, 0) + up_b[part * width : (part + 1) * width]
-        below = 0.5 * (1.0 + lax.erf(before * 0.7071067811865476))
-        active = (before * below).astype(BF16)
-        slopes.append((below + before * jnp.exp(-0.5 * before * before) * 0.3989422804014327).astype(BF16))
-        actives.append(active)
-        ffn_out = ffn_out + mm(active, downs[part * width : (part + 1) * width], 1, 0)
+    before = mm(settled_low, up_w, 1, 0) + up_b
+    below = 0.5 * (1.0 + lax.erf(before * 0.7071067811865476))
+    active = (before * below).astype(BF16)
+    slope = (below + before * jnp.exp(-0.5 * before * before) * 0.3989422804014327).astype(BF16)
+    ffn_out = mm(active, down_w, 1, 0) + down_b
     result, normed_two, inverse_two = norm_rows(settled + ffn_out, ffn_g, ffn_s)
-    return result, (
+    return result, (qkv_w, proj_w, up_w, down_w), (
         hidden_low, qkv, out, lse, context, normed_one, inverse_one, settled_low,
-        actives, slopes, normed_two, inverse_two,
-    )
-
-
-def fast_backward(grad, mats, downs, vecs, saved, spans, seg_col, seg_row):
+        active, slope, normed_two, inverse_two,
+    )
+
+
+def fast_backward(grad, weights, vecs, saved, spans, seg_col, seg_row):
     query_b, value_b, proj_b, attn_g, attn_s, down_b, ffn_g, ffn_s, up_b = vecs
+    qkv_w, proj_w, up_w, down_w = weights
     (
         hidden_low, qkv, out, lse, context, normed_one, inverse_one, settled_low,
-        actives, slopes, normed_two, inverse_two,
+        active, slope, normed_two, inverse_two,
     ) = saved
     width = grad.shape[1]
     grad_two, ffn_g_sum, ffn_s_sum = norm_rows_back(grad, normed_two, inverse_two, ffn_g)
     grad_ffn = grad_two.astype(BF16)
     down_b_sum = jnp.sum(grad_ffn.astype(F32), axis=0)
-    grad_settled = grad_two
-    mat_grads = [None] * len(mats)
-    down_grads, up_b_sums = ([], [])
-    for part in range(len(actives)):
-        rows = slice(part * width, (part + 1) * width)
-        grad_before = (mm(grad_ffn, downs[rows], 1, 1) * slopes[part].astype(F32)).astype(BF16)
-        down_grads.append(mm(actives[part], grad_ffn, 0, 0).astype(BF16))
-        mat_grads[4 + part] = mm(settled_low, grad_before, 0, 0).astype(BF16)
-        up_b_sums.append(jnp.sum(grad_before.astype(F32), axis=0))
-        grad_settled = grad_settled + mm(grad_before, mats[4 + part], 1, 1)
+    grad_before = (mm(grad_ffn, down_w, 1, 1) * slope.astype(F32)).astype(BF16)
+    down_grad = mm(active, grad_ffn, 0, 0).astype(BF16)
+    up_grad = mm(settled_low, grad_before, 0, 0).astype(BF16)
+    up_b_sum = jnp.sum(grad_before.astype(F32), axis=0)
+    grad_settled = grad_two + mm(grad_before, up_w, 1, 1)
     grad_one, attn_g_sum, attn_s_sum = norm_rows_back(grad_settled, normed_one, inverse_one, attn_g)
     grad_attn = grad_one.astype(BF16)
     proj_b_sum = jnp.sum(grad_attn.astype(F32), axis=0)
-    grad_context = mm(mats[3], grad_attn, 1, 1).astype(BF16)
-    mat_grads[3] = mm(context, grad_attn, 1, 0).astype(BF16)
+    grad_context = mm(proj_w, grad_attn, 1, 1).astype(BF16)
+    proj_grad = mm(context, grad_attn, 1, 0).astype(BF16)
     grad_out = swap(grad_context.reshape(GROUP, width // GROUP, grad_context.shape[1]))
     moved = swap(attend_back(qkv, grad_out, out, lse, spans, seg_col, seg_row))
     share = width // GROUP
-    pieces = [
-        moved[:, part * share : (part + 1) * share].reshape(width, moved.shape[2]) for part in range(3)
+    mixed = jnp.transpose(moved.reshape(GROUP, 3, share, moved.shape[2]), (1, 0, 2, 3))
+    mixed = mixed.reshape(3 * width, moved.shape[2])
+    qkv_grad = mm(hidden_low, mixed, 0, 1).astype(BF16)
+    grad_hidden = grad_one + mm(mixed, qkv_w, 0, 1)
+    mixed_sum = jnp.sum(mixed.astype(F32), axis=1)
+    sums = [
+        mixed_sum[:width], mixed_sum[2 * width :], proj_b_sum, attn_g_sum, attn_s_sum, down_b_sum,
+        ffn_g_sum, ffn_s_sum,
     ]
-    grad_hidden = grad_one
-    for part in range(3):
-        mat_grads[part] = mm(hidden_low, pieces[part], 0, 1).astype(BF16)
-        grad_hidden = grad_hidden + mm(pieces[part], mats[part], 0, 1)
-    query_b_sum = jnp.sum(pieces[0].astype(F32), axis=1)
-    value_b_sum = jnp.sum(pieces[2].astype(F32), axis=1)
-    sums = [
-        query_b_sum, value_b_sum, proj_b_sum, attn_g_sum, attn_s_sum, down_b_sum, ffn_g_sum, ffn_s_sum,
-    ] + up_b_sums
-    return grad_hidden, mat_grads, down_grads, sums
-
-
-def gather_weights(mats, downs):
-    return (
-        lax.all_gather(mats, "shard", axis=1, tiled=True),
-        lax.all_gather(downs, "shard", axis=0, tiled=True),
-    )
-
-
-def scatter_grads(mat_grads, down_grads):
-    mats = lax.psum_scatter(jnp.stack(mat_grads), "shard", scatter_dimension=1, tiled=True)
-    downs = lax.psum_scatter(
-        jnp.concatenate(down_grads, axis=0), "shard", scatter_dimension=0, tiled=True
-    )
-    return (lax.psum(mats, "rep").astype(F32), lax.psum(downs, "rep").astype(F32))
+    sums += [up_b_sum[part * width : (part + 1) * width] for part in range(up_w.shape[1] // width)]
+    return grad_hidden, (qkv_grad, proj_grad, up_grad, down_grad), sums
+
+
+MESH = pl.DeviceIdType.MESH
+
+
+def places():
+    rep, shard = (lax.axis_index("rep"), lax.axis_index("shard"))
+    core, y, z = (lax.rem(rep, 2), lax.rem(shard, 2), lax.div(shard, 2))
+    across_x = lax.rem(rep + 2, 4)
+    across_core = rep + 1 - 2 * core
+    zs = (z, z + 1 - 2 * lax.rem(z, 2), lax.rem(z + 2, 4), 3 - z)
+    return (rep, shard, core, y, across_x, across_core, zs)
+
+
+def greet(diagonal=False):
+    rep, shard, core, y, across_x, across_core, zs = places()
+    barrier = pltpu.get_barrier_semaphore()
+    partners = [(rep, 2 * other + y) for other in zs[1:]]
+    partners += [(rep, 2 * zs[0] + 1 - y), (across_x, shard), (across_core, shard)]
+    if diagonal:
+        partners += [(rep, 2 * other + 1 - y) for other in zs[1:]]
+    for partner in partners:
+        pl.semaphore_signal(barrier, inc=1, device_id=partner, device_id_type=MESH)
+    pl.semaphore_wait(barrier, len(partners))
+
+
+class Sends:
+    def __init__(self, sems):
+        self.sems = sems
+        self.copies = []
+
+    def push(self, source, target, arrived, device):
+        copy = pltpu.make_async_remote_copy(
+            source, target, self.sems.at[len(self.copies)], arrived, device_id=device, device_id_type=MESH
+        )
+        copy.start()
+        self.copies.append(copy)
+
+    def finish(self):
+        for copy in self.copies:
+            copy.wait_send()
+
+
+def gather_kernel(fourths, smalls, swaps, *refs):
+    count = fourths + smalls
+    total = count + swaps
+    owns, fulls = (refs[:total], refs[total : 2 * total])
+    local_sems, send_sems, fourth_sems, small_sems, swap_sems = refs[2 * total :]
+    rep, shard, core, y, across_x, across_core, zs = places()
+    member = lax.rem(shard, GROUP)
+    greet(smalls + swaps > 0)
+    sends = Sends(send_sems)
+    beside, past_x, past_core = ((rep, 2 * zs[0] + 1 - y), (across_x, shard), (across_core, shard))
+
+    def send(n, chunk, part, device, own=False):
+        target = fulls[n].at[chunk, part]
+        source = owns[n].at[part] if own else target
+        sends.push(source, target, fourth_sems.at[n, chunk, part], device)
+
+    def arrive(n, chunk, part):
+        piece = fulls[n].at[chunk, part]
+        pltpu.make_async_copy(piece, piece, fourth_sems.at[n, chunk, part]).wait()
+
+    near_members = ((1, y), (0, 1 - y), (1, 1 - y))
+    for n in range(smalls):
+        for k in range(4):
+            for other in (y, 1 - y) if k else (1 - y,):
+                sends.push(
+                    owns[fourths + n],
+                    fulls[fourths + n].at[shard],
+                    small_sems.at[shard],
+                    (rep, 2 * zs[k] + other),
+                )
+    for n in range(fourths):
+        send(n, shard, rep, beside, True)
+        for k in (1, 2, 3):
+            send(n, shard, rep, (rep, 2 * zs[k] + y), True)
+    for n in range(swaps):
+        for k, other in near_members:
+            target = 2 * zs[k] + other
+            sends.push(
+                owns[count + n].at[lax.rem(target, GROUP)],
+                fulls[count + n].at[member],
+                swap_sems.at[n, member],
+                (rep, target),
+            )
+    local = [
+        pltpu.make_async_copy(owns[n], fulls[n].at[shard], local_sems.at[n]) for n in range(count)
+    ]
+    local += [
+        pltpu.make_async_copy(owns[n].at[member], fulls[n].at[member], local_sems.at[n])
+        for n in range(count, total)
+    ]
+    for copy in local:
+        copy.start()
+
+    events = ((0, 1), (1, 0), (2, 0), (1, 1), (3, 0), (2, 1), (3, 1))
+    chunks = [2 * zs[k] + (1 - y if far else y) for k, far in events]
+
+    def from_x(chunk):
+        for n in range(fourths):
+            arrive(n, chunk, across_x)
+            send(n, chunk, across_x, past_core)
+
+    for at, (chunk, (k, far)) in enumerate(zip(chunks, events)):
+        for n in range(fourths):
+            arrive(n, chunk, rep)
+            if not far:
+                send(n, chunk, rep, beside)
+            send(n, chunk, rep, past_x)
+            send(n, chunk, rep, past_core)
+        if at >= 3:
+            from_x(chunks[at - 3])
+    for chunk in chunks[-3:]:
+        from_x(chunk)
+    for chunk in chunks:
+        for n in range(fourths):
+            arrive(n, chunk, across_core)
+            arrive(n, chunk, lax.rem(across_core + 2, 4))
+        for n in range(smalls):
+            piece = fulls[fourths + n].at[chunk]
+            pltpu.make_async_copy(piece, piece, small_sems.at[chunk]).wait()
+    for n in range(swaps):
+        for k, other in near_members:
+            source = lax.rem(2 * zs[k] + other, GROUP)
+            piece = fulls[count + n].at[source]
+            pltpu.make_async_copy(piece, piece, swap_sems.at[n, source]).wait()
+    for copy in local:
+        copy.wait()
+    sends.finish()
+
+
+def gather_fast(fourths, smalls, swaps, name, collective_id):
+    split = [item.reshape(4, item.shape[0] // 4, item.shape[1]) for item in fourths] + smalls
+    owns = split + swaps
+    dma = pltpu.SemaphoreType.DMA
+    fulls = pl.pallas_call(
+        functools.partial(gather_kernel, len(fourths), len(smalls), len(swaps)),
+        name=name,
+        out_shape=[jax.ShapeDtypeStruct((8,) + item.shape, BF16) for item in split]
+        + [jax.ShapeDtypeStruct(item.shape, BF16) for item in swaps],
+        in_specs=in_vmem(len(owns)),
+        out_specs=[pl.BlockSpec(memory_space=pl.ANY)] * len(owns),
+        scratch_shapes=[
+            dma((len(owns),)),
+            dma((28 * len(fourths) + 7 * len(smalls) + 3 * len(swaps),)),
+            dma((len(fourths), 8, 4)),
+            dma((8,)),
+            dma((max(1, len(swaps)), GROUP)),
+        ],
+        compiler_params=pltpu.CompilerParams(collective_id=collective_id, has_side_effects=True),
+    )(*owns)
+    wide = len(fourths)
+    return [item.reshape(-1, item.shape[3]) for item in fulls[:wide]] + list(fulls[wide:])
+
+
+def reduce_kernel(
+    qkv_grad, proj_grad, down_grad, small, qkv_out, proj_out, down_out, small_out, *scratch
+):
+    kinds = 2
+    mats, core_mats, x_mats, y_mats, z_mats, x_stage, y_stage, z_stage, all_mats = [
+        scratch[kinds * n : kinds * n + kinds] for n in range(9)
+    ]
+    (
+        small_sum, small_got, local_sems, send_sems, core_sems, x_sems, y_sems, z_sems, all_sems, small_sems,
+    ) = scratch[9 * kinds :]
+    rep, shard, core, y, across_x, across_core, zs = places()
+    x = lax.div(rep, 2)
+    beside, past_x, past_core = ((rep, 2 * zs[0] + 1 - y), (across_x, shard), (across_core, shard))
+    cut = qkv_grad.shape[3]
+    local = [
+        pltpu.make_async_copy(qkv_grad, mats[0].at[:, :, :, :cut], local_sems.at[0]),
+        pltpu.make_async_copy(proj_grad, mats[0].at[:, :, :, cut:], local_sems.at[1]),
+        pltpu.make_async_copy(down_grad, mats[1], local_sems.at[2]),
+    ]
+    for copy in local:
+        copy.start()
+    small_sum[0] = small[...]
+    greet()
+    sends = Sends(send_sems)
+
+    def arrive(ref, sem):
+        pltpu.make_async_copy(ref, ref, sem).wait()
+
+    def chunk_of(k, far):
+        return 2 * zs[k] + (1 - y if far else y)
+
+    def add(target, parts):
+        steps = 6
+        lanes = target.shape[1] // steps
+
+        def body(step, carry):
+            at = pl.ds(pl.multiple_of(step * lanes, lanes), lanes)
+            total = parts[0][:, at].astype(F32)
+            for part in parts[1:]:
+                total = total + part[:, at].astype(F32)
+            target[:, at] = total.astype(BF16)
+            return carry
+
+        lax.fori_loop(0, steps, body, 0)
+
+    small_partners = (past_core, past_x, beside, (rep, 2 * zs[1] + y), (rep, 2 * zs[2] + y))
+
+    def small_send(step):
+        sends.push(small_sum.at[step], small_got.at[step], small_sems.at[step], small_partners[step])
+
+    def small_step(step):
+        arrive(small_got.at[step], small_sems.at[step])
+        small_sum[step + 1] = small_sum[step] + small_got[step]
+        if step + 1 < len(small_partners):
+            small_send(step + 1)
+
+    small_send(0)
+    far = [(k, 1) for k in (2, 3, 1, 0)]
+    near = [(k, 0) for k in (2, 3, 1)]
+    own = (0, 0)
+    for copy in local:
+        copy.wait()
+    for place in far + near + [own]:
+        chunk = chunk_of(*place)
+        for n in range(kinds):
+            for which in (1 - x, x):
+                sends.push(
+                    mats[n].at[chunk, 2 * which + 1 - core],
+                    core_mats[n].at[chunk, which],
+                    core_sems.at[n, chunk, which],
+                    past_core,
+                )
+
+    def step_x(slot, place):
+        chunk = chunk_of(*place)
+        for n in range(kinds):
+            arrive(core_mats[n].at[chunk, 1 - x], core_sems.at[n, chunk, 1 - x])
+            add(x_stage[n].at[slot], [mats[n].at[chunk, across_x], core_mats[n].at[chunk, 1 - x]])
+            sends.push(x_stage[n].at[slot], x_mats[n].at[chunk], x_sems.at[n, chunk], past_x)
+
+    def parts_of(n, chunk):
+        arrive(core_mats[n].at[chunk, x], core_sems.at[n, chunk, x])
+        arrive(x_mats[n].at[chunk], x_sems.at[n, chunk])
+        return [mats[n].at[chunk, rep], core_mats[n].at[chunk, x], x_mats[n].at[chunk]]
+
+    def step_y(place):
+        k = place[0]
+        for n in range(kinds):
+            add(y_stage[n].at[k], parts_of(n, chunk_of(*place)))
+            sends.push(y_stage[n].at[k], y_mats[n].at[k], y_sems.at[n, k], beside)
+
+    def step_z(place):
+        k = place[0]
+        for n in range(kinds):
+            parts = parts_of(n, chunk_of(*place))
+            arrive(y_mats[n].at[k], y_sems.at[n, k])
+            add(z_stage[n].at[k - 1], parts + [y_mats[n].at[k]])
+            sends.push(
+                z_stage[n].at[k - 1], z_mats[n].at[k - 1], z_sems.at[n, k - 1], (rep, 2 * zs[k] + y)
+            )
+
+    step_x(0, far[0])
+    step_x(1, far[1])
+    step_x(2, far[2])
+    small_step(0)
+    step_y(far[0])
+    step_x(3, far[3])
+    step_y(far[1])
+    step_x(4, near[0])
+    small_step(1)
+    step_y(far[2])
+    step_x(5, near[1])
+    step_y(far[3])
+    step_x(6, near[2])
+    small_step(2)
+    step_z(near[0])
+    step_x(7, own)
+    step_z(near[1])
+    small_step(3)
+    step_z(near[2])
+    small_step(4)
+    small_out[...] = small_sum[len(small_partners)]
+
+    for n in range(kinds):
+        parts = parts_of(n, shard)
+        arrive(y_mats[n].at[0], y_sems.at[n, 0])
+        for k in range(3):
+            arrive(z_mats[n].at[k], z_sems.at[n, k])
+        mine = all_mats[n].at[rep]
+        add(mine, parts + [y_mats[n].at[0]] + [z_mats[n].at[k] for k in range(3)])
+        sends.push(mine, mine, all_sems.at[n, rep], past_x)
+        sends.push(mine, mine, all_sems.at[n, rep], past_core)
+    for n in range(kinds):
+        theirs = all_mats[n].at[across_x]
+        arrive(theirs, all_sems.at[n, across_x])
+        sends.push(theirs, theirs, all_sems.at[n, across_x], past_core)
+    opposite = lax.rem(across_core + 2, 4)
+    for n in range(kinds):
+        arrive(all_mats[n].at[across_core], all_sems.at[n, across_core])
+        arrive(all_mats[n].at[opposite], all_sems.at[n, opposite])
+    rows = mats[0].shape[2]
+    tall = mats[1].shape[2]
+    for q in range(4):
+        qkv_out[q * rows : (q + 1) * rows, :] = all_mats[0][q, :, :cut].astype(F32)
+        proj_out[q * rows : (q + 1) * rows, :] = all_mats[0][q, :, cut:].astype(F32)
+        down_out[q * tall : (q + 1) * tall, :] = all_mats[1][q].astype(F32)
+    sends.finish()
+
+
+def reduce_fast(qkv_grad, proj_grad, down_grad, small):
+    rows, tall = (proj_grad.shape[0] // 32, down_grad.shape[0] // 32)
+    wide = qkv_grad.shape[1] + proj_grad.shape[1]
+    sizes = ((rows, wide), (tall, down_grad.shape[1]))
+    buffers = []
+    for lead in ((8, 4), (8, 2), (8,), (4,), (3,), (8,), (4,), (3,), (4,)):
+        buffers += [pltpu.VMEM(lead + size, BF16) for size in sizes]
+    dma = pltpu.SemaphoreType.DMA
+    return pl.pallas_call(
+        reduce_kernel,
+        name="reduce",
+        out_shape=(
+            jax.ShapeDtypeStruct((4 * rows, qkv_grad.shape[1]), F32),
+            jax.ShapeDtypeStruct((4 * rows, proj_grad.shape[1]), F32),
+            jax.ShapeDtypeStruct((4 * tall, down_grad.shape[1]), F32),
+            jax.ShapeDtypeStruct(small.shape, F32),
+        ),
+        in_specs=[pl.BlockSpec(memory_space=pl.ANY)] * 3 + in_vmem(1),
+        out_specs=in_vmem(4),
+        scratch_shapes=buffers
+        + [
+            pltpu.VMEM((6,) + small.shape, F32), pltpu.VMEM((5,) + small.shape, F32),
+            dma((3,)), dma((2 * 34 + 5,)), dma((2, 8, 2)), dma((2, 8)), dma((2, 4)), dma((2, 3)),
+            dma((2, 4)), dma((5,)),
+        ],
+        compiler_params=pltpu.CompilerParams(
+            collective_id=1, has_side_effects=True, vmem_limit_bytes=56 * 1024 * 1024
+        ),
+    )(
+        qkv_grad.reshape(8, 4, rows, -1), proj_grad.reshape(8, 4, rows, -1),
+        down_grad.reshape(8, 4, tall, -1), small,
+    )
+
+
+def by_rep(grad, width):
+    blocks = grad.shape[1] // width
+    split = grad.reshape(8, 4, grad.shape[0] // 32, blocks, width)
+    return jnp.transpose(split, (1, 0, 3, 2, 4)).reshape(4, 8, grad.size // (32 * width), width)
+
+
+def scatter_all(grads, width):
+    packed = jnp.concatenate([by_rep(grad, width) for grad in grads], axis=2)
+    flat = packed.reshape(-1, width)
+    return lax.psum_scatter(flat, ("rep", "shard"), scatter_dimension=0, tiled=True)
+
+
+def spread_rep(piece):
+    rep = lax.axis_index("rep")
+    for bit in range(2):
+        other = exchange(piece, "rep", 1 << bit)
+        piece = ordered((rep >> bit) & 1 == 0, piece, other)
+    return piece.reshape((4,) + piece.shape[2:])
+
+
+def unpack(pieces, start, blocks, rows):
+    parts = [pieces[:, start + b * rows : start + (b + 1) * rows] for b in range(blocks)]
+    return jnp.concatenate([part.reshape(-1, part.shape[2]) for part in parts], axis=1).astype(F32)
 
 
 def on_device_fast(
@@ -852,12 +1202,6 @@
     share = memory_table.shape[1]
     ups = up_weight.shape[2] // width
 
-    weights = []
-    for layer in range(LAYERS):
-        own = jnp.concatenate([qkv_weight[layer], proj_weight[layer], up_weight[layer]], axis=1)
-        own = jnp.stack([own[:, part * width : (part + 1) * width] for part in range(4 + ups)])
-        weights.append(gather_weights(own, down_weight[layer]))
-
     vec_args = (
         query_bias, value_bias, proj_bias, attn_gain, attn_shift, down_bias, ffn_gain, ffn_shift,
     )
@@ -865,8 +1209,12 @@
     rows = [item[layer][None] for layer in range(LAYERS) for item in vec_args]
     rows += [up_bias[layer].reshape(ups, share) for layer in range(LAYERS)]
     rows.append(memory_table)
-    small = gather_small(jnp.concatenate(rows, axis=0)).astype(F32)
-    wide = jnp.transpose(small, (1, 0, 2)).reshape(small.shape[1], width)
+    small = jnp.concatenate(rows, axis=0)
+    used = small.shape[0]
+    small = jnp.pad(small, ((0, -used % 16), (0, 128 - share)))
+    first_qkv, small = gather_fast([qkv_weight[0]], [small], [], "gather_first", 0)
+    small = small[:, :used, :share].astype(F32)
+    wide = jnp.transpose(small, (1, 0, 2)).reshape(used, width)
     vecs = []
     for layer in range(LAYERS):
         start = LAYERS * plain + layer * ups
@@ -876,6 +1224,23 @@
         )
     table = wide[LAYERS * (plain + ups) :].astype(BF16)
 
+    second_qkv = []
+
+    def rest_first(packed):
+        proj_w, up_w, qkv_w, down_w, qkv = gather_fast(
+            [proj_weight[0], up_weight[0], qkv_weight[1], down_weight[0]], [], [packed],
+            "gather_middle", 2,
+        )
+        second_qkv.append(qkv_w)
+        return proj_w, up_w, down_w, qkv
+
+    def rest_second(packed):
+        return gather_fast(
+            [proj_weight[1], up_weight[1], down_weight[1]], [], [packed], "gather_last", 3
+        )
+
+    rests = (rest_first, rest_second)
+
     segs = jnp.where(index < GROUP, segment_ids[0], segment_ids[1])
     tiles = segs.reshape(-1, BLOCK)
     first, last = (tiles[:, 0], tiles[:, -1])
@@ -889,27 +1254,44 @@
     slots = to_groups(memory_slot[..., None], index)[:, 0]
     slot_hot = slots[:, None] == jnp.arange(MEMS, dtype=jnp.int32)
     hidden = to_groups(inputs, index).astype(F32) + mm(slot_hot.astype(BF16), table, 1, 0)
-    saved = []
+    saved, held = ([], [])
     for layer in range(LAYERS):
-        mats, downs = weights[layer]
-        hidden, state = fast_forward(hidden, mats, downs, vecs[layer], spans, seg_col, seg_row)
+        qkv_w = second_qkv[0] if layer else first_qkv
+        hidden, mats, state = fast_forward(
+            hidden, (qkv_w, rests[layer]), vecs[layer], spans, seg_col, seg_row
+        )
         saved.append(state)
+        held.append(mats)
     layer_output = from_groups(hidden, index)
 
     grad = to_groups(cotangent, index).astype(F32)
     sums, shares = ([None] * LAYERS, [None] * LAYERS)
     for layer in range(LAYERS - 1, -1, -1):
-        mats, downs = weights[layer]
-        grad, mat_grads, down_grads, sums[layer] = fast_backward(
-            grad, mats, downs, vecs[layer], saved[layer], spans, seg_col, seg_row
+        grad, (qkv_grad, proj_grad, up_grad, down_grad), sums[layer] = fast_backward(
+            grad, held[layer], vecs[layer], saved[layer], spans, seg_col, seg_row
         )
-        shares[layer] = scatter_grads(mat_grads, down_grads)
+        if layer:
+            early = scatter_all([up_grad, down_grad], width)
+            waiting = [qkv_grad, proj_grad]
+    late = scatter_all(waiting + [up_grad], width)
     input_grad = from_groups(grad, index)
     memory_sum = lax.dot_general(
         slot_hot.astype(F32), grad, (((0,), (0,)), ((), ())), precision=lax.Precision.HIGHEST
     )
     flat = jnp.concatenate([jnp.stack(sums[layer]) for layer in range(LAYERS)] + [memory_sum], axis=0)
-    flat = sum_small(flat)
+    used = flat.shape[0]
+    flat = jnp.pad(flat, ((0, -used % 8), (0, 0)))
+    qkv_own, proj_own, down_own, flat = reduce_fast(qkv_grad, proj_grad, down_grad, flat)
+    flat = flat[:used]
+    rows, tall = (width // 32, width * ups // 32)
+    early, late = (spread_rep(early), spread_rep(late))
+    shares[1] = (
+        unpack(late, 0, 3, rows),
+        unpack(late, 3 * rows, 1, rows),
+        unpack(early, 0, ups, rows),
+        unpack(early, ups * rows, 1, tall),
+    )
+    shares[0] = (qkv_own, proj_own, unpack(late, 4 * rows, ups, rows), down_own)
     per = plain + ups
     own = lax.dynamic_slice_in_dim(flat, index * share, share, 1)
     vec_grads = [
@@ -919,25 +1301,23 @@
     upbias_grad = lax.dynamic_slice_in_dim(up_sums, index * share * ups, share * ups, 1)
     memory_grad = own[LAYERS * per :]
 
-    def wide_grad(low, high):
-        return jnp.stack(
-            [jnp.concatenate(list(shares[layer][0][low:high]), axis=1) for layer in range(LAYERS)]
-        )
+    def wide_grad(member):
+        return jnp.stack([shares[layer][member] for layer in range(LAYERS)])
 
     return (
         layer_output,
         input_grad,
         memory_grad,
-        wide_grad(0, 3),
+        wide_grad(0),
         vec_grads[0],
         vec_grads[1],
-        wide_grad(3, 4),
+        wide_grad(1),
         vec_grads[2],
         vec_grads[3],
         vec_grads[4],
-        wide_grad(4, 4 + ups),
+        wide_grad(2),
         upbias_grad,
-        jnp.stack([shares[layer][1] for layer in range(LAYERS)]),
+        wide_grad(3),
         vec_grads[5],
         vec_grads[6],
         vec_grads[7],

time: 1290 us -> 842 us (0.65)
  waiting for transfers between devices: 638 us -> 133 us
  Pallas kernels: 142 us -> 392 us
  blocking collectives: 203 us -> 23.6 us
  matrix products: 153 us -> 103 us
  local copies, waits for them, and re-layouts: 43.5 us -> 79.2 us
    pallas_call x0 -> x4, Pallas kernels: none -> 291 us  [the longest x3 199 us: gather_fast(): pl.pallas_call(functools.partial(gather_kernel, len(fourths), len(smalls)...]
    reduce_scatter x4 -> x2, waiting for transfers between devices: 242 us -> 0.01 us  [scatter_all(): lax.psum_scatter(flat, ('rep', 'shard'), scatter_dimension=0, tiled=True)]
    all_gather x4 -> x0, waiting for transfers between devices: 196 us -> none  [the longest x2 196 us: gather_weights(): lax.all_gather(mats, 'shard', axis=1, tiled=True)]
    all_to_all x5 -> x2, blocking collectives: 203 us -> 23.6 us  [swap(): lax.all_to_all(flat, 'shard', 0, 0, axis_index_groups=[[0, 1, 2, 3], [4,...]
    psum x1 -> x0, waiting for transfers between devices: 60.2 us -> none  [scatter_grads(): lax.psum(mats, 'rep').astype(F32)]
    dot_general x73 -> x25, matrix products: 152 us -> 103 us  [mm(): lax.dot_general(left, right, (((left_dim,), (right_dim,)), ((), ())), pre...]
    reshape x0 -> x7, local copies, waits for them, and re-layouts: none -> 35.6 us  [by_rep(): split = grad.reshape(8, 4, grad.shape[0] // 32, blocks, width)]
    pallas_call x2, Pallas kernels: 69.3 us -> 46 us  [attend(): pl.pallas_call(attend_kernel, name='attend', out_shape=(jax.ShapeDtypeStr...]
  transfers between devices with their start and end apart: 25 -> 15, of which waited for: 14 -> 7; matrix products, arithmetic and copies ran while one was open for 15% -> 17% of each run, Pallas kernels for 11% -> 22%
where the time goes in v3:
time: 842 us; the launch traced here: 836 us
  Pallas kernels  392 us (47%)
  waiting for transfers between devices  133 us (16%)
  matrix products  103 us (12%)
  local copies, waits for them, and re-layouts  79.2 us (9%)
  other arithmetic  49.7 us (6%)
  starting transfers between devices  39.8 us (5%)
  blocking collectives  23.6 us (3%)
  between operations  16 us (2%)
    pallas_call x3, Pallas kernels, gather_fast(): pl.pallas_call(functools.partial(gather_kernel, len(fourths), len(smalls)...  199 us
    dot_general x25, matrix products, mm(): lax.dot_general(left, right, (((left_dim,), (right_dim,)), ((), ())), pre...  103 us
    pallas_call x1, Pallas kernels, reduce_fast(): pl.pallas_call(reduce_kernel, name='reduce', out_shape=(jax.ShapeDtypeStr...  92.1 us
    ppermute x9, waiting for transfers between devices, exchange(): return lax.ppermute(tensor, axis, [(i, i ^ mask) for i in range(count)])  75.9 us
    all_to_all x4, waiting for transfers between devices, swap(): lax.all_to_all(flat, 'shard', 0, 0, axis_index_groups=[[0, 1, 2, 3], [4,...  57.1 us
    pallas_call x2, Pallas kernels, attend_back(): pl.pallas_call(attend_back_kernel, name='attend_back', out_shape=jax.Shap...  54.8 us
    pallas_call x2, Pallas kernels, attend(): pl.pallas_call(attend_kernel, name='attend', out_shape=(jax.ShapeDtypeStr...  46 us
    reshape x7, local copies, waits for them, and re-layouts, by_rep(): split = grad.reshape(8, 4, grad.shape[0] // 32, blocks, width)  35.6 us
  transfers between devices with their start and end apart: 15, of which 7 were waited for; matrix products, arithmetic and copies ran while one was open for 17% of the time, Pallas kernels for 22%

profile of v3, /device:TPU:0, one launch (start us, length us, event | category | flops | bytes accessed | tf_op | source)
XLA Modules:
  0.0 836.2 jit_solution(12325388998082342570)
XLA Ops:
  8.5 4.1 collective-permute-start
  16.2 39.0 %gather_first.1 = (bf16[8,4,24,2304]{3,2,1,0:T(8,128)(2,1)}, bf16[8,48,128]{2,1,0:T(8,128)(2,1)}) custom-call(bf16[4,24,2304]{2,1,0:T(8,128)(2,1)} %bitcast.264, bf16[48,128]{1,0:T(8,128)(2,1)} %pad.8.refs_1_), custom_call_target="tpu_custom_call" | custom-call | tf_op jit(solution)/shard_map/gather_first/pallas_call | solution.py:967
  64.8 2.1 fusion.89
  67.4 1.6 pad_maximum_fusion.2.refs_4_
  68.9 90.3 %gather_middle.1 = (bf16[8,4,24,768]{3,2,1,0:T(8,128)(2,1)}, bf16[8,4,24,3072]{3,2,1,0:T(8,128)(2,1)}, bf16[8,4,24,2304]{3,2,1,0:T(8,128)(2,1)}, bf16[8,4,96,768]{3,2,1,0:T(8,128)(2,1)}, bf16[4,576,512]{2,1,0:T(8,128)(2,1)}) custom-call(bf16[4,24,768]{2,1,0:T(8,128)(2,1)} %bitcast.280, bf16[4,24,3072]{2,1,0:T(8,128)(2,1)} %bitcast.262, ...), custom_call_target="tpu_custom_call" | custom-call | tf_op jit(solution)/shard_map/gather_middle/pallas_call | solution.py:967
  160.6 23.0 %attend.2 = (bf16[4,192,512]{2,1,0:T(8,128)(2,1)}, f32[4,192,512]{2,1,0:T(8,128)}, f32[3,8,1,256]{3,2,1,0:T(1,128)}) custom-call(s32[8]{0:T(128)} %get-tuple-element.93.lo_ref, s32[8]{0:T(128)} %get-tuple-element.92.hi_ref, bf16[4,576,512]{2,1,0:T(8,128)(2,1)} %get-tuple-element.39.x_ref, s32[2048,128]{1,0:T(8,128)} %broadcast_in_dim.2.seg_col, ...), custom_call_target="tpu_custom_call" | custom-call | tf_op jit(solution)/shard_map/attend/pallas_call | solution.py:709
  183.6 3.7 all-to-all-start
  188.0 11.1 %all-to-all-done = bf16[4,192,512]{2,1,0:T(8,128)(2,1)S(1)} async-done(((bf16[4,192,512]{2,1,0:T(8,128)(2,1)}), bf16[4,192,512]{2,1,0:T(8,128)(2,1)S(1)}, u32[]{:S(2)}, u32[]{:S(2)}) %all-to-all-start) | async-done | bytes 786464 | tf_op jit(solution)/shard_map/all_to_all | solution.py:542
  199.1 2.5 fusion.85
  201.9 7.4 multiply_convert_fusion.3
  209.4 2.7 fusion.86
  212.5 2.3 fusion.57
  215.3 1.6 pad_maximum_fusion.3.refs_3_
  216.9 69.4 %gather_last.1 = (bf16[8,4,24,768]{3,2,1,0:T(8,128)(2,1)}, bf16[8,4,24,3072]{3,2,1,0:T(8,128)(2,1)}, bf16[8,4,96,768]{3,2,1,0:T(8,128)(2,1)}, bf16[4,576,512]{2,1,0:T(8,128)(2,1)}) custom-call(bf16[4,24,768]{2,1,0:T(8,128)(2,1)} %bitcast.279, bf16[4,24,3072]{2,1,0:T(8,128)(2,1)} %bitcast.260, bf16[4,96,768]{2,1,0:T(8,128)(2,1)} %bitcast.261, ...), custom_call_target="tpu_custom_call" | custom-call | tf_op jit(solution)/shard_map/gather_last/pallas_call | solution.py:967
  286.3 23.0 %attend.3 = (bf16[4,192,512]{2,1,0:T(8,128)(2,1)}, f32[4,192,512]{2,1,0:T(8,128)}, f32[3,8,1,256]{3,2,1,0:T(1,128)}) custom-call(s32[8]{0:T(128)} %get-tuple-element.93.lo_ref, s32[8]{0:T(128)} %get-tuple-element.92.hi_ref, bf16[4,576,512]{2,1,0:T(8,128)(2,1)} %get-tuple-element.45.x_ref, s32[2048,128]{1,0:T(8,128)} %broadcast_in_dim.2.seg_col, ...), custom_call_target="tpu_custom_call" | custom-call | tf_op jit(solution)/shard_map/attend/pallas_call | solution.py:709
  309.3 3.6 all-to-all-start.1
  314.2 4.6 collective-permute-start.3
  325.8 9.5 %collective-permute-done.3 = bf16[256,768]{1,0:T(8,128)(2,1)S(1)} collective-permute-done((bf16[256,768]{1,0:T(8,128)(2,1)}, bf16[256,768]{1,0:T(8,128)(2,1)S(1)}, u32[]{:S(2)}, u32[]{:S(2)}) %collective-permute-start.3) | collective-permute-done | bytes 393248 | tf_op jit(solution)/shard_map/ppermute | solution.py:512
  337.4 2.4 fusion.87
  340.6 6.5 multiply_convert_fusion.2
  347.1 2.8 fusion.88
  351.5 2.4 convert_reduce_fusion.5
  354.0 4.6 convolution_convert_fusion
  358.5 4.7 convert_reduce_fusion
  363.3 1.6 copy-done.87
  364.9 4.9 convolution_convert_fusion.1
  369.8 9.8 %reshape.626 = bf16[8,4,24,4,768]{4,3,2,1,0:T(4,128)(2,1)} reshape(bf16[768,3072]{1,0:T(8,128)(2,1)} %convolution_convert_fusion.1) | data formatting | bytes 9437184 | tf_op jit(solution)/shard_map/reshape | solution.py:1172
  379.6 3.4 copy.55
  383.6 4.0 pad_maximum_fusion.1
  389.0 7.4 multiply_reduce_fusion
  398.6 11.6 %all_to_all.48.go_ref = bf16[4,192,512]{2,1,0:T(8,128)(2,1)} all-to-all(bf16[4,192,512]{2,1,0:T(8,128)(2,1)S(1)} %bitcast.268), channel_id=1, replica_groups={{0,1,2,3},{4,5,6,7},{8,9,10,11},{12,13,14,15},{16,17,18,19},{20,21,22,2..., dimensions={0} | all-to-all | bytes 1572864 | tf_op jit(solution)/shard_map/all_to_all | solution.py:542
  410.2 27.4 %attend_back.2 = bf16[4,576,512]{2,1,0:T(8,128)(2,1)} custom-call(s32[8]{0:T(128)} %get-tuple-element.93.lo_ref, s32[8]{0:T(128)} %get-tuple-element.92.hi_ref, bf16[4,576,512]{2,1,0:T(8,128)(2,1)} %get-tuple-element.45.x_ref, bf16[4,192,512]{2,1,0:T(8,128)(2,1)} %all_to_all.48.go_ref, f32[4,192,512]{2,1,0:T(8,128)} %get-tuple-element.50.out_ref, ...), custom_call_target="tpu_custom_call" | custom-call | tf_op jit(solution)/shard_map/attend_back/pallas_call | solution.py:731
  437.7 3.8 all-to-all-start.3
  441.9 2.2 convolution_convert_fusion.6
  444.2 46.0 %all-to-all-done.3 = bf16[4,576,512]{2,1,0:T(8,128)(2,1)S(1)} async-done(((bf16[4,576,512]{2,1,0:T(8,128)(2,1)}), bf16[4,576,512]{2,1,0:T(8,128)(2,1)S(1)}, u32[]{:S(2)}, u32[]{:S(2)}) %all-to-all-start.3) | async-done | bytes 2359328 | tf_op jit(solution)/shard_map/all_to_all | solution.py:542
  492.4 4.1 convolution_convert_fusion.3
  496.4 8.7 %reshape.618 = bf16[8,4,24,3,768]{4,3,2,1,0:T(4,128)(2,1)} reshape(bf16[768,2304]{1,0:T(8,128)(2,1)} %convolution_convert_fusion.3) | data formatting | bytes 7077888 | tf_op jit(solution)/shard_map/reshape | solution.py:1172
  505.2 5.3 copy.52
  510.6 6.1 multiply_reduce_fusion.1
  517.9 5.3 convert_reduce_fusion.1
  523.2 1.7 copy-done.88
  524.9 4.8 convolution_convert_fusion.2
  529.7 9.8 %reshape.622 = bf16[8,4,24,4,768]{4,3,2,1,0:T(4,128)(2,1)} reshape(bf16[768,3072]{1,0:T(8,128)(2,1)} %convolution_convert_fusion.2) | data formatting | bytes 9437184 | tf_op jit(solution)/shard_map/reshape | solution.py:1172
  539.5 3.4 copy.54
  543.0 4.1 pad_maximum_fusion
  547.7 7.3 multiply_reduce_fusion.2
  557.2 12.0 %all_to_all.49.go_ref = bf16[4,192,512]{2,1,0:T(8,128)(2,1)} all-to-all(bf16[4,192,512]{2,1,0:T(8,128)(2,1)S(1)} %bitcast.269), channel_id=1, replica_groups={{0,1,2,3},{4,5,6,7},{8,9,10,11},{12,13,14,15},{16,17,18,19},{20,21,22,2..., dimensions={0} | all-to-all | bytes 1572864 | tf_op jit(solution)/shard_map/all_to_all | solution.py:542
  569.2 27.4 %attend_back.3 = bf16[4,576,512]{2,1,0:T(8,128)(2,1)} custom-call(s32[8]{0:T(128)} %get-tuple-element.93.lo_ref, s32[8]{0:T(128)} %get-tuple-element.92.hi_ref, bf16[4,576,512]{2,1,0:T(8,128)(2,1)} %get-tuple-element.39.x_ref, bf16[4,192,512]{2,1,0:T(8,128)(2,1)} %all_to_all.49.go_ref, f32[4,192,512]{2,1,0:T(8,128)} %get-tuple-element.52.out_ref, ...), custom_call_target="tpu_custom_call" | custom-call | tf_op jit(solution)/shard_map/attend_back/pallas_call | solution.py:731
  596.6 4.5 all-to-all-start.5
  602.6 9.7 %collective-permute-start.2 = (bf16[256,768]{1,0:T(8,128)(2,1)S(1)}, bf16[256,768]{1,0:T(8,128)(2,1)S(1)}, u32[]{:S(2)}, u32[]{:S(2)}) collective-permute-start(bf16[256,768]{1,0:T(8,128)(2,1)S(1)} %select_convert_fusion.1), channel_id=1, source_target_pairs={{0,4},{1,5},{2,6},{3,7},{4,0},{5,1},{6,2},{7,3},{8,12},{9,13},{10,... | collective-permute-start | bytes 1179656 | tf_op jit(solution)/shard_map/ppermute | solution.py:512
  612.5 44.1 %collective-permute-done.2 = bf16[256,768]{1,0:T(8,128)(2,1)S(1)} collective-permute-done((bf16[256,768]{1,0:T(8,128)(2,1)S(1)}, bf16[256,768]{1,0:T(8,128)(2,1)S(1)}, u32[]{:S(2)}, u32[]{:S(2)}) %collective-permute-start.2) | collective-permute-done | bytes 393248 | tf_op jit(solution)/shard_map/ppermute | solution.py:512
  656.6 1.5 fusion.25
  660.5 3.4 convolution_convert_fusion.7
  663.9 6.8 convolution_convert_fusion.4
  670.7 3.4 copy.51
  674.1 2.3 convert_reduce_fusion.3
  676.5 4.8 convolution_add_fusion
  682.1 3.3 collective-permute-start.4
  687.0 5.6 convolution_convert_fusion.5
  692.5 92.1 %reduce.78 = (f32[96,2304]{1,0:T(8,128)}, f32[96,768]{1,0:T(8,128)}, f32[384,768]{1,0:T(8,128)}, f32[48,768]{1,0:T(8,128)}) custom-call(bf16[8,4,24,2304]{3,2,1,0:T(8,128)(2,1)} %bitcast.243, bf16[8,4,24,768]{3,2,1,0:T(8,128)(2,1)} %bitcast.233, bf16[8,4,96,768]{3,2,1,0:T(8,128)(2,1)} %bitcast.236, f32[48,768]{1,0:T(8,128)} %pad.9.small), custom_call_target="tpu_custom_call" | custom-call | tf_op jit(solution)/shard_map/reduce/pallas_call | solution.py:1144
  797.9 10.2 %collective-permute-done.8 = bf16[2,192,768]{2,1,0:T(8,128)(2,1)S(1)} collective-permute-done((bf16[2,192,768]{2,1,0:T(8,128)(2,1)S(1)}, bf16[2,192,768]{2,1,0:T(8,128)(2,1)S(1)}, u32[]{:S(2)}, u32[]{:S(2)}) %collective-permute-start.8) | collective-permute-done | bytes 589856 | tf_op jit(solution)/shard_map/ppermute | solution.py:512
  810.4 1.6 pad_maximum_fusion.4
  812.0 12.0 %collective-permute-done.6 = bf16[2,192,768]{2,1,0:T(8,128)(2,1)S(1)} collective-permute-done((bf16[2,192,768]{2,1,0:T(8,128)(2,1)S(1)}, bf16[2,192,768]{2,1,0:T(8,128)(2,1)S(1)}, u32[]{:S(2)}, u32[]{:S(2)}) %collective-permute-start.6) | collective-permute-done | bytes 589856 | tf_op jit(solution)/shard_map/ppermute | solution.py:512
  827.5 1.7 maximum_convert_fusion
  (376 shorter events, 66.4 us)
Async XLA Ops:
  7.2 7.2 copy-start.26
  7.2 8.2 copy-start.75
  7.2 8.2 copy-start.74
  7.2 8.2 copy-start.77
  7.2 8.2 copy-start.76
  7.2 8.2 copy-start.79
  7.2 8.2 copy-start.78
  7.3 8.2 copy-start.81
  7.3 8.2 copy-start.80
  7.3 8.2 copy-start.63
  8.5 48.5 %copy-start.22 = (bf16[2,96,3072]{2,1,0:T(8,128)(2,1)S(1)}, bf16[2,96,3072]{2,1,0:T(8,128)(2,1)}, u32[]{:S(2)}) copy-start(bf16[2,96,3072]{2,1,0:T(8,128)(2,1)} %param.30) | copy-start | bytes 3538948
  8.5 53.9 %collective-permute-start = (bf16[256,768]{1,0:T(8,128)(2,1)S(1)}, bf16[256,768]{1,0:T(8,128)(2,1)S(1)}, u32[]{:S(2)}, u32[]{:S(2)}) collective-permute-start(bf16[256,768]{1,0:T(8,128)(2,1)S(1)} %select_bitcast_fusion.5), channel_id=1, source_target_pairs={{0,4},{1,5},{2,6},{3,7},{4,0},{5,1},{6,2},{7,3},{8,12},{9,13},{10,... | collective-permute-start | bytes 1179656 | tf_op jit(solution)/shard_map/ppermute | solution.py:512
  13.4 49.0 %collective-permute-start.1 = (s32[256,1]{0,1:T(1,128)S(1)}, s32[256,1]{0,1:T(1,128)S(1)}, u32[]{:S(2)}, u32[]{:S(2)}) collective-permute-start(s32[256,1]{0,1:T(1,128)S(1)} %fusion.44), channel_id=1, source_target_pairs={{0,4},{1,5},{2,6},{3,7},{4,0},{5,1},{6,2},{7,3},{8,12},{9,13},{10,... | collective-permute-start | bytes 3080 | tf_op jit(solution)/shard_map/ppermute | solution.py:512
  61.1 98.1 %copy-start.32 = (s32[1,2048]{1,0:T(1,128)}, s32[1,2048]{1,0:T(1,128)S(1)}, u32[]{:S(2)}) copy-start(s32[1,2048]{1,0:T(1,128)S(1)} %get-tuple-element.103) | copy-start | bytes 24580
  183.6 15.5 %all-to-all-start = ((bf16[4,192,512]{2,1,0:T(8,128)(2,1)}), bf16[4,192,512]{2,1,0:T(8,128)(2,1)S(1)}, u32[]{:S(2)}, u32[]{:S(2)}) async-start(bf16[4,192,512]{2,1,0:T(8,128)(2,1)} %get-tuple-element.40), calls=%async_computation | async-start | bytes 1572864 | tf_op jit(solution)/shard_map/all_to_all | solution.py:542
  187.4 21.9 %copy-start.45 = (f32[768]{0:T(1024)}, f32[768]{0:T(1024)S(1)}, u32[]{:S(2)}) copy-start(f32[768]{0:T(1024)S(1)} %mul.258) | copy-start | bytes 9220
  187.5 21.8 %copy-start.68 = (f32[768]{0:T(1024)}, f32[768]{0:T(1024)S(1)}, u32[]{:S(2)}) copy-start(f32[768]{0:T(1024)S(1)} %add.237) | copy-start | bytes 9220
  187.6 14.3 %copy-start.53 = (f32[3072]{0:T(1024)}, f32[3072]{0:T(1024)S(1)}, u32[]{:S(2)}) copy-start(f32[3072]{0:T(1024)S(1)} %add.240) | copy-start | bytes 36868
  187.7 24.8 %copy-start.48 = (f32[768]{0:T(1024)}, f32[768]{0:T(1024)S(1)}, u32[]{:S(2)}) copy-start(f32[768]{0:T(1024)S(1)} %mul.267) | copy-start | bytes 9220
  187.8 24.7 %copy-start.70 = (f32[768]{0:T(1024)}, f32[768]{0:T(1024)S(1)}, u32[]{:S(2)}) copy-start(f32[768]{0:T(1024)S(1)} %add.249) | copy-start | bytes 9220
  201.6 7.8 copy-start.5
  201.6 7.8 copy-start.34
  201.6 7.8 slice-start.2
  201.9 7.4 copy-start.56
  201.9 7.4 slice-start.3
  212.1 125.3 %copy-start.8 = (f32[512,768]{1,0:T(8,128)}, f32[512,768]{1,0:T(8,128)S(1)}, u32[]{:S(2)}) copy-start(f32[512,768]{1,0:T(8,128)S(1)} %get-tuple-element.206) | copy-start | bytes 4718596
  309.3 28.1 %all-to-all-start.1 = ((bf16[4,192,512]{2,1,0:T(8,128)(2,1)}), bf16[4,192,512]{2,1,0:T(8,128)(2,1)S(1)}, u32[]{:S(2)}, u32[]{:S(2)}) async-start(bf16[4,192,512]{2,1,0:T(8,128)(2,1)} %get-tuple-element.46), calls=%async_computation.1 | async-start | bytes 1572864 | tf_op jit(solution)/shard_map/all_to_all | solution.py:542
  312.9 476.3 %reduce-scatter.5.cloned.1.call-start = ((), (), s32[]{:S(2)}) async-start(), calls=%async_computation.9 | async-start | bytes 9732096 | tf_op jit(solution)/shard_map/reduce_scatter | solution.py:1179
  314.2 21.1 %collective-permute-start.3 = (bf16[256,768]{1,0:T(8,128)(2,1)}, bf16[256,768]{1,0:T(8,128)(2,1)S(1)}, u32[]{:S(2)}, u32[]{:S(2)}) collective-permute-start(bf16[256,768]{1,0:T(8,128)(2,1)} %select_bitcast_fusion.4), channel_id=1, source_target_pairs={{0,4},{1,5},{2,6},{3,7},{4,0},{5,1},{6,2},{7,3},{8,12},{9,13},{10,... | collective-permute-start | bytes 1179656 | tf_op jit(solution)/shard_map/ppermute | solution.py:512
  323.5 13.9 %copy-start.73 = (f32[768]{0:T(1024)S(1)}, f32[768]{0:T(1024)}, u32[]{:S(2)}) copy-start(f32[768]{0:T(1024)} %add.258) | copy-start | bytes 9220
  339.8 23.5 %copy-start.11 = (f32[512,768]{1,0:T(8,128)}, f32[512,768]{1,0:T(8,128)S(1)}, u32[]{:S(2)}) copy-start(f32[512,768]{1,0:T(8,128)S(1)} %get-tuple-element.208) | copy-start | bytes 4718596
  339.9 7.2 slice-start.6
  340.6 6.5 slice-start.7
  369.8 13.2 %slice-start = ((s8[4718592]{0:T(1024)(128)(4,1)}), s8[524288]{0:T(1024)(128)(4,1)S(1)}, s32[]{:S(2)}) async-start(s8[4718592]{0:T(1024)(128)(4,1)} %bitcast.237), calls=%async_computation.10 | async-start | bytes 1048576
  437.7 52.6 %all-to-all-start.3 = ((bf16[4,576,512]{2,1,0:T(8,128)(2,1)}), bf16[4,576,512]{2,1,0:T(8,128)(2,1)S(1)}, u32[]{:S(2)}, u32[]{:S(2)}) async-start(bf16[4,576,512]{2,1,0:T(8,128)(2,1)} %attend_back.2), calls=%async_computation.3 | async-start | bytes 4718592 | tf_op jit(solution)/shard_map/all_to_all | solution.py:542
  441.5 356.1 %reduce-scatter.3.cloned.1.call-start = ((), (), s32[]{:S(2)}) async-start(), calls=%async_computation.8 | async-start | bytes 9732096 | tf_op jit(solution)/shard_map/reduce_scatter | solution.py:1179
  505.2 5.4 copy-start.50
  505.2 5.4 copy-start.61
  505.2 12.6 %slice-start.4 = ((s8[4718592]{0:T(1024)(128)(4,1)}), s8[4194304]{0:T(1024)(128)(4,1)S(1)}, s32[]{:S(2)}) async-start(s8[4718592]{0:T(1024)(128)(4,1)} %bitcast.304), calls=%async_computation.14 | async-start | bytes 8388608
  505.2 12.6 %slice-start.8 = ((s8[6291456]{0:T(1024)(128)(4,1)}), s8[4194304]{0:T(1024)(128)(4,1)S(1)}, s32[]{:S(2)}) async-start(s8[6291456]{0:T(1024)(128)(4,1)} %bitcast.321), calls=%async_computation.18 | async-start | bytes 8388608
  510.6 7.2 slice-start.5
  510.6 7.2 slice-start.9
  517.8 5.4 copy-start.19
  517.8 7.0 copy-start.6
  517.8 7.0 copy-start.35
  517.8 7.0 copy-start.46
  517.9 7.0 copy-start.57
  517.9 7.0 copy-start.69
  547.7 7.4 copy-start.7
  596.6 15.8 %copy-start.40 = (f32[768]{0:T(1024)S(1)}, f32[768]{0:T(1024)}, u32[]{:S(2)}) copy-start(f32[768]{0:T(1024)} %get-tuple-element.72) | copy-start | bytes 9220
  596.6 15.8 %copy-start.44 = (f32[768]{0:T(1024)S(1)}, f32[768]{0:T(1024)}, u32[]{:S(2)}) copy-start(f32[768]{0:T(1024)} %get-tuple-element.96) | copy-start | bytes 9220
  596.6 15.8 %copy-start.67 = (f32[768]{0:T(1024)S(1)}, f32[768]{0:T(1024)}, u32[]{:S(2)}) copy-start(f32[768]{0:T(1024)} %get-tuple-element.58) | copy-start | bytes 9220
  596.6 15.8 %copy-start.66 = (f32[768]{0:T(1024)S(1)}, f32[768]{0:T(1024)}, u32[]{:S(2)}) copy-start(f32[768]{0:T(1024)} %get-tuple-element.69) | copy-start | bytes 9220
  596.6 15.9 %copy-start.42 = (f32[768]{0:T(1024)S(1)}, f32[768]{0:T(1024)}, u32[]{:S(2)}) copy-start(f32[768]{0:T(1024)} %get-tuple-element.94) | copy-start | bytes 9220
  596.6 15.9 %copy-start.41 = (f32[768]{0:T(1024)S(1)}, f32[768]{0:T(1024)}, u32[]{:S(2)}) copy-start(f32[768]{0:T(1024)} %get-tuple-element.64) | copy-start | bytes 9220
  596.6 74.1 %all-to-all-start.5 = ((bf16[4,576,512]{2,1,0:T(8,128)(2,1)}), bf16[4,576,512]{2,1,0:T(8,128)(2,1)}, u32[]{:S(2)}, u32[]{:S(2)}) async-start(bf16[4,576,512]{2,1,0:T(8,128)(2,1)} %attend_back.3), calls=%async_computation.5 | async-start | bytes 4718592 | tf_op jit(solution)/shard_map/all_to_all | solution.py:542
  602.6 54.0 %collective-permute-start.2 = (bf16[256,768]{1,0:T(8,128)(2,1)S(1)}, bf16[256,768]{1,0:T(8,128)(2,1)S(1)}, u32[]{:S(2)}, u32[]{:S(2)}) collective-permute-start(bf16[256,768]{1,0:T(8,128)(2,1)S(1)} %select_convert_fusion.1), channel_id=1, source_target_pairs={{0,4},{1,5},{2,6},{3,7},{4,0},{5,1},{6,2},{7,3},{8,12},{9,13},{10,... | collective-permute-start | bytes 1179656 | tf_op jit(solution)/shard_map/ppermute | solution.py:512
  676.5 8.9 %copy-start.39 = (s32[1,2,2,128]{3,1,2,0:T(2,128)S(1)}, s32[1,2,2,128]{3,1,2,0:T(2,128)}, u32[]{:S(2)}) copy-start(s32[1,2,2,128]{3,1,2,0:T(2,128)} %copy-done.38) | copy-start | bytes 6148
  681.3 5.7 copy-start.28
  682.1 113.0 %collective-permute-start.4 = (bf16[256,768]{1,0:T(8,128)(2,1)}, bf16[256,768]{1,0:T(8,128)(2,1)}, u32[]{:S(2)}, u32[]{:S(2)}) collective-permute-start(bf16[256,768]{1,0:T(8,128)(2,1)} %select_convert_fusion), channel_id=1, source_target_pairs={{0,4},{1,5},{2,6},{3,7},{4,0},{5,1},{6,2},{7,3},{8,12},{9,13},{10,... | collective-permute-start | bytes 1179656 | tf_op jit(solution)/shard_map/ppermute | solution.py:512
  789.2 2.1 collective-permute-start.7
  792.4 15.7 %collective-permute-start.8 = (bf16[2,192,768]{2,1,0:T(8,128)(2,1)S(1)}, bf16[2,192,768]{2,1,0:T(8,128)(2,1)S(1)}, u32[]{:S(2)}, u32[]{:S(2)}) collective-permute-start(bf16[2,192,768]{2,1,0:T(8,128)(2,1)S(1)} %pad_maximum_fusion.14), channel_id=1, source_target_pairs={{0,16},{8,24},{16,0},{24,8},{1,17},{9,25},{17,1},{25,9},{2,18},{10... | collective-permute-start | bytes 1769480 | tf_op jit(solution)/shard_map/ppermute | solution.py:512
  797.5 10.8 %collective-permute-start.5 = (bf16[192,768]{1,0:T(8,128)(2,1)}, bf16[192,768]{1,0:T(8,128)(2,1)S(1)}, u32[]{:S(2)}, u32[]{:S(2)}) collective-permute-start(bf16[192,768]{1,0:T(8,128)(2,1)} %reduce-scatter.3.cloned.1.call-done), channel_id=1, source_target_pairs={{0,8},{8,0},{16,24},{24,16},{1,9},{9,1},{17,25},{25,17},{2,10},{10... | collective-permute-start | bytes 884744 | tf_op jit(solution)/shard_map/ppermute | solution.py:512
  809.2 14.8 %collective-permute-start.6 = (bf16[2,192,768]{2,1,0:T(8,128)(2,1)S(1)}, bf16[2,192,768]{2,1,0:T(8,128)(2,1)S(1)}, u32[]{:S(2)}, u32[]{:S(2)}) collective-permute-start(bf16[2,192,768]{2,1,0:T(8,128)(2,1)S(1)} %pad_maximum_fusion.12), channel_id=1, source_target_pairs={{0,16},{8,24},{16,0},{24,8},{1,17},{9,25},{17,1},{25,9},{2,18},{10... | collective-permute-start | bytes 1769480 | tf_op jit(solution)/shard_map/ppermute | solution.py:512
  (50 other events, 110.7 us)
Sparse Core Ops, SparseCore 0:
  387.7 158.9 reduce-scatter.4
  552.6 164.9 reduce-scatter.2

commit v4 on v3

--- a/solution.py
+++ b/solution.py
@@ -793,7 +793,7 @@
     )
 
 
-def fast_backward(grad, weights, vecs, saved, spans, seg_col, seg_row):
+def fast_backward(grad, weights, vecs, saved, spans, seg_col, seg_row, give_back):
     query_b, value_b, proj_b, attn_g, attn_s, down_b, ffn_g, ffn_s, up_b = vecs
     qkv_w, proj_w, up_w, down_w = weights
     (
@@ -815,7 +815,7 @@
     grad_context = mm(proj_w, grad_attn, 1, 1).astype(BF16)
     proj_grad = mm(context, grad_attn, 1, 0).astype(BF16)
     grad_out = swap(grad_context.reshape(GROUP, width // GROUP, grad_context.shape[1]))
-    moved = swap(attend_back(qkv, grad_out, out, lse, spans, seg_col, seg_row))
+    moved = give_back(attend_back(qkv, grad_out, out, lse, spans, seg_col, seg_row))
     share = width // GROUP
     mixed = jnp.transpose(moved.reshape(GROUP, 3, share, moved.shape[2]), (1, 0, 2, 3))
     mixed = mixed.reshape(3 * width, moved.shape[2])
@@ -984,36 +984,35 @@
     return [item.reshape(-1, item.shape[3]) for item in fulls[:wide]] + list(fulls[wide:])
 
 
-def reduce_kernel(
-    qkv_grad, proj_grad, down_grad, small, qkv_out, proj_out, down_out, small_out, *scratch
-):
-    kinds = 2
-    mats, core_mats, x_mats, y_mats, z_mats, x_stage, y_stage, z_stage, all_mats = [
+def reduce_kernel(x_first, smalls, swaps, *refs):
+    kinds = len(x_first)
+    total = kinds + smalls + swaps
+    grads, extra = (refs[:kinds], refs[kinds:total])
+    outs, extra_out = (refs[total : total + kinds], refs[total + kinds : 2 * total])
+    scratch = refs[2 * total :]
+    mats, cores, ones, twos, threes, stage_one, stage_two, stage_three, alls = [
         scratch[kinds * n : kinds * n + kinds] for n in range(9)
     ]
     (
-        small_sum, small_got, local_sems, send_sems, core_sems, x_sems, y_sems, z_sems, all_sems, small_sems,
+        small_sum, small_got, local_sems, send_sems, core_sems, one_sems, two_sems, three_sems, all_sems,
+        small_sems, swap_sems,
     ) = scratch[9 * kinds :]
     rep, shard, core, y, across_x, across_core, zs = places()
     x = lax.div(rep, 2)
+    member = lax.rem(shard, GROUP)
     beside, past_x, past_core = ((rep, 2 * zs[0] + 1 - y), (across_x, shard), (across_core, shard))
-    cut = qkv_grad.shape[3]
-    local = [
-        pltpu.make_async_copy(qkv_grad, mats[0].at[:, :, :, :cut], local_sems.at[0]),
-        pltpu.make_async_copy(proj_grad, mats[0].at[:, :, :, cut:], local_sems.at[1]),
-        pltpu.make_async_copy(down_grad, mats[1], local_sems.at[2]),
-    ]
+    local = [pltpu.make_async_copy(grads[n], mats[n], local_sems.at[n]) for n in range(kinds)]
     for copy in local:
         copy.start()
-    small_sum[0] = small[...]
-    greet()
+    greet(swaps > 0)
     sends = Sends(send_sems)
 
     def arrive(ref, sem):
         pltpu.make_async_copy(ref, ref, sem).wait()
 
-    def chunk_of(k, far):
-        return 2 * zs[k] + (1 - y if far else y)
+    def mat(n, k, fy, fx, side=0):
+        chunk = 2 * zs[k] + (1 - y if fy else y)
+        return mats[n].at[chunk, 2 * (1 - x if fx else x) + (1 - core if side else core)]
 
     def add(target, parts):
         steps = 6
@@ -1035,161 +1034,157 @@
         sends.push(small_sum.at[step], small_got.at[step], small_sems.at[step], small_partners[step])
 
     def small_step(step):
+        if not smalls:
+            return
         arrive(small_got.at[step], small_sems.at[step])
         small_sum[step + 1] = small_sum[step] + small_got[step]
         if step + 1 < len(small_partners):
             small_send(step + 1)
-
-    small_send(0)
-    far = [(k, 1) for k in (2, 3, 1, 0)]
-    near = [(k, 0) for k in (2, 3, 1)]
-    own = (0, 0)
+        else:
+            extra_out[0][...] = small_sum[step + 1]
+
+    if smalls:
+        small_sum[0] = extra[0][...]
+        small_send(0)
+    order = (2, 3, 1, 0)
     for copy in local:
         copy.wait()
-    for place in far + near + [own]:
-        chunk = chunk_of(*place)
+    for fy in (1, 0):
+        for k in order:
+            for n in range(kinds):
+                for fx in (1, 0):
+                    sends.push(
+                        mat(n, k, fy, fx, 1), cores[n].at[k, fy, fx], core_sems.at[n, k, fy, fx], past_core
+                    )
+
+    def cored(n, k, fy, fx):
+        arrive(cores[n].at[k, fy, fx], core_sems.at[n, k, fy, fx])
+        return [mat(n, k, fy, fx), cores[n].at[k, fy, fx]]
+
+    def oned(n, k, fy, fx):
+        flag = fy if x_first[n] else fx
+        arrive(ones[n].at[k, flag], one_sems.at[n, k, flag])
+        return cored(n, k, fy, fx) + [ones[n].at[k, flag]]
+
+    def step_one(slot, k, flag):
         for n in range(kinds):
-            for which in (1 - x, x):
-                sends.push(
-                    mats[n].at[chunk, 2 * which + 1 - core],
-                    core_mats[n].at[chunk, which],
-                    core_sems.at[n, chunk, which],
-                    past_core,
-                )
-
-    def step_x(slot, place):
-        chunk = chunk_of(*place)
+            stage = stage_one[n].at[slot]
+            add(stage, cored(n, k, flag, 1) if x_first[n] else cored(n, k, 1, flag))
+            sends.push(
+                stage, ones[n].at[k, flag], one_sems.at[n, k, flag], past_x if x_first[n] else beside
+            )
+
+    def step_two(k):
         for n in range(kinds):
-            arrive(core_mats[n].at[chunk, 1 - x], core_sems.at[n, chunk, 1 - x])
-            add(x_stage[n].at[slot], [mats[n].at[chunk, across_x], core_mats[n].at[chunk, 1 - x]])
-            sends.push(x_stage[n].at[slot], x_mats[n].at[chunk], x_sems.at[n, chunk], past_x)
-
-    def parts_of(n, chunk):
-        arrive(core_mats[n].at[chunk, x], core_sems.at[n, chunk, x])
-        arrive(x_mats[n].at[chunk], x_sems.at[n, chunk])
-        return [mats[n].at[chunk, rep], core_mats[n].at[chunk, x], x_mats[n].at[chunk]]
-
-    def step_y(place):
-        k = place[0]
+            stage = stage_two[n].at[k]
+            add(stage, oned(n, k, 1, 0) if x_first[n] else oned(n, k, 0, 1))
+            sends.push(stage, twos[n].at[k], two_sems.at[n, k], beside if x_first[n] else past_x)
+
+    def twod(n, k):
+        parts = oned(n, k, 0, 0)
+        arrive(twos[n].at[k], two_sems.at[n, k])
+        return parts + [twos[n].at[k]]
+
+    def step_three(k):
         for n in range(kinds):
-            add(y_stage[n].at[k], parts_of(n, chunk_of(*place)))
-            sends.push(y_stage[n].at[k], y_mats[n].at[k], y_sems.at[n, k], beside)
-
-    def step_z(place):
-        k = place[0]
-        for n in range(kinds):
-            parts = parts_of(n, chunk_of(*place))
-            arrive(y_mats[n].at[k], y_sems.at[n, k])
-            add(z_stage[n].at[k - 1], parts + [y_mats[n].at[k]])
+            stage = stage_three[n].at[k - 1]
+            add(stage, twod(n, k))
+            sends.push(stage, threes[n].at[k - 1], three_sems.at[n, k - 1], (rep, 2 * zs[k] + y))
+
+    step_one(0, 2, 1)
+    near_members = ((1, y), (0, 1 - y), (1, 1 - y))
+    for n in range(swaps):
+        for k, other in near_members:
+            target = 2 * zs[k] + other
             sends.push(
-                z_stage[n].at[k - 1], z_mats[n].at[k - 1], z_sems.at[n, k - 1], (rep, 2 * zs[k] + y)
+                extra[smalls + n].at[lax.rem(target, GROUP)],
+                extra_out[smalls + n].at[member],
+                swap_sems.at[n, member],
+                (rep, target),
             )
-
-    step_x(0, far[0])
-    step_x(1, far[1])
-    step_x(2, far[2])
+    own_swaps = [
+        pltpu.make_async_copy(
+            extra[smalls + n].at[member], extra_out[smalls + n].at[member], local_sems.at[kinds + n]
+        )
+        for n in range(swaps)
+    ]
+    for copy in own_swaps:
+        copy.start()
+    step_one(1, 3, 1)
+    step_one(2, 1, 1)
     small_step(0)
-    step_y(far[0])
-    step_x(3, far[3])
-    step_y(far[1])
-    step_x(4, near[0])
+    step_two(2)
+    step_one(3, 0, 1)
+    step_two(3)
+    step_one(4, 2, 0)
     small_step(1)
-    step_y(far[2])
-    step_x(5, near[1])
-    step_y(far[3])
-    step_x(6, near[2])
+    step_two(1)
+    step_one(5, 3, 0)
+    step_two(0)
+    step_one(6, 1, 0)
     small_step(2)
-    step_z(near[0])
-    step_x(7, own)
-    step_z(near[1])
+    step_three(2)
+    step_one(7, 0, 0)
+    step_three(3)
     small_step(3)
-    step_z(near[2])
+    step_three(1)
     small_step(4)
-    small_out[...] = small_sum[len(small_partners)]
 
     for n in range(kinds):
-        parts = parts_of(n, shard)
-        arrive(y_mats[n].at[0], y_sems.at[n, 0])
+        parts = twod(n, 0)
         for k in range(3):
-            arrive(z_mats[n].at[k], z_sems.at[n, k])
-        mine = all_mats[n].at[rep]
-        add(mine, parts + [y_mats[n].at[0]] + [z_mats[n].at[k] for k in range(3)])
+            arrive(threes[n].at[k], three_sems.at[n, k])
+        mine = alls[n].at[rep]
+        add(mine, parts + [threes[n].at[k] for k in range(3)])
         sends.push(mine, mine, all_sems.at[n, rep], past_x)
         sends.push(mine, mine, all_sems.at[n, rep], past_core)
     for n in range(kinds):
-        theirs = all_mats[n].at[across_x]
+        theirs = alls[n].at[across_x]
         arrive(theirs, all_sems.at[n, across_x])
         sends.push(theirs, theirs, all_sems.at[n, across_x], past_core)
     opposite = lax.rem(across_core + 2, 4)
     for n in range(kinds):
-        arrive(all_mats[n].at[across_core], all_sems.at[n, across_core])
-        arrive(all_mats[n].at[opposite], all_sems.at[n, opposite])
-    rows = mats[0].shape[2]
-    tall = mats[1].shape[2]
-    for q in range(4):
-        qkv_out[q * rows : (q + 1) * rows, :] = all_mats[0][q, :, :cut].astype(F32)
-        proj_out[q * rows : (q + 1) * rows, :] = all_mats[0][q, :, cut:].astype(F32)
-        down_out[q * tall : (q + 1) * tall, :] = all_mats[1][q].astype(F32)
+        arrive(alls[n].at[across_core], all_sems.at[n, across_core])
+        arrive(alls[n].at[opposite], all_sems.at[n, opposite])
+        rows = mats[n].shape[2]
+        for q in range(4):
+            outs[n][q * rows : (q + 1) * rows, :] = alls[n][q].astype(F32)
+    for n in range(swaps):
+        for k, other in near_members:
+            source = lax.rem(2 * zs[k] + other, GROUP)
+            arrive(extra_out[smalls + n].at[source], swap_sems.at[n, source])
+    for copy in own_swaps:
+        copy.wait()
     sends.finish()
 
 
-def reduce_fast(qkv_grad, proj_grad, down_grad, small):
-    rows, tall = (proj_grad.shape[0] // 32, down_grad.shape[0] // 32)
-    wide = qkv_grad.shape[1] + proj_grad.shape[1]
-    sizes = ((rows, wide), (tall, down_grad.shape[1]))
+def reduce_fast(grads, x_first, small, swapped, name, collective_id):
+    kinds = len(grads)
+    extra = small + swapped
+    sizes = [(item.shape[0] // 32, item.shape[1]) for item in grads]
     buffers = []
-    for lead in ((8, 4), (8, 2), (8,), (4,), (3,), (8,), (4,), (3,), (4,)):
+    for lead in ((8, 4), (4, 2, 2), (4, 2), (4,), (3,), (8,), (4,), (3,), (4,)):
         buffers += [pltpu.VMEM(lead + size, BF16) for size in sizes]
+    small_shape = small[0].shape if small else (8, 128)
     dma = pltpu.SemaphoreType.DMA
+    anywhere = pl.BlockSpec(memory_space=pl.ANY)
     return pl.pallas_call(
-        reduce_kernel,
-        name="reduce",
-        out_shape=(
-            jax.ShapeDtypeStruct((4 * rows, qkv_grad.shape[1]), F32),
-            jax.ShapeDtypeStruct((4 * rows, proj_grad.shape[1]), F32),
-            jax.ShapeDtypeStruct((4 * tall, down_grad.shape[1]), F32),
-            jax.ShapeDtypeStruct(small.shape, F32),
-        ),
-        in_specs=[pl.BlockSpec(memory_space=pl.ANY)] * 3 + in_vmem(1),
-        out_specs=in_vmem(4),
+        functools.partial(reduce_kernel, x_first, len(small), len(swapped)),
+        name=name,
+        out_shape=[jax.ShapeDtypeStruct((4 * size[0], size[1]), F32) for size in sizes]
+        + [jax.ShapeDtypeStruct(item.shape, item.dtype) for item in extra],
+        in_specs=[anywhere] * kinds + in_vmem(len(extra)),
+        out_specs=in_vmem(kinds + len(small)) + [anywhere] * len(swapped),
         scratch_shapes=buffers
         + [
-            pltpu.VMEM((6,) + small.shape, F32), pltpu.VMEM((5,) + small.shape, F32),
-            dma((3,)), dma((2 * 34 + 5,)), dma((2, 8, 2)), dma((2, 8)), dma((2, 4)), dma((2, 3)),
-            dma((2, 4)), dma((5,)),
+            pltpu.VMEM((6,) + small_shape, F32), pltpu.VMEM((5,) + small_shape, F32),
+            dma((kinds + 1,)), dma((34 * kinds + 8,)), dma((kinds, 4, 2, 2)), dma((kinds, 4, 2)),
+            dma((kinds, 4)), dma((kinds, 3)), dma((kinds, 4)), dma((5,)), dma((1, GROUP)),
         ],
         compiler_params=pltpu.CompilerParams(
-            collective_id=1, has_side_effects=True, vmem_limit_bytes=56 * 1024 * 1024
+            collective_id=collective_id, has_side_effects=True, vmem_limit_bytes=58 * 1024 * 1024
         ),
-    )(
-        qkv_grad.reshape(8, 4, rows, -1), proj_grad.reshape(8, 4, rows, -1),
-        down_grad.reshape(8, 4, tall, -1), small,
-    )
-
-
-def by_rep(grad, width):
-    blocks = grad.shape[1] // width
-    split = grad.reshape(8, 4, grad.shape[0] // 32, blocks, width)
-    return jnp.transpose(split, (1, 0, 3, 2, 4)).reshape(4, 8, grad.size // (32 * width), width)
-
-
-def scatter_all(grads, width):
-    packed = jnp.concatenate([by_rep(grad, width) for grad in grads], axis=2)
-    flat = packed.reshape(-1, width)
-    return lax.psum_scatter(flat, ("rep", "shard"), scatter_dimension=0, tiled=True)
-
-
-def spread_rep(piece):
-    rep = lax.axis_index("rep")
-    for bit in range(2):
-        other = exchange(piece, "rep", 1 << bit)
-        piece = ordered((rep >> bit) & 1 == 0, piece, other)
-    return piece.reshape((4,) + piece.shape[2:])
-
-
-def unpack(pieces, start, blocks, rows):
-    parts = [pieces[:, start + b * rows : start + (b + 1) * rows] for b in range(blocks)]
-    return jnp.concatenate([part.reshape(-1, part.shape[2]) for part in parts], axis=1).astype(F32)
+    )(*[item.reshape((8, 4) + size) for item, size in zip(grads, sizes)], *extra)
 
 
 def on_device_fast(
@@ -1266,14 +1261,19 @@
 
     grad = to_groups(cotangent, index).astype(F32)
     sums, shares = ([None] * LAYERS, [None] * LAYERS)
+    found = []
+
+    def sum_second(grad_qkv):
+        parts = reduce_fast(found[0], (1, 1, 1, 1), [], [grad_qkv], "reduce_second", 4)
+        shares[1] = parts[:4]
+        return parts[4]
+
     for layer in range(LAYERS - 1, -1, -1):
-        grad, (qkv_grad, proj_grad, up_grad, down_grad), sums[layer] = fast_backward(
-            grad, held[layer], vecs[layer], saved[layer], spans, seg_col, seg_row
+        grad, mat_grads, sums[layer] = fast_backward(
+            grad, held[layer], vecs[layer], saved[layer], spans, seg_col, seg_row,
+            swap if layer else sum_second,
         )
-        if layer:
-            early = scatter_all([up_grad, down_grad], width)
-            waiting = [qkv_grad, proj_grad]
-    late = scatter_all(waiting + [up_grad], width)
+        found.append(mat_grads)
     input_grad = from_groups(grad, index)
     memory_sum = lax.dot_general(
         slot_hot.astype(F32), grad, (((0,), (0,)), ((), ())), precision=lax.Precision.HIGHEST
@@ -1281,17 +1281,9 @@
     flat = jnp.concatenate([jnp.stack(sums[layer]) for layer in range(LAYERS)] + [memory_sum], axis=0)
     used = flat.shape[0]
     flat = jnp.pad(flat, ((0, -used % 8), (0, 0)))
-    qkv_own, proj_own, down_own, flat = reduce_fast(qkv_grad, proj_grad, down_grad, flat)
+    *first_shares, flat = reduce_fast(found[1], (0, 1, 1, 0), [flat], [], "reduce_first", 1)
+    shares[0] = first_shares
     flat = flat[:used]
-    rows, tall = (width // 32, width * ups // 32)
-    early, late = (spread_rep(early), spread_rep(late))
-    shares[1] = (
-        unpack(late, 0, 3, rows),
-        unpack(late, 3 * rows, 1, rows),
-        unpack(early, 0, ups, rows),
-        unpack(early, ups * rows, 1, tall),
-    )
-    shares[0] = (qkv_own, proj_own, unpack(late, 4 * rows, ups, rows), down_own)
     per = plain + ups
     own = lax.dynamic_slice_in_dim(flat, index * share, share, 1)
     vec_grads = [

time: 842 us -> 765 us (0.909)
  Pallas kernels: 392 us -> 512 us
  waiting for transfers between devices: 133 us -> 32.8 us
  local copies, waits for them, and re-layouts: 79.2 us -> 29.6 us
  other arithmetic: 49.7 us -> 33.5 us
  between operations: 16 us -> 2.67 us
  matrix products: 103 us -> 90.9 us
    pallas_call x1 -> x2, Pallas kernels: 92.1 us -> 213 us  [reduce_fast(): pl.pallas_call(functools.partial(reduce_kernel, x_first, len(small), len(...]
    ppermute x9 -> x5, waiting for transfers between devices: 75.9 us -> 20.4 us  [exchange(): return lax.ppermute(tensor, axis, [(i, i ^ mask) for i in range(count)])]
    all_to_all x4, waiting for transfers between devices: 57.1 us -> 12.4 us  [swap(): lax.all_to_all(flat, 'shard', 0, 0, axis_index_groups=[[0, 1, 2, 3], [4,...]
    reshape x7 -> x1, local copies, waits for them, and re-layouts: 35.6 us -> 1.97 us  [fast_backward(): moved.reshape(GROUP, 3, share, moved.shape[2])]
    dot_general x25, matrix products: 103 us -> 90.2 us  [mm(): lax.dot_general(left, right, (((left_dim,), (right_dim,)), ((), ())), pre...]
    ppermute x9 -> x5, starting transfers between devices: 23.2 us -> 15.3 us  [exchange(): return lax.ppermute(tensor, axis, [(i, i ^ mask) for i in range(count)])]
    all_to_all x2 -> x1, blocking collectives: 23.6 us -> 18.9 us  [swap(): lax.all_to_all(flat, 'shard', 0, 0, axis_index_groups=[[0, 1, 2, 3], [4,...]
  transfers between devices with their start and end apart: 15 -> 9, of which waited for: 7 -> 6; matrix products, arithmetic and copies ran while one was open for 17% -> 8% of each run, Pallas kernels for 22% -> 5%
where the time goes in v4:
time: 765 us; the launch traced here: 758 us
  Pallas kernels  512 us (67%)
  matrix products  90.9 us (12%)
  starting transfers between devices  37 us (5%)
  other arithmetic  33.5 us (4%)
  waiting for transfers between devices  32.8 us (4%)
  local copies, waits for them, and re-layouts  29.6 us (4%)
  blocking collectives  18.9 us (2%)
    pallas_call x2, Pallas kernels, reduce_fast(): pl.pallas_call(functools.partial(reduce_kernel, x_first, len(small), len(...  213 us
    pallas_call x3, Pallas kernels, gather_fast(): pl.pallas_call(functools.partial(gather_kernel, len(fourths), len(smalls)...  199 us
    dot_general x25, matrix products, mm(): lax.dot_general(left, right, (((left_dim,), (right_dim,)), ((), ())), pre...  90.2 us
    pallas_call x2, Pallas kernels, attend_back(): pl.pallas_call(attend_back_kernel, name='attend_back', out_shape=jax.Shap...  54.4 us
    pallas_call x2, Pallas kernels, attend(): pl.pallas_call(attend_kernel, name='attend', out_shape=(jax.ShapeDtypeStr...  46 us
    all_to_all x4, starting transfers between devices, swap(): lax.all_to_all(flat, 'shard', 0, 0, axis_index_groups=[[0, 1, 2, 3], [4,...  21.7 us
    ppermute x5, waiting for transfers between devices, exchange(): return lax.ppermute(tensor, axis, [(i, i ^ mask) for i in range(count)])  20.4 us
    all_to_all x1, blocking collectives, swap(): lax.all_to_all(flat, 'shard', 0, 0, axis_index_groups=[[0, 1, 2, 3], [4,...  18.9 us
  transfers between devices with their start and end apart: 9, of which 6 were waited for; matrix products, arithmetic and copies ran while one was open for 8% of the time, Pallas kernels for 5%

profile of v4, /device:TPU:0, one launch (start us, length us, event | category | flops | bytes accessed | tf_op | source)
XLA Modules:
  0.0 757.7 jit_solution(6823803326938191623)
XLA Ops:
  0.8 1.2 select_bitcast_fusion.1
  2.0 4.1 collective-permute-start
  9.7 39.0 %gather_first.1 = (bf16[8,4,24,2304]{3,2,1,0:T(8,128)(2,1)}, bf16[8,48,128]{2,1,0:T(8,128)(2,1)}) custom-call(bf16[4,24,2304]{2,1,0:T(8,128)(2,1)} %bitcast.206, bf16[48,128]{1,0:T(8,128)(2,1)} %pad.8.refs_1_), custom_call_target="tpu_custom_call" | custom-call | tf_op jit(solution)/shard_map/gather_first/pallas_call | solution.py:967
  51.5 1.1 fusion.64
  56.9 1.4 copy-done.66
  58.3 2.1 fusion.87
  60.8 1.6 pad_maximum_fusion.refs_4_
  62.4 90.3 %gather_middle.1 = (bf16[8,4,24,768]{3,2,1,0:T(8,128)(2,1)}, bf16[8,4,24,3072]{3,2,1,0:T(8,128)(2,1)}, bf16[8,4,24,2304]{3,2,1,0:T(8,128)(2,1)}, bf16[8,4,96,768]{3,2,1,0:T(8,128)(2,1)}, bf16[4,576,512]{2,1,0:T(8,128)(2,1)}) custom-call(bf16[4,24,768]{2,1,0:T(8,128)(2,1)} %bitcast.217, bf16[4,24,3072]{2,1,0:T(8,128)(2,1)} %bitcast.204, ...), custom_call_target="tpu_custom_call" | custom-call | tf_op jit(solution)/shard_map/gather_middle/pallas_call | solution.py:967
  152.7 1.3 broadcast_in_dim.2.seg_col
  154.1 23.0 %attend.2 = (bf16[4,192,512]{2,1,0:T(8,128)(2,1)}, f32[4,192,512]{2,1,0:T(8,128)}, f32[3,8,1,256]{3,2,1,0:T(1,128)}) custom-call(s32[8]{0:T(128)} %get-tuple-element.105.lo_ref, s32[8]{0:T(128)} %get-tuple-element.104.hi_ref, bf16[4,576,512]{2,1,0:T(8,128)(2,1)} %get-tuple-element.45.x_ref, s32[2048,128]{1,0:T(8,128)} %broadcast_in_dim.2.seg_col, ...), custom_call_target="tpu_custom_call" | custom-call | tf_op jit(solution)/shard_map/attend/pallas_call | solution.py:709
  177.0 3.7 all-to-all-start
  181.4 11.1 %all-to-all-done = bf16[4,192,512]{2,1,0:T(8,128)(2,1)S(1)} async-done(((bf16[4,192,512]{2,1,0:T(8,128)(2,1)}), bf16[4,192,512]{2,1,0:T(8,128)(2,1)S(1)}, u32[]{:S(2)}, u32[]{:S(2)}) %all-to-all-start) | async-done | bytes 786464 | tf_op jit(solution)/shard_map/all_to_all | solution.py:542
  192.5 2.5 fusion.83
  195.4 7.3 multiply_convert_fusion.3
  202.8 2.7 fusion.84
  205.9 2.3 fusion.57
  208.7 1.6 pad_maximum_fusion.1.refs_3_
  210.3 69.9 %gather_last.1 = (bf16[8,4,24,768]{3,2,1,0:T(8,128)(2,1)}, bf16[8,4,24,3072]{3,2,1,0:T(8,128)(2,1)}, bf16[8,4,96,768]{3,2,1,0:T(8,128)(2,1)}, bf16[4,576,512]{2,1,0:T(8,128)(2,1)}) custom-call(bf16[4,24,768]{2,1,0:T(8,128)(2,1)} %bitcast.216, bf16[4,24,3072]{2,1,0:T(8,128)(2,1)} %bitcast.202, bf16[4,96,768]{2,1,0:T(8,128)(2,1)} %bitcast.203, ...), custom_call_target="tpu_custom_call" | custom-call | tf_op jit(solution)/shard_map/gather_last/pallas_call | solution.py:967
  280.2 23.0 %attend.3 = (bf16[4,192,512]{2,1,0:T(8,128)(2,1)}, f32[4,192,512]{2,1,0:T(8,128)}, f32[3,8,1,256]{3,2,1,0:T(1,128)}) custom-call(s32[8]{0:T(128)} %get-tuple-element.105.lo_ref, s32[8]{0:T(128)} %get-tuple-element.104.hi_ref, bf16[4,576,512]{2,1,0:T(8,128)(2,1)} %get-tuple-element.51.x_ref, s32[2048,128]{1,0:T(8,128)} %broadcast_in_dim.2.seg_col, ...), custom_call_target="tpu_custom_call" | custom-call | tf_op jit(solution)/shard_map/attend/pallas_call | solution.py:709
  303.1 4.0 all-to-all-start.1
  308.0 4.0 collective-permute-start.3
  312.0 1.3 add.254
  313.4 1.3 mul.274
  314.7 1.3 add.259
  319.0 6.4 collective-permute-done.3
  325.3 1.2 fusion.31
  327.4 2.4 fusion.85
  330.5 6.5 multiply_convert_fusion.2
  337.0 2.8 fusion.86
  340.9 1.8 convert_reduce_fusion.5
  342.7 4.7 convert_reduce_fusion
  347.5 3.1 multiply_reduce_fusion
  352.8 18.9 %all_to_all.42.go_ref = bf16[4,192,512]{2,1,0:T(8,128)(2,1)} all-to-all(bf16[4,192,512]{2,1,0:T(8,128)(2,1)S(1)} %bitcast.215), channel_id=1, replica_groups={{0,1,2,3},{4,5,6,7},{8,9,10,11},{12,13,14,15},{16,17,18,19},{20,21,22,2..., dimensions={0} | all-to-all | bytes 1572864 | tf_op jit(solution)/shard_map/all_to_all | solution.py:542
  371.7 27.2 %attend_back.2 = bf16[4,576,512]{2,1,0:T(8,128)(2,1)} custom-call(s32[8]{0:T(128)} %get-tuple-element.105.lo_ref, s32[8]{0:T(128)} %get-tuple-element.104.hi_ref, bf16[4,576,512]{2,1,0:T(8,128)(2,1)} %get-tuple-element.51.x_ref, bf16[4,192,512]{2,1,0:T(8,128)(2,1)} %all_to_all.42.go_ref, f32[4,192,512]{2,1,0:T(8,128)} %get-tuple-element.56.out_ref, ...), custom_call_target="tpu_custom_call" | custom-call | tf_op jit(solution)/shard_map/attend_back/pallas_call | solution.py:731
  398.9 3.8 all-to-all-start.3
  402.7 1.4 select_convert_fusion.1
  404.1 7.0 collective-permute-start.2
  411.1 7.1 convolution_convert_fusion.3
  418.3 4.9 convolution_convert_fusion.4
  423.3 1.8 convolution_convert_fusion.7
  425.1 9.7 %collective-permute-done.2 = bf16[256,768]{1,0:T(8,128)(2,1)S(1)} collective-permute-done((bf16[256,768]{1,0:T(8,128)(2,1)S(1)}, bf16[256,768]{1,0:T(8,128)(2,1)S(1)}, u32[]{:S(2)}, u32[]{:S(2)}) %collective-permute-start.2) | collective-permute-done | bytes 393248 | tf_op jit(solution)/shard_map/ppermute | solution.py:512
  434.9 1.2 pad_maximum_fusion.5
  437.3 1.2 copy-done.4
  439.0 4.8 multiply_reduce_fusion.1
  443.9 4.2 convolution_convert_fusion.5
  449.3 4.9 convert_reduce_fusion.1
  454.4 3.1 multiply_reduce_fusion.2
  458.8 1.7 convolution_convert_fusion.8
  460.5 1.8 convolution_convert_fusion.6
  462.3 10.2 %all-to-all-start.4 = ((bf16[4,192,512]{2,1,0:T(8,128)(2,1)}), bf16[4,192,512]{2,1,0:T(8,128)(2,1)}, u32[]{:S(2)}, u32[]{:S(2)}) async-start(bf16[4,192,512]{2,1,0:T(8,128)(2,1)} %bitcast.214), calls=%async_computation.4 | async-start | bytes 1572864 | tf_op jit(solution)/shard_map/all_to_all | solution.py:542
  472.8 7.3 convolution_convert_fusion
  480.1 4.9 convolution_convert_fusion.1
  485.0 27.2 %attend_back.3.refs_4_ = bf16[4,576,512]{2,1,0:T(8,128)(2,1)} custom-call(s32[8]{0:T(128)} %get-tuple-element.105.lo_ref, s32[8]{0:T(128)} %get-tuple-element.104.hi_ref, bf16[4,576,512]{2,1,0:T(8,128)(2,1)} %get-tuple-element.45.x_ref, bf16[4,192,512]{2,1,0:T(8,128)(2,1)} %all-to-all-done.4.go_ref, f32[4,192,512]{2,1,0:T(8,128)} %get-tuple-element.58.out_ref, ...), custom_call_target="tpu_custom_call" | custom-call | tf_op jit(solution)/shard_map/attend_back/pallas_call | solution.py:731
  512.2 103.5 %reduce_second.1 = (f32[96,2304]{1,0:T(8,128)}, f32[96,768]{1,0:T(8,128)}, f32[96,3072]{1,0:T(8,128)}, f32[384,768]{1,0:T(8,128)}, bf16[4,576,512]{2,1,0:T(8,128)(2,1)}) custom-call(bf16[8,4,24,2304]{3,2,1,0:T(8,128)(2,1)} %bitcast.186, bf16[8,4,24,768]{3,2,1,0:T(8,128)(2,1)} %bitcast.179, bf16[8,4,24,3072]{3,2,1,0:T(8,128)(2,1)} %bitcast.182, ...), custom_call_target="tpu_custom_call" | custom-call | tf_op jit(solution)/shard_map/reduce_second/pallas_call | solution.py:1171
  615.8 2.0 copy.45
  619.2 2.0 convolution_add_fusion
  621.2 3.9 convolution_convert_fusion.2
  626.9 109.2 %reduce_first.1 = (f32[96,2304]{1,0:T(8,128)}, f32[96,768]{1,0:T(8,128)}, f32[96,3072]{1,0:T(8,128)}, f32[384,768]{1,0:T(8,128)}, f32[48,768]{1,0:T(8,128)}) custom-call(bf16[8,4,24,2304]{3,2,1,0:T(8,128)(2,1)} %bitcast.185, bf16[8,4,24,768]{3,2,1,0:T(8,128)(2,1)} %bitcast.180, bf16[8,4,24,3072]{3,2,1,0:T(8,128)(2,1)} %bitcast.184, ...), custom_call_target="tpu_custom_call" | custom-call | tf_op jit(solution)/shard_map/reduce_first/pallas_call | solution.py:1171
  737.0 1.4 dynamic-slice
  741.2 3.0 pad_maximum_fusion.3
  744.2 1.6 pad_maximum_fusion.2
  750.2 1.3 pad_maximum_fusion.4
  751.5 4.3 collective-permute-done.4
  756.0 1.2 pad_maximum_fusion.6
  (319 shorter events, 36.9 us)
Async XLA Ops:
  0.6 7.2 copy-start.24
  0.7 8.2 %copy-start.59 = (bf16[2,96]{1,0:T(2,128)(2,1)S(1)}, bf16[2,96]{1,0:T(2,128)(2,1)}, u32[]{:S(2)}) copy-start(bf16[2,96]{1,0:T(2,128)(2,1)} %param.34) | copy-start | bytes 1156
  0.7 8.2 %copy-start.58 = (bf16[2,96]{1,0:T(2,128)(2,1)S(1)}, bf16[2,96]{1,0:T(2,128)(2,1)}, u32[]{:S(2)}) copy-start(bf16[2,96]{1,0:T(2,128)(2,1)} %param.35) | copy-start | bytes 1156
  0.7 8.2 %copy-start.61 = (bf16[2,96]{1,0:T(2,128)(2,1)S(1)}, bf16[2,96]{1,0:T(2,128)(2,1)}, u32[]{:S(2)}) copy-start(bf16[2,96]{1,0:T(2,128)(2,1)} %param.29) | copy-start | bytes 1156
  0.7 8.2 %copy-start.60 = (bf16[2,96]{1,0:T(2,128)(2,1)S(1)}, bf16[2,96]{1,0:T(2,128)(2,1)}, u32[]{:S(2)}) copy-start(bf16[2,96]{1,0:T(2,128)(2,1)} %param.33) | copy-start | bytes 1156
  0.7 8.2 %copy-start.63 = (bf16[2,96]{1,0:T(2,128)(2,1)S(1)}, bf16[2,96]{1,0:T(2,128)(2,1)}, u32[]{:S(2)}) copy-start(bf16[2,96]{1,0:T(2,128)(2,1)} %param.27) | copy-start | bytes 1156
  0.7 8.2 %copy-start.62 = (bf16[2,96]{1,0:T(2,128)(2,1)S(1)}, bf16[2,96]{1,0:T(2,128)(2,1)}, u32[]{:S(2)}) copy-start(bf16[2,96]{1,0:T(2,128)(2,1)} %param.28) | copy-start | bytes 1156
  0.7 8.2 %copy-start.65 = (bf16[2,96]{1,0:T(2,128)(2,1)S(1)}, bf16[2,96]{1,0:T(2,128)(2,1)}, u32[]{:S(2)}) copy-start(bf16[2,96]{1,0:T(2,128)(2,1)} %param.24) | copy-start | bytes 1156
  0.7 8.2 %copy-start.64 = (bf16[2,96]{1,0:T(2,128)(2,1)S(1)}, bf16[2,96]{1,0:T(2,128)(2,1)}, u32[]{:S(2)}) copy-start(bf16[2,96]{1,0:T(2,128)(2,1)} %param.25) | copy-start | bytes 1156
  0.7 8.2 %copy-start.51 = (bf16[20,96]{1,0:T(8,128)(2,1)S(1)}, bf16[20,96]{1,0:T(8,128)(2,1)}, u32[]{:S(2)}) copy-start(bf16[20,96]{1,0:T(8,128)(2,1)} %param.22) | copy-start | bytes 11524
  2.0 48.5 %copy-start.17 = (bf16[2,96,3072]{2,1,0:T(8,128)(2,1)S(1)}, bf16[2,96,3072]{2,1,0:T(8,128)(2,1)}, u32[]{:S(2)}) copy-start(bf16[2,96,3072]{2,1,0:T(8,128)(2,1)} %param.30) | copy-start | bytes 3538948
  2.0 53.9 %collective-permute-start = (bf16[256,768]{1,0:T(8,128)(2,1)S(1)}, bf16[256,768]{1,0:T(8,128)(2,1)S(1)}, u32[]{:S(2)}, u32[]{:S(2)}) collective-permute-start(bf16[256,768]{1,0:T(8,128)(2,1)S(1)} %select_bitcast_fusion.1), channel_id=1, source_target_pairs={{0,4},{1,5},{2,6},{3,7},{4,0},{5,1},{6,2},{7,3},{8,12},{9,13},{10,... | collective-permute-start | bytes 1179656 | tf_op jit(solution)/shard_map/ppermute | solution.py:512
  6.9 49.0 %collective-permute-start.1 = (s32[256,1]{0,1:T(1,128)S(1)}, s32[256,1]{0,1:T(1,128)S(1)}, u32[]{:S(2)}, u32[]{:S(2)}) collective-permute-start(s32[256,1]{0,1:T(1,128)S(1)} %fusion.44), channel_id=1, source_target_pairs={{0,4},{1,5},{2,6},{3,7},{4,0},{5,1},{6,2},{7,3},{8,12},{9,13},{10,... | collective-permute-start | bytes 3080 | tf_op jit(solution)/shard_map/ppermute | solution.py:512
  51.5 4.3 copy-start.50
  51.5 4.4 copy-start.13
  54.6 98.2 %copy-start.30 = (s32[1,2048]{1,0:T(1,128)}, s32[1,2048]{1,0:T(1,128)S(1)}, u32[]{:S(2)}) copy-start(s32[1,2048]{1,0:T(1,128)S(1)} %get-tuple-element.115) | copy-start | bytes 24580
  177.0 15.5 %all-to-all-start = ((bf16[4,192,512]{2,1,0:T(8,128)(2,1)}), bf16[4,192,512]{2,1,0:T(8,128)(2,1)S(1)}, u32[]{:S(2)}, u32[]{:S(2)}) async-start(bf16[4,192,512]{2,1,0:T(8,128)(2,1)} %get-tuple-element.46), calls=%async_computation | async-start | bytes 1572864 | tf_op jit(solution)/shard_map/all_to_all | solution.py:542
  180.9 21.8 %copy-start.37 = (f32[768]{0:T(1024)}, f32[768]{0:T(1024)S(1)}, u32[]{:S(2)}) copy-start(f32[768]{0:T(1024)S(1)} %mul.258) | copy-start | bytes 9220
  181.0 21.8 %copy-start.52 = (f32[768]{0:T(1024)}, f32[768]{0:T(1024)S(1)}, u32[]{:S(2)}) copy-start(f32[768]{0:T(1024)S(1)} %add.233) | copy-start | bytes 9220
  181.1 14.3 %copy-start.43 = (f32[3072]{0:T(1024)}, f32[3072]{0:T(1024)S(1)}, u32[]{:S(2)}) copy-start(f32[3072]{0:T(1024)S(1)} %add.236) | copy-start | bytes 36868
  181.2 24.7 %copy-start.39 = (f32[768]{0:T(1024)}, f32[768]{0:T(1024)S(1)}, u32[]{:S(2)}) copy-start(f32[768]{0:T(1024)S(1)} %mul.267) | copy-start | bytes 9220
  181.3 24.6 %copy-start.54 = (f32[768]{0:T(1024)}, f32[768]{0:T(1024)S(1)}, u32[]{:S(2)}) copy-start(f32[768]{0:T(1024)S(1)} %add.245) | copy-start | bytes 9220
  195.0 7.7 %copy-start.5 = (f32[512,768]{1,0:T(8,128)}, f32[512,768]{1,0:T(8,128)S(1)}, u32[]{:S(2)}) copy-start(f32[512,768]{1,0:T(8,128)S(1)} %get-tuple-element.194) | copy-start | bytes 4718596
  195.1 7.7 %copy-start.31 = (f32[512]{0:T(512)}, f32[512]{0:T(512)S(1)}, u32[]{:S(2)}) copy-start(f32[512]{0:T(512)S(1)} %broadcast_multiply_fusion.10) | copy-start | bytes 6148
  195.1 7.7 %slice-start.2 = ((s8[4718592]{0:T(1024)(128)(4,1)}), s8[4194304]{0:T(1024)(128)(4,1)S(1)}, s32[]{:S(2)}) async-start(s8[4718592]{0:T(1024)(128)(4,1)} %bitcast.238), calls=%async_computation.7 | async-start | bytes 8388608
  195.4 7.4 copy-start.46
  195.4 7.4 slice-start.3
  205.6 121.8 %copy-start.7 = (f32[512,768]{1,0:T(8,128)}, f32[512,768]{1,0:T(8,128)S(1)}, u32[]{:S(2)}) copy-start(f32[512,768]{1,0:T(8,128)S(1)} %get-tuple-element.198) | copy-start | bytes 4718596
  303.1 4.0 copy-start.14
  303.1 24.2 %all-to-all-start.1 = ((bf16[4,192,512]{2,1,0:T(8,128)(2,1)}), bf16[4,192,512]{2,1,0:T(8,128)(2,1)S(1)}, u32[]{:S(2)}, u32[]{:S(2)}) async-start(bf16[4,192,512]{2,1,0:T(8,128)(2,1)} %get-tuple-element.52), calls=%async_computation.1 | async-start | bytes 1572864 | tf_op jit(solution)/shard_map/all_to_all | solution.py:542
  308.0 17.3 %collective-permute-start.3 = (bf16[256,768]{1,0:T(8,128)(2,1)}, bf16[256,768]{1,0:T(8,128)(2,1)S(1)}, u32[]{:S(2)}, u32[]{:S(2)}) collective-permute-start(bf16[256,768]{1,0:T(8,128)(2,1)} %select_bitcast_fusion), channel_id=1, source_target_pairs={{0,4},{1,5},{2,6},{3,7},{4,0},{5,1},{6,2},{7,3},{8,12},{9,13},{10,... | collective-permute-start | bytes 1179656 | tf_op jit(solution)/shard_map/ppermute | solution.py:512
  316.7 10.6 %copy-start.57 = (f32[768]{0:T(1024)S(1)}, f32[768]{0:T(1024)}, u32[]{:S(2)}) copy-start(f32[768]{0:T(1024)} %add.254) | copy-start | bytes 9220
  329.7 20.9 %copy-start.9 = (f32[512,768]{1,0:T(8,128)}, f32[512,768]{1,0:T(8,128)S(1)}, u32[]{:S(2)}) copy-start(f32[512,768]{1,0:T(8,128)S(1)} %get-tuple-element.200) | copy-start | bytes 4718596
  329.8 7.2 slice-start.8
  330.5 6.5 slice-start.9
  340.9 6.6 slice-start.6
  342.7 4.7 copy-start.15
  342.7 4.8 slice-start.7
  398.9 38.3 %all-to-all-start.3 = ((bf16[4,576,512]{2,1,0:T(8,128)(2,1)}), bf16[4,576,512]{2,1,0:T(8,128)(2,1)S(1)}, u32[]{:S(2)}, u32[]{:S(2)}) async-start(bf16[4,576,512]{2,1,0:T(8,128)(2,1)} %attend_back.2), calls=%async_computation.3 | async-start | bytes 4718592 | tf_op jit(solution)/shard_map/all_to_all | solution.py:542
  404.1 14.1 %copy-start.10 = (f32[512,768]{1,0:T(8,128)S(1)}, f32[512,768]{1,0:T(8,128)}, u32[]{:S(2)}) copy-start(f32[512,768]{1,0:T(8,128)} %copy-done.9) | copy-start | bytes 4718596
  404.1 14.1 %copy-start.74 = (bf16[512,3072]{1,0:T(8,128)(2,1)S(1)}, bf16[512,3072]{1,0:T(8,128)(2,1)}, u32[]{:S(2)}) copy-start(bf16[512,3072]{1,0:T(8,128)(2,1)} %copy-done.73) | copy-start | bytes 9437188
  404.1 30.7 %collective-permute-start.2 = (bf16[256,768]{1,0:T(8,128)(2,1)S(1)}, bf16[256,768]{1,0:T(8,128)(2,1)S(1)}, u32[]{:S(2)}, u32[]{:S(2)}) collective-permute-start(bf16[256,768]{1,0:T(8,128)(2,1)S(1)} %select_convert_fusion.1), channel_id=1, source_target_pairs={{0,4},{1,5},{2,6},{3,7},{4,0},{5,1},{6,2},{7,3},{8,12},{9,13},{10,... | collective-permute-start | bytes 1179656 | tf_op jit(solution)/shard_map/ppermute | solution.py:512
  418.3 5.0 copy-start.3
  423.3 11.5 %copy-start = (f32[512,768]{1,0:T(8,128)S(1)}, f32[512,768]{1,0:T(8,128)}, u32[]{:S(2)}) copy-start(f32[512,768]{1,0:T(8,128)} %get-tuple-element.124) | copy-start | bytes 4718596
  439.0 4.9 copy-start.55
  439.0 10.1 %slice-start.4 = ((s8[4718592]{0:T(1024)(128)(4,1)}), s8[4194304]{0:T(1024)(128)(4,1)S(1)}, s32[]{:S(2)}) async-start(s8[4718592]{0:T(1024)(128)(4,1)} %bitcast.241), calls=%async_computation.9 | async-start | bytes 8388608
  439.0 10.1 %slice-start.10 = ((s8[6291456]{0:T(1024)(128)(4,1)}), s8[4194304]{0:T(1024)(128)(4,1)S(1)}, s32[]{:S(2)}) async-start(s8[6291456]{0:T(1024)(128)(4,1)} %bitcast.260), calls=%async_computation.15 | async-start | bytes 8388608
  443.9 5.3 slice-start.5
  443.9 5.3 slice-start.11
  448.6 5.7 slice-start
  449.1 5.2 copy-start.16
  449.3 5.0 copy-start.6
  449.3 5.0 copy-start.32
  449.3 5.0 copy-start.38
  449.3 5.0 copy-start.47
  449.3 5.0 slice-start.1
  462.3 22.7 %all-to-all-start.4 = ((bf16[4,192,512]{2,1,0:T(8,128)(2,1)}), bf16[4,192,512]{2,1,0:T(8,128)(2,1)}, u32[]{:S(2)}, u32[]{:S(2)}) async-start(bf16[4,192,512]{2,1,0:T(8,128)(2,1)} %bitcast.214), calls=%async_computation.4 | async-start | bytes 1572864 | tf_op jit(solution)/shard_map/all_to_all | solution.py:542
  472.8 7.3 copy-start.53
  472.8 7.3 copy-start.76
  621.2 3.9 copy-start.36
  626.9 114.3 %copy-start.20 = (f32[384,768]{1,0:T(8,128)S(1)}, f32[384,768]{1,0:T(8,128)}, u32[]{:S(2)}) copy-start(f32[384,768]{1,0:T(8,128)} %get-tuple-element.69) | copy-start | bytes 3538948
  736.9 18.9 %collective-permute-start.4 = (bf16[256,768]{1,0:T(8,128)(2,1)S(1)}, bf16[256,768]{1,0:T(8,128)(2,1)S(1)}, u32[]{:S(2)}, u32[]{:S(2)}) collective-permute-start(bf16[256,768]{1,0:T(8,128)(2,1)S(1)} %select_convert_fusion), channel_id=1, source_target_pairs={{0,4},{1,5},{2,6},{3,7},{4,0},{5,1},{6,2},{7,3},{8,12},{9,13},{10,... | collective-permute-start | bytes 1179656 | tf_op jit(solution)/shard_map/ppermute | solution.py:512
  744.2 6.0 copy-start.23
  745.9 4.4 copy-start.22
  (34 other events, 73.6 us)

commit v5 on v4

--- a/solution.py
+++ b/solution.py
@@ -518,22 +518,24 @@
     )
 
 
-def to_groups(tensor, index):
+def outgoing(tensor, index):
+    return jnp.where(index < GROUP, tensor[1], tensor[0])
+
+
+def to_groups(tensor, other, index):
     low = index < GROUP
-    mine = jnp.where(low, tensor[0], tensor[1])
-    other = exchange(jnp.where(low, tensor[1], tensor[0]), "shard", GROUP)
-    both = ordered(low, mine, other)
+    both = ordered(low, jnp.where(low, tensor[0], tensor[1]), other)
     return both.reshape((2 * tensor.shape[1],) + tensor.shape[2:])
 
 
-def from_groups(tensor, index):
+def in_halves(tensor):
+    return tensor.reshape((2, tensor.shape[0] // 2) + tensor.shape[1:])
+
+
+def from_groups(tensor, other, index):
     low = index < GROUP
-    half = tensor.shape[0] // 2
-    mine = jnp.where(low, tensor[:half], tensor[half:])
-    other = exchange(
-        jnp.where(low, tensor[half:], tensor[:half]).astype(BF16), "shard", GROUP
-    ).astype(tensor.dtype)
-    return ordered(low, mine, other)
+    halves = in_halves(tensor)
+    return ordered(low, jnp.where(low, halves[0], halves[1]), other.astype(tensor.dtype))
 
 
 def swap(tensor):
@@ -871,11 +873,12 @@
             copy.wait_send()
 
 
-def gather_kernel(fourths, smalls, swaps, *refs):
+def gather_kernel(fourths, smalls, swaps, trades, *refs):
     count = fourths + smalls
     total = count + swaps
-    owns, fulls = (refs[:total], refs[total : 2 * total])
-    local_sems, send_sems, fourth_sems, small_sems, swap_sems = refs[2 * total :]
+    every = total + trades
+    owns, fulls = (refs[:every], refs[every : 2 * every])
+    local_sems, send_sems, fourth_sems, small_sems, swap_sems, trade_sems = refs[2 * every :]
     rep, shard, core, y, across_x, across_core, zs = places()
     member = lax.rem(shard, GROUP)
     greet(smalls + swaps > 0)
@@ -905,6 +908,8 @@
         send(n, shard, rep, beside, True)
         for k in (1, 2, 3):
             send(n, shard, rep, (rep, 2 * zs[k] + y), True)
+    for n in range(trades):
+        sends.push(owns[total + n], fulls[total + n], trade_sems.at[n], (rep, 2 * zs[2] + y))
     for n in range(swaps):
         for k, other in near_members:
             target = 2 * zs[k] + other
@@ -955,28 +960,33 @@
             source = lax.rem(2 * zs[k] + other, GROUP)
             piece = fulls[count + n].at[source]
             pltpu.make_async_copy(piece, piece, swap_sems.at[n, source]).wait()
+    for n in range(trades):
+        piece = fulls[total + n]
+        pltpu.make_async_copy(piece, piece, trade_sems.at[n]).wait()
     for copy in local:
         copy.wait()
     sends.finish()
 
 
-def gather_fast(fourths, smalls, swaps, name, collective_id):
+def gather_fast(fourths, smalls, swaps, trades, name, collective_id):
     split = [item.reshape(4, item.shape[0] // 4, item.shape[1]) for item in fourths] + smalls
-    owns = split + swaps
+    extra = swaps + trades
+    owns = split + extra
     dma = pltpu.SemaphoreType.DMA
     fulls = pl.pallas_call(
-        functools.partial(gather_kernel, len(fourths), len(smalls), len(swaps)),
+        functools.partial(gather_kernel, len(fourths), len(smalls), len(swaps), len(trades)),
         name=name,
         out_shape=[jax.ShapeDtypeStruct((8,) + item.shape, BF16) for item in split]
-        + [jax.ShapeDtypeStruct(item.shape, BF16) for item in swaps],
+        + [jax.ShapeDtypeStruct(item.shape, BF16) for item in extra],
         in_specs=in_vmem(len(owns)),
         out_specs=[pl.BlockSpec(memory_space=pl.ANY)] * len(owns),
         scratch_shapes=[
             dma((len(owns),)),
-            dma((28 * len(fourths) + 7 * len(smalls) + 3 * len(swaps),)),
+            dma((28 * len(fourths) + 7 * len(smalls) + 3 * len(swaps) + len(trades),)),
             dma((len(fourths), 8, 4)),
             dma((8,)),
             dma((max(1, len(swaps)), GROUP)),
+            dma((max(1, len(trades)),)),
         ],
         compiler_params=pltpu.CompilerParams(collective_id=collective_id, has_side_effects=True),
     )(*owns)
@@ -984,9 +994,9 @@
     return [item.reshape(-1, item.shape[3]) for item in fulls[:wide]] + list(fulls[wide:])
 
 
-def reduce_kernel(x_first, smalls, swaps, *refs):
+def reduce_kernel(x_first, groups, smalls, swaps, trades, *refs):
     kinds = len(x_first)
-    total = kinds + smalls + swaps
+    total = kinds + smalls + swaps + trades
     grads, extra = (refs[:kinds], refs[kinds:total])
     outs, extra_out = (refs[total : total + kinds], refs[total + kinds : 2 * total])
     scratch = refs[2 * total :]
@@ -995,7 +1005,7 @@
     ]
     (
         small_sum, small_got, local_sems, send_sems, core_sems, one_sems, two_sems, three_sems, all_sems,
-        small_sems, swap_sems,
+        small_sems, swap_sems, trade_sems,
     ) = scratch[9 * kinds :]
     rep, shard, core, y, across_x, across_core, zs = places()
     x = lax.div(rep, 2)
@@ -1047,15 +1057,20 @@
         small_sum[0] = extra[0][...]
         small_send(0)
     order = (2, 3, 1, 0)
-    for copy in local:
-        copy.wait()
-    for fy in (1, 0):
-        for k in order:
-            for n in range(kinds):
-                for fx in (1, 0):
-                    sends.push(
-                        mat(n, k, fy, fx, 1), cores[n].at[k, fy, fx], core_sems.at[n, k, fy, fx], past_core
-                    )
+
+    def open_group(group):
+        for n in group:
+            local[n].wait()
+        for fy in (1, 0):
+            for k in order:
+                for n in group:
+                    for fx in (1, 0):
+                        sends.push(
+                            mat(n, k, fy, fx, 1),
+                            cores[n].at[k, fy, fx],
+                            core_sems.at[n, k, fy, fx],
+                            past_core,
+                        )
 
     def cored(n, k, fy, fx):
         arrive(cores[n].at[k, fy, fx], core_sems.at[n, k, fy, fx])
@@ -1066,16 +1081,18 @@
         arrive(ones[n].at[k, flag], one_sems.at[n, k, flag])
         return cored(n, k, fy, fx) + [ones[n].at[k, flag]]
 
-    def step_one(slot, k, flag):
-        for n in range(kinds):
+    def step_one(group, slot):
+        k, flag = (order[slot % 4], 1 - slot // 4)
+        for n in group:
             stage = stage_one[n].at[slot]
             add(stage, cored(n, k, flag, 1) if x_first[n] else cored(n, k, 1, flag))
             sends.push(
                 stage, ones[n].at[k, flag], one_sems.at[n, k, flag], past_x if x_first[n] else beside
             )
 
-    def step_two(k):
-        for n in range(kinds):
+    def step_two(group, at):
+        k = order[at]
+        for n in group:
             stage = stage_two[n].at[k]
             add(stage, oned(n, k, 1, 0) if x_first[n] else oned(n, k, 0, 1))
             sends.push(stage, twos[n].at[k], two_sems.at[n, k], beside if x_first[n] else past_x)
@@ -1085,13 +1102,41 @@
         arrive(twos[n].at[k], two_sems.at[n, k])
         return parts + [twos[n].at[k]]
 
-    def step_three(k):
-        for n in range(kinds):
+    def step_three(group, at):
+        k = order[at]
+        for n in group:
             stage = stage_three[n].at[k - 1]
             add(stage, twod(n, k))
             sends.push(stage, threes[n].at[k - 1], three_sems.at[n, k - 1], (rep, 2 * zs[k] + y))
 
-    step_one(0, 2, 1)
+    def close(group):
+        for n in group:
+            parts = twod(n, 0)
+            for k in range(3):
+                arrive(threes[n].at[k], three_sems.at[n, k])
+            mine = alls[n].at[rep]
+            add(mine, parts + [threes[n].at[k] for k in range(3)])
+            sends.push(mine, mine, all_sems.at[n, rep], past_x)
+            sends.push(mine, mine, all_sems.at[n, rep], past_core)
+
+    def spread(group):
+        for n in group:
+            theirs = alls[n].at[across_x]
+            arrive(theirs, all_sems.at[n, across_x])
+            sends.push(theirs, theirs, all_sems.at[n, across_x], past_core)
+
+    def store(group):
+        opposite = lax.rem(across_core + 2, 4)
+        for n in group:
+            arrive(alls[n].at[across_core], all_sems.at[n, across_core])
+            arrive(alls[n].at[opposite], all_sems.at[n, opposite])
+            rows = mats[n].shape[2]
+            for q in range(4):
+                outs[n][q * rows : (q + 1) * rows, :] = alls[n][q].astype(F32)
+
+    one, two = groups
+    open_group(one)
+    step_one(one, 0)
     near_members = ((1, y), (0, 1 - y), (1, 1 - y))
     for n in range(swaps):
         for k, other in near_members:
@@ -1110,57 +1155,53 @@
     ]
     for copy in own_swaps:
         copy.start()
-    step_one(1, 3, 1)
-    step_one(2, 1, 1)
+    for n in range(trades):
+        spot = smalls + swaps + n
+        sends.push(extra[spot], extra_out[spot], trade_sems.at[n], (rep, 2 * zs[2] + y))
+    step_one(one, 1)
+    step_one(one, 2)
+    open_group(two)
     small_step(0)
-    step_two(2)
-    step_one(3, 0, 1)
-    step_two(3)
-    step_one(4, 2, 0)
+    step_one(one, 3)
+    for at in range(4):
+        step_one(one, 4 + at)
+        step_two(one, at)
     small_step(1)
-    step_two(1)
-    step_one(5, 3, 0)
-    step_two(0)
-    step_one(6, 1, 0)
+    step_one(two, 0)
+    step_one(two, 1)
+    for at in range(3):
+        step_three(one, at)
+        if at < 2:
+            step_one(two, 2 + at)
     small_step(2)
-    step_three(2)
-    step_one(7, 0, 0)
-    step_three(3)
+    for at in range(4):
+        step_one(two, 4 + at)
+        step_two(two, at)
     small_step(3)
-    step_three(1)
+    close(one)
+    for at in range(3):
+        step_three(two, at)
+    spread(one)
     small_step(4)
-
-    for n in range(kinds):
-        parts = twod(n, 0)
-        for k in range(3):
-            arrive(threes[n].at[k], three_sems.at[n, k])
-        mine = alls[n].at[rep]
-        add(mine, parts + [threes[n].at[k] for k in range(3)])
-        sends.push(mine, mine, all_sems.at[n, rep], past_x)
-        sends.push(mine, mine, all_sems.at[n, rep], past_core)
-    for n in range(kinds):
-        theirs = alls[n].at[across_x]
-        arrive(theirs, all_sems.at[n, across_x])
-        sends.push(theirs, theirs, all_sems.at[n, across_x], past_core)
-    opposite = lax.rem(across_core + 2, 4)
-    for n in range(kinds):
-        arrive(alls[n].at[across_core], all_sems.at[n, across_core])
-        arrive(alls[n].at[opposite], all_sems.at[n, opposite])
-        rows = mats[n].shape[2]
-        for q in range(4):
-            outs[n][q * rows : (q + 1) * rows, :] = alls[n][q].astype(F32)
+    close(two)
+    store(one)
+    spread(two)
+    store(two)
     for n in range(swaps):
         for k, other in near_members:
             source = lax.rem(2 * zs[k] + other, GROUP)
             arrive(extra_out[smalls + n].at[source], swap_sems.at[n, source])
+    for n in range(trades):
+        arrive(extra_out[smalls + swaps + n], trade_sems.at[n])
     for copy in own_swaps:
         copy.wait()
     sends.finish()
 
 
-def reduce_fast(grads, x_first, small, swapped, name, collective_id):
+def reduce_fast(grads, x_first, groups, small, swapped, traded, name, collective_id):
     kinds = len(grads)
-    extra = small + swapped
+    extra = small + swapped + traded
+    away = len(swapped) + len(traded)
     sizes = [(item.shape[0] // 32, item.shape[1]) for item in grads]
     buffers = []
     for lead in ((8, 4), (4, 2, 2), (4, 2), (4,), (3,), (8,), (4,), (3,), (4,)):
@@ -1169,17 +1210,18 @@
     dma = pltpu.SemaphoreType.DMA
     anywhere = pl.BlockSpec(memory_space=pl.ANY)
     return pl.pallas_call(
-        functools.partial(reduce_kernel, x_first, len(small), len(swapped)),
+        functools.partial(reduce_kernel, x_first, groups, len(small), len(swapped), len(traded)),
         name=name,
         out_shape=[jax.ShapeDtypeStruct((4 * size[0], size[1]), F32) for size in sizes]
         + [jax.ShapeDtypeStruct(item.shape, item.dtype) for item in extra],
         in_specs=[anywhere] * kinds + in_vmem(len(extra)),
-        out_specs=in_vmem(kinds + len(small)) + [anywhere] * len(swapped),
+        out_specs=in_vmem(kinds + len(small)) + [anywhere] * away,
         scratch_shapes=buffers
         + [
             pltpu.VMEM((6,) + small_shape, F32), pltpu.VMEM((5,) + small_shape, F32),
-            dma((kinds + 1,)), dma((34 * kinds + 8,)), dma((kinds, 4, 2, 2)), dma((kinds, 4, 2)),
+            dma((kinds + 1,)), dma((34 * kinds + 9,)), dma((kinds, 4, 2, 2)), dma((kinds, 4, 2)),
             dma((kinds, 4)), dma((kinds, 3)), dma((kinds, 4)), dma((5,)), dma((1, GROUP)),
+            dma((1,)),
         ],
         compiler_params=pltpu.CompilerParams(
             collective_id=collective_id, has_side_effects=True, vmem_limit_bytes=58 * 1024 * 1024
@@ -1207,7 +1249,9 @@
     small = jnp.concatenate(rows, axis=0)
     used = small.shape[0]
     small = jnp.pad(small, ((0, -used % 16), (0, 128 - share)))
-    first_qkv, small = gather_fast([qkv_weight[0]], [small], [], "gather_first", 0)
+    first_qkv, small, other_inputs = gather_fast(
+        [qkv_weight[0]], [small], [], [outgoing(inputs, index)], "gather_first", 0
+    )
     small = small[:, :used, :share].astype(F32)
     wide = jnp.transpose(small, (1, 0, 2)).reshape(used, width)
     vecs = []
@@ -1219,20 +1263,23 @@
         )
     table = wide[LAYERS * (plain + ups) :].astype(BF16)
 
-    second_qkv = []
+    second_qkv, others = ([], [])
 
     def rest_first(packed):
         proj_w, up_w, qkv_w, down_w, qkv = gather_fast(
-            [proj_weight[0], up_weight[0], qkv_weight[1], down_weight[0]], [], [packed],
+            [proj_weight[0], up_weight[0], qkv_weight[1], down_weight[0]], [], [packed], [],
             "gather_middle", 2,
         )
         second_qkv.append(qkv_w)
         return proj_w, up_w, down_w, qkv
 
     def rest_second(packed):
-        return gather_fast(
-            [proj_weight[1], up_weight[1], down_weight[1]], [], [packed], "gather_last", 3
+        *parts, other_cotangent = gather_fast(
+            [proj_weight[1], up_weight[1], down_weight[1]], [], [packed],
+            [outgoing(cotangent, index)], "gather_last", 3,
         )
+        others.append(other_cotangent)
+        return parts
 
     rests = (rest_first, rest_second)
 
@@ -1246,9 +1293,10 @@
     seg_row = tiles[:, None, :]
     seg_col = jnp.broadcast_to(segs[:, None], (segs.shape[0], 128))
 
-    slots = to_groups(memory_slot[..., None], index)[:, 0]
+    other_slots = exchange(outgoing(memory_slot, index), "shard", GROUP)
+    slots = to_groups(memory_slot, other_slots, index)
     slot_hot = slots[:, None] == jnp.arange(MEMS, dtype=jnp.int32)
-    hidden = to_groups(inputs, index).astype(F32) + mm(slot_hot.astype(BF16), table, 1, 0)
+    hidden = to_groups(inputs, other_inputs, index).astype(F32) + mm(slot_hot.astype(BF16), table, 1, 0)
     saved, held = ([], [])
     for layer in range(LAYERS):
         qkv_w = second_qkv[0] if layer else first_qkv
@@ -1257,15 +1305,18 @@
         )
         saved.append(state)
         held.append(mats)
-    layer_output = from_groups(hidden, index)
-
-    grad = to_groups(cotangent, index).astype(F32)
+
+    grad = to_groups(cotangent, others[0], index).astype(F32)
     sums, shares = ([None] * LAYERS, [None] * LAYERS)
     found = []
 
     def sum_second(grad_qkv):
-        parts = reduce_fast(found[0], (1, 1, 1, 1), [], [grad_qkv], "reduce_second", 4)
+        parts = reduce_fast(
+            found[0], (1, 1, 1, 1), ((2, 3), (0, 1)), [], [grad_qkv],
+            [outgoing(in_halves(hidden.astype(BF16)), index)], "reduce_second", 4,
+        )
         shares[1] = parts[:4]
+        others.append(parts[5])
         return parts[4]
 
     for layer in range(LAYERS - 1, -1, -1):
@@ -1274,14 +1325,18 @@
             swap if layer else sum_second,
         )
         found.append(mat_grads)
-    input_grad = from_groups(grad, index)
+    layer_output = from_groups(hidden, others[1], index)
     memory_sum = lax.dot_general(
         slot_hot.astype(F32), grad, (((0,), (0,)), ((), ())), precision=lax.Precision.HIGHEST
     )
     flat = jnp.concatenate([jnp.stack(sums[layer]) for layer in range(LAYERS)] + [memory_sum], axis=0)
     used = flat.shape[0]
     flat = jnp.pad(flat, ((0, -used % 8), (0, 0)))
-    *first_shares, flat = reduce_fast(found[1], (0, 1, 1, 0), [flat], [], "reduce_first", 1)
+    *first_shares, flat, other_grad = reduce_fast(
+        found[1], (0, 1, 1, 0), ((0, 2), (1, 3)), [flat], [],
+        [outgoing(in_halves(grad.astype(BF16)), index)], "reduce_first", 1,
+    )
+    input_grad = from_groups(grad, other_grad, index)
     shares[0] = first_shares
     flat = flat[:used]
     per = plain + ups

time: 765 us -> 729 us (0.953)
  starting transfers between devices: 37 us -> 20 us
  Pallas kernels: 512 us -> 496 us
    ppermute x5 -> x1, waiting for transfers between devices: 20.4 us -> 0.01 us  [exchange(): return lax.ppermute(tensor, axis, [(i, i ^ mask) for i in range(count)])]
    pallas_call x2, Pallas kernels: 213 us -> 194 us  [reduce_fast(): pl.pallas_call(functools.partial(reduce_kernel, x_first, groups, len(smal...]
    all_to_all x4, waiting for transfers between devices: 12.4 us -> 30.2 us  [swap(): lax.all_to_all(flat, 'shard', 0, 0, axis_index_groups=[[0, 1, 2, 3], [4,...]
    ppermute x5 -> x1, starting transfers between devices: 15.3 us -> 4.06 us  [exchange(): return lax.ppermute(tensor, axis, [(i, i ^ mask) for i in range(count)])]
  transfers between devices with their start and end apart: 9 -> 5, of which waited for: 6 -> 3; matrix products, arithmetic and copies ran while one was open for 8% -> 7% of each run, Pallas kernels for 5% -> 5%
where the time goes in v5:
time: 729 us; the launch traced here: 721 us
  Pallas kernels  496 us (68%)
  matrix products  91.6 us (13%)
  other arithmetic  33.6 us (5%)
  local copies, waits for them, and re-layouts  32 us (4%)
  waiting for transfers between devices  30.2 us (4%)
  starting transfers between devices  20 us (3%)
  blocking collectives  15.3 us (2%)
    pallas_call x3, Pallas kernels, gather_fast(): pl.pallas_call(functools.partial(gather_kernel, len(fourths), len(smalls)...  202 us
    pallas_call x2, Pallas kernels, reduce_fast(): pl.pallas_call(functools.partial(reduce_kernel, x_first, groups, len(smal...  194 us
    dot_general x25, matrix products, mm(): lax.dot_general(left, right, (((left_dim,), (right_dim,)), ((), ())), pre...  90.9 us
    pallas_call x2, Pallas kernels, attend_back(): pl.pallas_call(attend_back_kernel, name='attend_back', out_shape=jax.Shap...  54.3 us
    pallas_call x2, Pallas kernels, attend(): pl.pallas_call(attend_kernel, name='attend', out_shape=(jax.ShapeDtypeStr...  46 us
    all_to_all x4, waiting for transfers between devices, swap(): lax.all_to_all(flat, 'shard', 0, 0, axis_index_groups=[[0, 1, 2, 3], [4,...  30.2 us
    all_to_all x4, starting transfers between devices, swap(): lax.all_to_all(flat, 'shard', 0, 0, axis_index_groups=[[0, 1, 2, 3], [4,...  15.9 us
    all_to_all x1, blocking collectives, swap(): lax.all_to_all(flat, 'shard', 0, 0, axis_index_groups=[[0, 1, 2, 3], [4,...  15.3 us
  transfers between devices with their start and end apart: 5, of which 3 were waited for; matrix products, arithmetic and copies ran while one was open for 7% of the time, Pallas kernels for 5%

profile of v5, /device:TPU:0, one launch (start us, length us, event | category | flops | bytes accessed | tf_op | source)
XLA Modules:
  0.0 721.2 jit_solution(1098467969134781785)
XLA Ops:
  1.5 4.1 collective-permute-start
  12.4 1.9 select_bitcast_fusion.1.refs_2_
  14.3 1.0 fusion.64
  15.9 35.7 %gather_first.1 = (bf16[8,4,24,2304]{3,2,1,0:T(8,128)(2,1)}, bf16[8,48,128]{2,1,0:T(8,128)(2,1)}, bf16[256,768]{1,0:T(8,128)(2,1)}) custom-call(bf16[4,24,2304]{2,1,0:T(8,128)(2,1)} %bitcast.194, bf16[48,128]{1,0:T(8,128)(2,1)} %pad.8.refs_1_, bf16[256,768]{1,0:T(8,128)(2,1)} %select_bitcast_fusion.1.refs_2_), custom_call_target="tpu_custom_call" | custom-call | tf_op jit(solution)/shard_map/gather_first/pallas_call | solution.py:976
  51.7 1.1 fusion.32
  53.6 1.1 fusion.63
  54.7 1.1 fusion.62
  59.5 4.7 fusion.35
  64.7 1.6 pad_maximum_fusion.refs_4_
  66.2 88.4 %gather_middle.1 = (bf16[8,4,24,768]{3,2,1,0:T(8,128)(2,1)}, bf16[8,4,24,3072]{3,2,1,0:T(8,128)(2,1)}, bf16[8,4,24,2304]{3,2,1,0:T(8,128)(2,1)}, bf16[8,4,96,768]{3,2,1,0:T(8,128)(2,1)}, bf16[4,576,512]{2,1,0:T(8,128)(2,1)}) custom-call(bf16[4,24,768]{2,1,0:T(8,128)(2,1)} %bitcast.205, bf16[4,24,3072]{2,1,0:T(8,128)(2,1)} %bitcast.192, ...), custom_call_target="tpu_custom_call" | custom-call | tf_op jit(solution)/shard_map/gather_middle/pallas_call | solution.py:976
  154.7 1.3 broadcast_in_dim.2.seg_col
  156.0 23.0 %attend.2 = (bf16[4,192,512]{2,1,0:T(8,128)(2,1)}, f32[4,192,512]{2,1,0:T(8,128)}, f32[3,8,1,256]{3,2,1,0:T(1,128)}) custom-call(s32[8]{0:T(128)} %get-tuple-element.113.lo_ref, s32[8]{0:T(128)} %get-tuple-element.112.hi_ref, bf16[4,576,512]{2,1,0:T(8,128)(2,1)} %get-tuple-element.50.x_ref, s32[2048,128]{1,0:T(8,128)} %broadcast_in_dim.2.seg_col, ...), custom_call_target="tpu_custom_call" | custom-call | tf_op jit(solution)/shard_map/attend/pallas_call | solution.py:711
  179.0 3.8 all-to-all-start
  183.5 0.8 select_bitcast_fusion.refs_4_
  184.3 10.1 %all-to-all-done = bf16[4,192,512]{2,1,0:T(8,128)(2,1)S(1)} async-done(((bf16[4,192,512]{2,1,0:T(8,128)(2,1)}), bf16[4,192,512]{2,1,0:T(8,128)(2,1)S(1)}, u32[]{:S(2)}, u32[]{:S(2)}) %all-to-all-start) | async-done | bytes 786464 | tf_op jit(solution)/shard_map/all_to_all | solution.py:544
  194.4 2.5 fusion.81
  197.4 5.7 multiply_convert_fusion.3
  203.1 2.7 fusion.82
  206.2 2.3 fusion.54
  209.0 1.6 pad_maximum_fusion.1.refs_3_
  210.6 77.6 %gather_last.1 = (bf16[8,4,24,768]{3,2,1,0:T(8,128)(2,1)}, bf16[8,4,24,3072]{3,2,1,0:T(8,128)(2,1)}, bf16[8,4,96,768]{3,2,1,0:T(8,128)(2,1)}, bf16[4,576,512]{2,1,0:T(8,128)(2,1)}, bf16[256,768]{1,0:T(8,128)(2,1)}) custom-call(bf16[4,24,768]{2,1,0:T(8,128)(2,1)} %bitcast.204, bf16[4,24,3072]{2,1,0:T(8,128)(2,1)} %bitcast.190, bf16[4,96,768]{2,1,0:T(8,128)(2,1)} %bitcast.191, ...), custom_call_target="tpu_custom_call" | custom-call | tf_op jit(solution)/shard_map/gather_last/pallas_call | solution.py:976
  288.2 23.0 %attend.3 = (bf16[4,192,512]{2,1,0:T(8,128)(2,1)}, f32[4,192,512]{2,1,0:T(8,128)}, f32[3,8,1,256]{3,2,1,0:T(1,128)}) custom-call(s32[8]{0:T(128)} %get-tuple-element.113.lo_ref, s32[8]{0:T(128)} %get-tuple-element.112.hi_ref, bf16[4,576,512]{2,1,0:T(8,128)(2,1)} %get-tuple-element.56.x_ref, s32[2048,128]{1,0:T(8,128)} %broadcast_in_dim.2.seg_col, ...), custom_call_target="tpu_custom_call" | custom-call | tf_op jit(solution)/shard_map/attend/pallas_call | solution.py:711
  311.2 4.0 all-to-all-start.1
  318.8 1.2 fusion.30
  320.4 6.5 all-to-all-done.1
  326.9 2.4 fusion.83
  330.0 6.5 multiply_convert_fusion.2
  336.6 2.9 fusion.84
  340.4 2.1 fusion.60
  342.5 4.7 convert_reduce_fusion
  347.3 3.1 multiply_reduce_fusion
  351.8 0.8 convolution_convert_fusion.9
  352.6 15.3 %all_to_all.42.go_ref = bf16[4,192,512]{2,1,0:T(8,128)(2,1)} all-to-all(bf16[4,192,512]{2,1,0:T(8,128)(2,1)S(1)} %bitcast.203), channel_id=1, replica_groups={{0,1,2,3},{4,5,6,7},{8,9,10,11},{12,13,14,15},{16,17,18,19},{20,21,22,2..., dimensions={0} | all-to-all | bytes 1572864 | tf_op jit(solution)/shard_map/all_to_all | solution.py:544
  367.9 27.1 %attend_back.2 = bf16[4,576,512]{2,1,0:T(8,128)(2,1)} custom-call(s32[8]{0:T(128)} %get-tuple-element.113.lo_ref, s32[8]{0:T(128)} %get-tuple-element.112.hi_ref, bf16[4,576,512]{2,1,0:T(8,128)(2,1)} %get-tuple-element.56.x_ref, bf16[4,192,512]{2,1,0:T(8,128)(2,1)} %all_to_all.42.go_ref, f32[4,192,512]{2,1,0:T(8,128)} %get-tuple-element.62.out_ref, ...), custom_call_target="tpu_custom_call" | custom-call | tf_op jit(solution)/shard_map/attend_back/pallas_call | solution.py:733
  395.0 3.8 all-to-all-start.3
  399.0 2.1 slice_select_fusion.3.refs_5_
  401.0 3.4 convolution_convert_fusion.7
  404.4 4.3 convolution_convert_fusion.3
  408.8 4.8 convolution_convert_fusion.4
  413.6 13.7 %all-to-all-done.3 = bf16[4,576,512]{2,1,0:T(8,128)(2,1)S(1)} async-done(((bf16[4,576,512]{2,1,0:T(8,128)(2,1)}), bf16[4,576,512]{2,1,0:T(8,128)(2,1)S(1)}, u32[]{:S(2)}, u32[]{:S(2)}) %all-to-all-start.3) | async-done | bytes 2359328 | tf_op jit(solution)/shard_map/all_to_all | solution.py:544
  427.5 1.2 copy-done.3
  429.2 4.8 multiply_reduce_fusion.1
  434.1 4.2 convolution_convert_fusion.5
  439.5 5.0 convert_reduce_fusion.1
  444.6 3.1 multiply_reduce_fusion.2
  449.0 1.7 convolution_convert_fusion.8
  450.7 1.8 convolution_convert_fusion.6
  452.5 4.2 all-to-all-start.4
  457.0 7.3 %convolution_convert_fusion = bf16[3072,768]{1,0:T(8,128)(2,1)} fusion(bf16[512,3072]{1,0:T(8,128)(2,1)} %copy-done.74, f32[512,768]{1,0:T(8,128)} %copy-done.18), kind=kOutput, calls=%fused_computation.20 | convolution fusion | flops 2418671616 | bytes 9437184 | tf_op jit(solution)/shard_map/dot_general | solution.py:505
  464.4 4.9 convolution_convert_fusion.1
  469.2 27.2 %attend_back.3.refs_4_ = bf16[4,576,512]{2,1,0:T(8,128)(2,1)} custom-call(s32[8]{0:T(128)} %get-tuple-element.113.lo_ref, s32[8]{0:T(128)} %get-tuple-element.112.hi_ref, bf16[4,576,512]{2,1,0:T(8,128)(2,1)} %get-tuple-element.50.x_ref, bf16[4,192,512]{2,1,0:T(8,128)(2,1)} %all-to-all-done.4.go_ref, f32[4,192,512]{2,1,0:T(8,128)} %get-tuple-element.64.out_ref, ...), custom_call_target="tpu_custom_call" | custom-call | tf_op jit(solution)/shard_map/attend_back/pallas_call | solution.py:733
  496.4 101.9 %reduce_second.1 = (f32[96,2304]{1,0:T(8,128)}, f32[96,768]{1,0:T(8,128)}, f32[96,3072]{1,0:T(8,128)}, f32[384,768]{1,0:T(8,128)}, bf16[4,576,512]{2,1,0:T(8,128)(2,1)}, /*index=5*/bf16[256,768]{1,0:T(8,128)(2,1)}) custom-call(bf16[8,4,24,2304]{3,2,1,0:T(8,128)(2,1)} %bitcast.174, bf16[8,4,24,768]{3,2,1,0:T(8,128)(2,1)} %bitcast.167, ...), custom_call_target="tpu_custom_call" | custom-call | tf_op jit(solution)/shard_map/reduce_second/pallas_call | solution.py:1212
  598.4 2.0 copy.45
  601.8 2.9 fusion.85
  604.7 3.9 convolution_convert_fusion.2
  611.3 92.1 %reduce_first.1 = (f32[96,2304]{1,0:T(8,128)}, f32[96,768]{1,0:T(8,128)}, f32[96,3072]{1,0:T(8,128)}, f32[384,768]{1,0:T(8,128)}, f32[48,768]{1,0:T(8,128)}, /*index=5*/bf16[256,768]{1,0:T(8,128)(2,1)}) custom-call(bf16[8,4,24,2304]{3,2,1,0:T(8,128)(2,1)} %bitcast.173, bf16[8,4,24,768]{3,2,1,0:T(8,128)(2,1)} %bitcast.168, ...), custom_call_target="tpu_custom_call" | custom-call | tf_op jit(solution)/shard_map/reduce_first/pallas_call | solution.py:1212
  704.3 3.0 pad_maximum_fusion.3
  707.3 1.6 pad_maximum_fusion.2
  708.9 0.9 pad_maximum_fusion.9
  710.3 1.3 pad_maximum_fusion.4
  712.8 1.2 pad_maximum_fusion.6
  714.1 1.2 pad_maximum_fusion.5
  716.0 1.4 dynamic-slice
  717.4 1.1 fusion.67
  (318 shorter events, 35.1 us)
Async XLA Ops:
  0.6 13.6 %copy-start.26 = (bf16[2,96,2304]{2,1,0:T(8,128)(2,1)S(1)}, bf16[2,96,2304]{2,1,0:T(8,128)(2,1)}, u32[]{:S(2)}) copy-start(bf16[2,96,2304]{2,1,0:T(8,128)(2,1)} %param.23) | copy-start | bytes 2654212
  0.7 14.6 %copy-start.62 = (bf16[20,96]{1,0:T(8,128)(2,1)S(1)}, bf16[20,96]{1,0:T(8,128)(2,1)}, u32[]{:S(2)}) copy-start(bf16[20,96]{1,0:T(8,128)(2,1)} %param.22) | copy-start | bytes 11524
  1.5 57.6 %collective-permute-start = (s32[256]{0:T(256)S(1)}, s32[256]{0:T(256)S(1)}, u32[]{:S(2)}, u32[]{:S(2)}) collective-permute-start(s32[256]{0:T(256)S(1)} %bitcast.225), channel_id=1, source_target_pairs={{0,4},{1,5},{2,6},{3,7},{4,0},{5,1},{6,2},{7,3},{8,12},{9,13},{10,... | collective-permute-start | bytes 3080 | tf_op jit(solution)/shard_map/ppermute | solution.py:512
  14.3 37.4 %copy-start.12 = (bf16[2,256,768]{2,1,0:T(8,128)(2,1)S(1)}, bf16[2,256,768]{2,1,0:T(8,128)(2,1)}, u32[]{:S(2)}) copy-start(bf16[2,256,768]{2,1,0:T(8,128)(2,1)} %param.18) | copy-start | bytes 2359300
  15.9 37.6 %copy-start.19 = (bf16[2,96,3072]{2,1,0:T(8,128)(2,1)S(1)}, bf16[2,96,3072]{2,1,0:T(8,128)(2,1)}, u32[]{:S(2)}) copy-start(bf16[2,96,3072]{2,1,0:T(8,128)(2,1)} %param.30) | copy-start | bytes 3538948
  57.7 97.0 %copy-start.34 = (s32[1,2048]{1,0:T(1,128)}, s32[1,2048]{1,0:T(1,128)S(1)}, u32[]{:S(2)}) copy-start(s32[1,2048]{1,0:T(1,128)S(1)} %get-tuple-element.125) | copy-start | bytes 24580
  59.1 5.1 copy-start.41
  59.5 134.9 %copy-start.14 = (f32[512,768]{1,0:T(8,128)}, f32[512,768]{1,0:T(8,128)S(1)}, u32[]{:S(2)}) copy-start(f32[512,768]{1,0:T(8,128)S(1)} %convert_add_fusion) | copy-start | bytes 4718596
  179.0 4.5 copy-start.13
  179.0 15.4 %all-to-all-start = ((bf16[4,192,512]{2,1,0:T(8,128)(2,1)}), bf16[4,192,512]{2,1,0:T(8,128)(2,1)S(1)}, u32[]{:S(2)}, u32[]{:S(2)}) async-start(bf16[4,192,512]{2,1,0:T(8,128)(2,1)} %get-tuple-element.51), calls=%async_computation | async-start | bytes 1572864 | tf_op jit(solution)/shard_map/all_to_all | solution.py:544
  183.0 20.1 %copy-start.43 = (f32[768]{0:T(1024)}, f32[768]{0:T(1024)S(1)}, u32[]{:S(2)}) copy-start(f32[768]{0:T(1024)S(1)} %mul.258) | copy-start | bytes 9220
  183.0 20.0 %copy-start.63 = (f32[768]{0:T(1024)}, f32[768]{0:T(1024)S(1)}, u32[]{:S(2)}) copy-start(f32[768]{0:T(1024)S(1)} %add.233) | copy-start | bytes 9220
  183.1 14.1 %copy-start.55 = (f32[3072]{0:T(1024)}, f32[3072]{0:T(1024)S(1)}, u32[]{:S(2)}) copy-start(f32[3072]{0:T(1024)S(1)} %add.236) | copy-start | bytes 36868
  183.3 22.9 %copy-start.45 = (f32[768]{0:T(1024)}, f32[768]{0:T(1024)S(1)}, u32[]{:S(2)}) copy-start(f32[768]{0:T(1024)S(1)} %mul.267) | copy-start | bytes 9220
  183.4 22.9 %copy-start.65 = (f32[768]{0:T(1024)}, f32[768]{0:T(1024)S(1)}, u32[]{:S(2)}) copy-start(f32[768]{0:T(1024)S(1)} %add.245) | copy-start | bytes 9220
  196.9 6.2 copy-start.4
  196.9 6.1 copy-start.37
  196.9 6.2 slice-start.2
  197.2 5.8 copy-start.58
  197.4 5.7 slice-start.3
  203.1 3.1 copy-start.71
  205.9 121.0 %copy-start.6 = (f32[512,768]{1,0:T(8,128)}, f32[512,768]{1,0:T(8,128)S(1)}, u32[]{:S(2)}) copy-start(f32[512,768]{1,0:T(8,128)S(1)} %get-tuple-element.209) | copy-start | bytes 4718596
  311.2 4.1 copy-start.53
  311.2 4.8 copy-start.52
  311.2 5.4 copy-start.51
  311.2 6.1 copy-start.50
  311.2 7.4 %copy-start.49 = (f32[8,96]{1,0:T(8,128)S(1)}, f32[8,96]{1,0:T(8,128)}, u32[]{:S(2)}) copy-start(f32[8,96]{1,0:T(8,128)} %get-tuple-element.96) | copy-start | bytes 9220
  311.2 7.5 %copy-start.48 = (f32[8,96]{1,0:T(8,128)S(1)}, f32[8,96]{1,0:T(8,128)}, u32[]{:S(2)}) copy-start(f32[8,96]{1,0:T(8,128)} %get-tuple-element.94) | copy-start | bytes 9220
  311.2 7.6 %copy-start.30 = (bf16[256,768]{1,0:T(8,128)(2,1)S(1)}, bf16[256,768]{1,0:T(8,128)(2,1)}, u32[]{:S(2)}) copy-start(bf16[256,768]{1,0:T(8,128)(2,1)} %get-tuple-element.61) | copy-start | bytes 1179652
  311.2 15.6 %all-to-all-start.1 = ((bf16[4,192,512]{2,1,0:T(8,128)(2,1)}), bf16[4,192,512]{2,1,0:T(8,128)(2,1)S(1)}, u32[]{:S(2)}, u32[]{:S(2)}) async-start(bf16[4,192,512]{2,1,0:T(8,128)(2,1)} %get-tuple-element.57), calls=%async_computation.1 | async-start | bytes 1572864 | tf_op jit(solution)/shard_map/all_to_all | solution.py:544
  318.6 8.3 %copy-start.68 = (f32[768]{0:T(1024)S(1)}, f32[768]{0:T(1024)}, u32[]{:S(2)}) copy-start(f32[768]{0:T(1024)} %add.254) | copy-start | bytes 9220
  329.2 21.2 %copy-start.8 = (f32[512,768]{1,0:T(8,128)}, f32[512,768]{1,0:T(8,128)S(1)}, u32[]{:S(2)}) copy-start(f32[512,768]{1,0:T(8,128)S(1)} %get-tuple-element.211) | copy-start | bytes 4718596
  329.3 7.2 %slice-start.8 = ((s8[4718592]{0:T(1024)(128)(4,1)}), s8[4194304]{0:T(1024)(128)(4,1)S(1)}, s32[]{:S(2)}) async-start(s8[4718592]{0:T(1024)(128)(4,1)} %bitcast.240), calls=%async_computation.13 | async-start | bytes 8388608
  330.0 6.5 slice-start.9
  340.4 6.9 slice-start.6
  342.5 4.7 copy-start.16
  342.5 4.8 slice-start.7
  347.3 3.2 copy-start.77
  395.0 32.3 %all-to-all-start.3 = ((bf16[4,576,512]{2,1,0:T(8,128)(2,1)}), bf16[4,576,512]{2,1,0:T(8,128)(2,1)S(1)}, u32[]{:S(2)}, u32[]{:S(2)}) async-start(bf16[4,576,512]{2,1,0:T(8,128)(2,1)} %attend_back.2), calls=%async_computation.3 | async-start | bytes 4718592 | tf_op jit(solution)/shard_map/all_to_all | solution.py:544
  399.0 5.5 copy-start.76
  401.0 3.4 copy-start.17
  404.4 4.4 copy-start.9
  404.4 4.4 copy-start.78
  429.2 4.9 copy-start.66
  429.2 10.1 %slice-start.4 = ((s8[4718592]{0:T(1024)(128)(4,1)}), s8[4194304]{0:T(1024)(128)(4,1)S(1)}, s32[]{:S(2)}) async-start(s8[4718592]{0:T(1024)(128)(4,1)} %bitcast.233), calls=%async_computation.9 | async-start | bytes 8388608
  429.2 10.1 %slice-start.10 = ((s8[6291456]{0:T(1024)(128)(4,1)}), s8[4194304]{0:T(1024)(128)(4,1)S(1)}, s32[]{:S(2)}) async-start(s8[6291456]{0:T(1024)(128)(4,1)} %bitcast.252), calls=%async_computation.15 | async-start | bytes 8388608
  434.1 5.3 slice-start.5
  434.1 5.3 slice-start.11
  438.8 5.7 slice-start
  439.3 5.2 copy-start.18
  439.5 5.0 copy-start.5
  439.5 5.0 copy-start.38
  439.5 5.0 copy-start.44
  439.5 5.0 copy-start.59
  439.5 5.0 slice-start.1
  444.5 3.2 copy-start.79
  452.5 16.7 %all-to-all-start.4 = ((bf16[4,192,512]{2,1,0:T(8,128)(2,1)}), bf16[4,192,512]{2,1,0:T(8,128)(2,1)}, u32[]{:S(2)}, u32[]{:S(2)}) async-start(bf16[4,192,512]{2,1,0:T(8,128)(2,1)} %bitcast.202), calls=%async_computation.4 | async-start | bytes 1572864 | tf_op jit(solution)/shard_map/all_to_all | solution.py:544
  457.0 7.3 %copy-start.64 = (f32[768]{0:T(1024)S(1)}, f32[768]{0:T(1024)}, u32[]{:S(2)}) copy-start(f32[768]{0:T(1024)} %copy-done.63) | copy-start | bytes 9220
  457.0 7.3 %copy-start.80 = (bf16[512,3072]{1,0:T(8,128)(2,1)S(1)}, bf16[512,3072]{1,0:T(8,128)(2,1)}, u32[]{:S(2)}) copy-start(bf16[512,3072]{1,0:T(8,128)(2,1)} %copy-done.79) | copy-start | bytes 9437188
  598.3 3.4 copy-start.70
  604.7 3.9 copy-start.42
  611.3 92.9 %copy-start.22 = (f32[384,768]{1,0:T(8,128)S(1)}, f32[384,768]{1,0:T(8,128)}, u32[]{:S(2)}) copy-start(f32[384,768]{1,0:T(8,128)} %get-tuple-element.77) | copy-start | bytes 3538948
  704.2 3.0 copy-start.21
  704.2 3.0 copy-start.23
  (34 other events, 61.7 us)
